TPU v7x, 32 devices: a whole 2x2x4 slice. The times are simulated.
32 devices in a mesh: group: 4 (over y, x), ctx: 8 (over z, core).
Axes of the slice: x: 2, y: 2, z: 4, core: 2. Of those that a mesh axis runs over, the one named last changes fastest.
Arguments:
- tokens: bfloat16 [4, 1024, 2048], P('group', 'ctx'), may hold values from -8 to 8
- positions: int32 [4, 1024], P('group', 'ctx'), may hold values from 0 to 1023, as said below
- expert_ids: int32 [4, 1024, 8], P('group', 'ctx'), may hold values from 0 to 15, all different within a row; in each aligned block of 128 rows (0 to 127, 128 to 255, ..., all dimensions but the last counted through in order) at most 96 rows name the same one
- cotangent: bfloat16 [4, 1024, 2048], P('group', 'ctx'), may hold values from -6 to 6
- attention_gain: bfloat16 [2048], P('group'), may hold values from 0.5 to 1.5
- query_weight: bfloat16 [2048, 4096], P('group'), may hold values from -0.125 to 0.125
- key_weight: bfloat16 [2048, 512], P('group'), may hold values from -0.125 to 0.125
- value_weight: bfloat16 [2048, 512], P('group'), may hold values from -0.125 to 0.125
- output_weight: bfloat16 [2048, 4096], P('group'), may hold values from -2 to 2
- query_gain: bfloat16 [128], P('group'), may hold values from 0.099609375 to 1.8984375
- key_gain: bfloat16 [128], P('group'), may hold values from 0.099609375 to 1.8984375
- mixture_gain: bfloat16 [2048], P('group'), may hold values from 0.5 to 1.5
- router_weight: bfloat16 [2048, 16], P('group'), may hold values from -1 to 1
- gate_weight: bfloat16 [16, 2048, 768], P(None, 'group'), may hold values from -0.125 to 0.125
- up_weight: bfloat16 [16, 2048, 768], P(None, 'group'), may hold values from -0.125 to 0.125
- down_weight: bfloat16 [16, 2048, 768], P(None, 'group'), may hold values from -30 to 30
Outputs:
- layer_out: bfloat16 [4, 1024, 2048], P('group', 'ctx')
- tokens_grad: bfloat16 [4, 1024, 2048], P('group', 'ctx')
- attention_gain_grad: float32 [2048], P('group')
- query_weight_grad: float32 [2048, 4096], P('group')
- key_weight_grad: float32 [2048, 512], P('group')
- value_weight_grad: float32 [2048, 512], P('group')
- output_weight_grad: float32 [2048, 4096], P('group')
- query_gain_grad: float32 [128], P('group')
- key_gain_grad: float32 [128], P('group')
- mixture_gain_grad: float32 [2048], P('group')
- router_weight_grad: float32 [2048, 16], P('group')
- gate_weight_grad: float32 [16, 2048, 768], P(None, 'group')
- up_weight_grad: float32 [16, 2048, 768], P(None, 'group')
- down_weight_grad: float32 [16, 2048, 768], P(None, 'group')
Inputs may be any that keep to these rules, and one draw needn't show every extreme that they name: positions restart at 0 where a document begins and rise by one from token to token inside it; every sequence begins a document at its first token and holds one to four documents. `expert_ids`: each token names 8 different experts; among the 128 tokens of one device (aligned blocks of rows) no expert is named by more than 96 tokens, a bound that some block reaches.
All inputs are finite; a program needn't handle non-finite values.
Results may differ from a plain program's by a relative error of at most 0.03.
Values may be sent and summed in bfloat16 or wider, within the bound.
A program may use at most 576 MiB of HBM per device.

v0:
```python
import jax
import jax.numpy as jnp
from jax import lax
from jax.sharding import PartitionSpec as P

D = 2048
HQ = 32
HK = 4
HD = 128
TOPK = 8
EXPERTS = 16
CAP = 96


EPS = 1e-06
ROPE_BASE = 1000000.0
FLOOR = -1e30


def rms_parts(values, gains):
    factor = lax.rsqrt(jnp.mean(values * values, axis=-1, keepdims=True) + EPS)
    return (values * factor * gains, factor)


def rms_back(values, factor, gains, gradient):
    weighted = gradient * gains
    inner = jnp.mean(weighted * values, axis=-1, keepdims=True)
    grad_values = factor * weighted - values * (factor * factor * factor) * inner
    return (grad_values, gradient * values * factor)


def rope_tables(position_row):
    frequency = ROPE_BASE ** (-2.0 * jnp.arange(HD // 2, dtype=jnp.float32) / HD)
    angles = position_row.astype(jnp.float32)[:, None] * frequency[None, :]
    angles = jnp.concatenate([angles, angles], axis=-1)[:, None, :]
    return (jnp.cos(angles), jnp.sin(angles))


def rotate(values, cosine, sine):
    middle = values.shape[-1] // 2
    turned = jnp.concatenate([-values[..., middle:], values[..., :middle]], axis=-1)
    return values * cosine + turned * sine


def rotate_back(gradient, cosine, sine):
    middle = gradient.shape[-1] // 2
    rolled = gradient * sine
    turned = jnp.concatenate([rolled[..., middle:], -rolled[..., :middle]], axis=-1)
    return gradient * cosine + turned


def block_rows(count):
    size_now = count
    while size_now > 1024 and size_now % 2 == 0:
        size_now = size_now // 2
    return size_now


def per_device(
    tokens,
    positions,
    expert_ids,
    cotangent,
    attention_gain,
    query_weight,
    key_weight,
    value_weight,
    output_weight,
    query_gain,
    key_gain,
    mixture_gain,
    router_weight,
    gate_weight,
    up_weight,
    down_weight,
):
    row_count = tokens.shape[1]
    group_width = HQ // HK
    scaling = HD ** (-0.5)
    first_row = lax.axis_index("ctx") * row_count
    row_index = first_row + jnp.arange(row_count, dtype=jnp.int32)
    doc_start = row_index - positions[0]
    earliest = jnp.min(doc_start)
    latest = first_row + row_count - 1
    cosine, sine = rope_tables(positions[0])
    attn_set = (
        lax.all_gather(attention_gain, "group", axis=0, tiled=True),
        lax.all_gather(query_weight, "group", axis=0, tiled=True),
        lax.all_gather(key_weight, "group", axis=0, tiled=True),
        lax.all_gather(value_weight, "group", axis=0, tiled=True),
        lax.all_gather(output_weight, "group", axis=0, tiled=True),
        lax.all_gather(query_gain, "group", axis=0, tiled=True),
        lax.all_gather(key_gain, "group", axis=0, tiled=True),
        lax.all_gather(mixture_gain, "group", axis=0, tiled=True),
        lax.all_gather(router_weight, "group", axis=0, tiled=True),
    )
    expert_set = (
        lax.all_gather(gate_weight, "group", axis=1, tiled=True),
        lax.all_gather(up_weight, "group", axis=1, tiled=True),
        lax.all_gather(down_weight, "group", axis=1, tiled=True),
    )

    def allowed_mask(key_offset, key_count):
        key_index = key_offset + jnp.arange(key_count, dtype=jnp.int32)
        return (key_index[None, :] <= row_index[:, None]) & (
            key_index[None, :] >= doc_start[:, None]
        )

    inputs = tokens[0].astype(jnp.float32)
    normed, attn_factor = rms_parts(inputs, attn_set[0])
    normed_low = normed.astype(jnp.bfloat16)
    query_raw = jnp.dot(normed_low, attn_set[1], preferred_element_type=jnp.float32).reshape(
        row_count, HQ, HD
    )
    key_raw = jnp.dot(normed_low, attn_set[2], preferred_element_type=jnp.float32).reshape(
        row_count, HK, HD
    )
    value_low = (
        jnp.dot(normed_low, attn_set[3], preferred_element_type=jnp.float32)
        .astype(jnp.bfloat16)
        .reshape(row_count, HK, HD)
    )
    query_normed, query_factor = rms_parts(query_raw, attn_set[5])
    key_normed, key_factor = rms_parts(key_raw, attn_set[6])
    query_low = (
        rotate(query_normed, cosine, sine)
        .astype(jnp.bfloat16)
        .reshape(row_count, HK, group_width, HD)
    )
    key_low = rotate(key_normed, cosine, sine).astype(jnp.bfloat16)
    initial = (
        jnp.zeros((HK, group_width, row_count, HD), jnp.float32),
        jnp.full((HK, group_width, row_count), FLOOR, jnp.float32),
        jnp.zeros((HK, group_width, row_count), jnp.float32),
    )
    offset = jnp.int32(0)
    key_piece = lax.all_gather(key_low, "ctx", axis=0, tiled=True)
    value_piece = lax.all_gather(value_low, "ctx", axis=0, tiled=True)
    piece_rows = key_piece.shape[0]
    block_size = block_rows(piece_rows)

    def one_block(current, number):
        accumulated, highest, denominator = current
        block_start = number * block_size
        key_block = lax.dynamic_slice_in_dim(key_piece, block_start, block_size, 0)
        value_block = lax.dynamic_slice_in_dim(value_piece, block_start, block_size, 0)
        allowed = allowed_mask(block_start, block_size)
        scores = (
            jnp.einsum("tkgd,skd->kgts", query_low, key_block, preferred_element_type=jnp.float32)
            * scaling
        )
        masked = jnp.where(allowed, scores, FLOOR)
        raised = jnp.maximum(highest, jnp.max(masked, axis=-1))
        shrink = jnp.exp(highest - raised)
        weights = jnp.where(allowed, jnp.exp(masked - raised[..., None]), 0.0)
        denominator = denominator * shrink + jnp.sum(weights, axis=-1)
        accumulated = accumulated * shrink[..., None] + jnp.einsum(
            "kgts,skd->kgtd",
            weights.astype(jnp.bfloat16),
            value_block,
            preferred_element_type=jnp.float32,
        )
        return ((accumulated, raised, denominator), None)

    def absorb_compute(current):
        return lax.scan(one_block, current, jnp.arange(piece_rows // block_size, dtype=jnp.int32))[
            0
        ]

    def unchanged(current):
        return current

    useful = (offset <= latest) & (offset + piece_rows - 1 >= earliest)
    accumulated, highest, denominator = lax.cond(useful, absorb_compute, unchanged, initial)
    log_total = highest + jnp.log(denominator)
    mixed = jnp.transpose(accumulated / denominator[..., None], (2, 0, 1, 3)).reshape(
        row_count, HQ * HD
    )
    mixed_low = mixed.astype(jnp.bfloat16)
    attn_out = jnp.einsum("tf,df->td", mixed_low, attn_set[4], preferred_element_type=jnp.float32)
    hidden = inputs + attn_out
    moe_normed, moe_factor = rms_parts(hidden, attn_set[7])
    moe_low = moe_normed.astype(jnp.bfloat16)
    logits = jnp.dot(moe_low, attn_set[8], preferred_element_type=jnp.float32)
    onehot = (
        expert_ids[0][:, :, None] == jnp.arange(EXPERTS, dtype=jnp.int32)[None, None, :]
    ).astype(jnp.float32)
    chosen = jnp.sum(onehot * logits[:, None, :], axis=-1)
    expo = jnp.exp(chosen - jnp.max(chosen, axis=-1, keepdims=True))
    gates = expo / jnp.sum(expo, axis=-1, keepdims=True)
    pair_count = row_count * TOPK
    slot_total = EXPERTS * CAP
    pair_expert = expert_ids[0].reshape(pair_count)
    pair_table = (pair_expert[:, None] == jnp.arange(EXPERTS, dtype=jnp.int32)[None, :]).astype(
        jnp.int32
    )
    slot_rank = jnp.sum((jnp.cumsum(pair_table, axis=0) - 1) * pair_table, axis=1)
    slot_of_pair = pair_expert * CAP + slot_rank
    pair_token = jnp.arange(pair_count, dtype=jnp.int32) // TOPK
    slot_token = jnp.zeros((slot_total,), jnp.int32).at[slot_of_pair].set(pair_token)
    slot_live = jnp.zeros((slot_total,), jnp.float32).at[slot_of_pair].set(1.0)
    slot_weight = (
        jnp.zeros((slot_total,), jnp.float32).at[slot_of_pair].set(gates.reshape(pair_count))
    )
    expert_rows = jnp.where(
        slot_live[:, None] > 0.0, moe_low[slot_token], jnp.zeros((), jnp.bfloat16)
    ).reshape(EXPERTS, CAP, D)
    gate_all = jnp.einsum(
        "ecd,edf->ecf", expert_rows, expert_set[0], preferred_element_type=jnp.float32
    )
    up_all = jnp.einsum(
        "ecd,edf->ecf", expert_rows, expert_set[1], preferred_element_type=jnp.float32
    )
    sigmoid_all = lax.logistic(gate_all)
    act_low = (gate_all * sigmoid_all * up_all).astype(jnp.bfloat16)
    out_all = jnp.einsum("ecf,edf->ecd", act_low, expert_set[2], preferred_element_type=jnp.float32)
    picked = out_all.reshape(slot_total, D)[slot_of_pair].reshape(row_count, TOPK, D)
    mixture = jnp.sum(gates[:, :, None] * picked, axis=1)
    layer_out = (hidden + mixture).astype(jnp.bfloat16)[None]
    upstream = cotangent[0].astype(jnp.float32)
    expert_set = (
        lax.all_gather(gate_weight, "group", axis=1, tiled=True),
        lax.all_gather(up_weight, "group", axis=1, tiled=True),
        lax.all_gather(down_weight, "group", axis=1, tiled=True),
    )
    out_grad_low = (
        (slot_weight[:, None] * upstream[slot_token]).astype(jnp.bfloat16).reshape(EXPERTS, CAP, D)
    )
    gates_grad = jnp.sum(picked * upstream[:, None, :], axis=-1)
    act_grad = jnp.einsum(
        "ecd,edf->ecf", out_grad_low, expert_set[2], preferred_element_type=jnp.float32
    )
    gate_grad_low = (
        act_grad * up_all * sigmoid_all * (1.0 + gate_all * (1.0 - sigmoid_all))
    ).astype(jnp.bfloat16)
    up_grad_low = (act_grad * gate_all * sigmoid_all).astype(jnp.bfloat16)
    rows_cols, out_cols = (
        lax.all_to_all(expert_rows, "group", split_axis=2, concat_axis=1, tiled=True),
        lax.all_to_all(out_grad_low, "group", split_axis=2, concat_axis=1, tiled=True),
    )
    gate_every, up_every, act_every = (
        lax.all_gather(gate_grad_low, "group", axis=1, tiled=True),
        lax.all_gather(up_grad_low, "group", axis=1, tiled=True),
        lax.all_gather(act_low, "group", axis=1, tiled=True),
    )
    expert_shares = (
        jnp.einsum("ecd,ecf->edf", rows_cols, gate_every, preferred_element_type=jnp.float32),
        jnp.einsum("ecd,ecf->edf", rows_cols, up_every, preferred_element_type=jnp.float32),
        jnp.einsum("ecd,ecf->edf", out_cols, act_every, preferred_element_type=jnp.float32),
    )
    slot_grad = jnp.einsum(
        "ecf,edf->ecd", gate_grad_low, expert_set[0], preferred_element_type=jnp.float32
    )
    slot_grad = slot_grad + jnp.einsum(
        "ecf,edf->ecd", up_grad_low, expert_set[1], preferred_element_type=jnp.float32
    )
    moe_grad = jnp.sum(
        slot_grad.reshape(slot_total, D)[slot_of_pair].reshape(row_count, TOPK, D), axis=1
    )
    attn_set = (
        lax.all_gather(attention_gain, "group", axis=0, tiled=True),
        lax.all_gather(query_weight, "group", axis=0, tiled=True),
        lax.all_gather(key_weight, "group", axis=0, tiled=True),
        lax.all_gather(value_weight, "group", axis=0, tiled=True),
        lax.all_gather(output_weight, "group", axis=0, tiled=True),
        lax.all_gather(query_gain, "group", axis=0, tiled=True),
        lax.all_gather(key_gain, "group", axis=0, tiled=True),
        lax.all_gather(mixture_gain, "group", axis=0, tiled=True),
        lax.all_gather(router_weight, "group", axis=0, tiled=True),
    )
    chosen_grad = gates * (gates_grad - jnp.sum(gates * gates_grad, axis=-1, keepdims=True))
    logit_grad_low = jnp.einsum("tk,tke->te", chosen_grad, onehot).astype(jnp.bfloat16)
    router_partial = jnp.einsum(
        "td,te->de", moe_low, logit_grad_low, preferred_element_type=jnp.float32
    )
    moe_grad = moe_grad + jnp.einsum(
        "te,de->td", logit_grad_low, attn_set[8], preferred_element_type=jnp.float32
    )
    hidden_part, mixture_terms = rms_back(hidden, moe_factor, attn_set[7], moe_grad)
    mixture_partial = jnp.sum(mixture_terms, axis=0)
    hidden_grad = upstream + hidden_part
    attn_grad_low = hidden_grad.astype(jnp.bfloat16)
    output_partial = jnp.einsum(
        "td,tf->df", attn_grad_low, mixed_low, preferred_element_type=jnp.float32
    )
    mixed_grad_low = jnp.dot(attn_grad_low, attn_set[4], preferred_element_type=jnp.float32).astype(
        jnp.bfloat16
    )
    mixed_grad_heads = mixed_grad_low.reshape(row_count, HK, group_width, HD)
    delta = jnp.transpose(
        jnp.sum(
            mixed_grad_heads.astype(jnp.float32) * mixed.reshape(row_count, HK, group_width, HD),
            axis=-1,
        ),
        (1, 2, 0),
    )
    key_every, value_every = (
        lax.all_gather(key_low, "ctx", axis=0, tiled=True),
        lax.all_gather(value_low, "ctx", axis=0, tiled=True),
    )
    total_rows = key_every.shape[0]
    span = 512

    def back_block(query_accum, number):
        block_start = number * span
        key_block = lax.dynamic_slice_in_dim(key_every, block_start, span, 0)
        value_block = lax.dynamic_slice_in_dim(value_every, block_start, span, 0)
        allowed = allowed_mask(block_start, span)

        def back_compute(unused):
            scores = (
                jnp.einsum(
                    "tkgd,skd->kgts", query_low, key_block, preferred_element_type=jnp.float32
                )
                * scaling
            )
            probs = jnp.where(allowed, jnp.exp(scores - log_total[..., None]), 0.0)
            prob_grad = jnp.einsum(
                "tkgd,skd->kgts", mixed_grad_heads, value_block, preferred_element_type=jnp.float32
            )
            score_grad = (probs * (prob_grad - delta[..., None])).astype(jnp.bfloat16)
            query_part = (
                jnp.einsum(
                    "kgts,skd->tkgd", score_grad, key_block, preferred_element_type=jnp.float32
                )
                * scaling
            )
            key_part = (
                jnp.einsum(
                    "kgts,tkgd->skd", score_grad, query_low, preferred_element_type=jnp.float32
                )
                * scaling
            )
            value_part = jnp.einsum(
                "kgts,tkgd->skd",
                probs.astype(jnp.bfloat16),
                mixed_grad_heads,
                preferred_element_type=jnp.float32,
            )
            return (query_part, key_part, value_part)

        def skipped(unused):
            return (
                jnp.zeros((row_count, HK, group_width, HD), jnp.float32),
                jnp.zeros((span, HK, HD), jnp.float32),
                jnp.zeros((span, HK, HD), jnp.float32),
            )

        useful = (block_start <= latest) & (block_start + span - 1 >= earliest)
        query_part, key_part, value_part = lax.cond(useful, back_compute, skipped, number)
        return (query_accum + query_part, (key_part, value_part))

    query_grad, (key_parts, value_parts) = lax.scan(
        back_block,
        jnp.zeros((row_count, HK, group_width, HD), jnp.float32),
        jnp.arange(total_rows // span, dtype=jnp.int32),
    )
    key_grad, value_grad = (
        lax.psum_scatter(
            key_parts.reshape(total_rows, HK, HD).astype(jnp.bfloat16),
            "ctx",
            scatter_dimension=0,
            tiled=True,
        ).astype(jnp.float32),
        lax.psum_scatter(
            value_parts.reshape(total_rows, HK, HD).astype(jnp.bfloat16),
            "ctx",
            scatter_dimension=0,
            tiled=True,
        ).astype(jnp.float32),
    )
    query_rot = rotate_back(query_grad.reshape(row_count, HQ, HD), cosine, sine)
    query_raw_grad, query_terms = rms_back(query_raw, query_factor, attn_set[5], query_rot)
    key_rot = rotate_back(key_grad, cosine, sine)
    key_raw_grad, key_terms = rms_back(key_raw, key_factor, attn_set[6], key_rot)
    query_gain_partial = jnp.sum(query_terms, axis=(0, 1))
    key_gain_partial = jnp.sum(key_terms, axis=(0, 1))
    query_raw_low = query_raw_grad.reshape(row_count, HQ * HD).astype(jnp.bfloat16)
    key_raw_low = key_raw_grad.reshape(row_count, HK * HD).astype(jnp.bfloat16)
    value_raw_low = value_grad.reshape(row_count, HK * HD).astype(jnp.bfloat16)
    query_partial = jnp.einsum(
        "td,tf->df", normed_low, query_raw_low, preferred_element_type=jnp.float32
    )
    key_partial = jnp.einsum(
        "td,tf->df", normed_low, key_raw_low, preferred_element_type=jnp.float32
    )
    value_partial = jnp.einsum(
        "td,tf->df", normed_low, value_raw_low, preferred_element_type=jnp.float32
    )
    normed_grad = jnp.einsum(
        "tf,df->td", query_raw_low, attn_set[1], preferred_element_type=jnp.float32
    )
    normed_grad = normed_grad + jnp.einsum(
        "tf,df->td", key_raw_low, attn_set[2], preferred_element_type=jnp.float32
    )
    normed_grad = normed_grad + jnp.einsum(
        "tf,df->td", value_raw_low, attn_set[3], preferred_element_type=jnp.float32
    )
    input_part, attention_terms = rms_back(inputs, attn_factor, attn_set[0], normed_grad)
    attention_partial = jnp.sum(attention_terms, axis=0)
    tokens_grad = (hidden_grad + input_part).astype(jnp.bfloat16)[None]
    attn_shares = (
        lax.psum_scatter(
            attention_partial.astype(jnp.bfloat16), "group", scatter_dimension=0, tiled=True
        ).astype(jnp.float32),
        lax.psum_scatter(
            query_partial.astype(jnp.bfloat16), "group", scatter_dimension=0, tiled=True
        ).astype(jnp.float32),
        lax.psum_scatter(
            key_partial.astype(jnp.bfloat16), "group", scatter_dimension=0, tiled=True
        ).astype(jnp.float32),
        lax.psum_scatter(
            value_partial.astype(jnp.bfloat16), "group", scatter_dimension=0, tiled=True
        ).astype(jnp.float32),
        lax.psum_scatter(
            output_partial.astype(jnp.bfloat16), "group", scatter_dimension=0, tiled=True
        ).astype(jnp.float32),
        lax.psum_scatter(
            query_gain_partial.astype(jnp.bfloat16), "group", scatter_dimension=0, tiled=True
        ).astype(jnp.float32),
        lax.psum_scatter(
            key_gain_partial.astype(jnp.bfloat16), "group", scatter_dimension=0, tiled=True
        ).astype(jnp.float32),
        lax.psum_scatter(
            mixture_partial.astype(jnp.bfloat16), "group", scatter_dimension=0, tiled=True
        ).astype(jnp.float32),
        lax.psum_scatter(
            router_partial.astype(jnp.bfloat16), "group", scatter_dimension=0, tiled=True
        ).astype(jnp.float32),
    )
    finished = (
        lax.psum(attn_shares[0].astype(jnp.bfloat16), "ctx").astype(jnp.float32),
        lax.psum(attn_shares[1].astype(jnp.bfloat16), "ctx").astype(jnp.float32),
        lax.psum(attn_shares[2].astype(jnp.bfloat16), "ctx").astype(jnp.float32),
        lax.psum(attn_shares[3].astype(jnp.bfloat16), "ctx").astype(jnp.float32),
        lax.psum(attn_shares[4].astype(jnp.bfloat16), "ctx").astype(jnp.float32),
        lax.psum(attn_shares[5].astype(jnp.bfloat16), "ctx").astype(jnp.float32),
        lax.psum(attn_shares[6].astype(jnp.bfloat16), "ctx").astype(jnp.float32),
        lax.psum(attn_shares[7].astype(jnp.bfloat16), "ctx").astype(jnp.float32),
        lax.psum(attn_shares[8].astype(jnp.bfloat16), "ctx").astype(jnp.float32),
        lax.psum(expert_shares[0].astype(jnp.bfloat16), "ctx").astype(jnp.float32),
        lax.psum(expert_shares[1].astype(jnp.bfloat16), "ctx").astype(jnp.float32),
        lax.psum(expert_shares[2].astype(jnp.bfloat16), "ctx").astype(jnp.float32),
    )
    return (
        layer_out,
        tokens_grad,
        finished[0],
        finished[1],
        finished[2],
        finished[3],
        finished[4],
        finished[5],
        finished[6],
        finished[7],
        finished[8],
        finished[9],
        finished[10],
        finished[11],
    )


def solution(mesh):
    return jax.shard_map(
        per_device,
        mesh=mesh,
        in_specs=(
            P("group", "ctx", None),
            P("group", "ctx"),
            P("group", "ctx", None),
            P("group", "ctx", None),
            P("group"),
            P("group", None),
            P("group", None),
            P("group", None),
            P("group", None),
            P("group"),
            P("group"),
            P("group"),
            P("group", None),
            P(None, "group", None),
            P(None, "group", None),
            P(None, "group", None),
        ),
        out_specs=(
            P("group", "ctx", None),
            P("group", "ctx", None),
            P("group"),
            P("group", None),
            P("group", None),
            P("group", None),
            P("group", None),
            P("group"),
            P("group"),
            P("group"),
            P("group", None),
            P(None, "group", None),
            P(None, "group", None),
            P(None, "group", None),
        ),
        check_vma=False,
    )
```

profile of v0, /device:TPU:17, one launch (start us, length us, event | category | flops | bytes accessed | tf_op | source)
XLA Modules:
  0.0 3878.3 jit_solution(12172570764174206456)
XLA Ops:
  55.1 28.4 all-gather.21.cloned.1.call-done
  128.4 139.5 %all-gather.19.cloned.1.call-done = bf16[2048,4096]{1,0:T(8,128)(2,1)} async-done(((bf16[512,4096]{1,0:T(8,128)(2,1)}), bf16[2048,4096]{1,0:T(8,128)(2,1)}) %all-gather.19.cloned.1.call-update) | async-done | bytes 16777232 | tf_op jit(solution)/shard_map/all_gather | solution.py:88
  323.5 127.4 %all-gather.25.cloned.1.call-done = bf16[2048,4096]{1,0:T(8,128)(2,1)} async-done(((bf16[512,4096]{1,0:T(8,128)(2,1)}), bf16[2048,4096]{1,0:T(8,128)(2,1)}) %all-gather.25.cloned.1.call-update) | async-done | bytes 16777232 | tf_op jit(solution)/shard_map/all_gather | solution.py:91
  517.3 373.3 %all-gather.27.cloned.1.call-done = bf16[16,2048,768]{2,1,0:T(8,128)(2,1)} async-done(((bf16[16,512,768]{2,1,0:T(8,128)(2,1)}), bf16[16,2048,768]{2,1,0:T(8,128)(2,1)}) %all-gather.27.cloned.1.call-update) | async-done | bytes 50331664 | tf_op jit(solution)/shard_map/all_gather | solution.py:98
  890.6 30.4 fusion.115
  921.1 409.3 %all-gather.29.cloned.1.call-done = bf16[16,2048,768]{2,1,0:T(8,128)(2,1)} async-done(((bf16[16,512,768]{2,1,0:T(8,128)(2,1)}), bf16[16,2048,768]{2,1,0:T(8,128)(2,1)}) %all-gather.29.cloned.1.call-update) | async-done | bytes 50331664 | tf_op jit(solution)/shard_map/all_gather | solution.py:99
  1330.4 30.3 fusion.116
  1360.7 409.5 %all-gather.31.cloned.1.call-done = bf16[16,2048,768]{2,1,0:T(8,128)(2,1)} async-done(((bf16[16,512,768]{2,1,0:T(8,128)(2,1)}), bf16[16,2048,768]{2,1,0:T(8,128)(2,1)}) %all-gather.31.cloned.1.call-update) | async-done | bytes 50331664 | tf_op jit(solution)/shard_map/all_gather | solution.py:100
  1770.2 24.8 multiply_convert_fusion.1
  1795.0 26.3 fusion.118
  1821.3 29.6 convolution_add_fusion
  1869.9 24.8 fusion.117
  1932.3 29.6 while.25
  1967.8 34.0 reduce-scatter.22.cloned.1.call-done
  2005.6 29.3 reduce-scatter.10.cloned.1.call-done
  2082.4 119.4 %all-to-all-done = bf16[16,96,2048]{1,0,2:T(8,128)(2,1)} async-done(((bf16[16,96,2048]{1,0,2:T(8,128)(2,1)}), bf16[16,96,2048]{1,0,2:T(8,128)(2,1)}, u32[]{:S(2)}, u32[]{:S(2)}) %all-to-all-start) | async-done | bytes 6291488 | tf_op jit(solution)/shard_map/all_to_all | solution.py:238
  2225.7 105.0 %all-to-all-done.1 = bf16[16,96,2048]{1,0,2:T(8,128)(2,1)} async-done(((bf16[16,96,2048]{1,0,2:T(8,128)(2,1)}), bf16[16,96,2048]{1,0,2:T(8,128)(2,1)}, u32[]{:S(2)}, u32[]{:S(2)}) %all-to-all-start.1) | async-done | bytes 6291488 | tf_op jit(solution)/shard_map/all_to_all | solution.py:239
  2364.8 27.2 all-gather.35.cloned.1.call-done
  2406.7 83.4 %all-gather.37.cloned.1.call-done = bf16[16,384,768]{2,1,0:T(8,128)(2,1)} async-done(((bf16[16,96,768]{2,1,0:T(8,128)(2,1)}), bf16[16,384,768]{2,1,0:T(8,128)(2,1)}) %all-gather.37.cloned.1.call-update) | async-done | bytes 9437200 | tf_op jit(solution)/shard_map/all_gather | solution.py:244
  2528.2 38.3 reduce-scatter.16.cloned.1.call-done
  2566.5 157.3 %reduce-scatter.12.cloned.1.call-done = bf16[512,4096]{1,0:T(8,128)(2,1)} async-done(((bf16[2048,4096]{1,0:T(8,128)(2,1)}), bf16[512,4096]{1,0:T(8,128)(2,1)}) %reduce-scatter.12.cloned.1.call-update) | async-done | bytes 4194320 | tf_op jit(solution)/shard_map/reduce_scatter | solution.py:406
  2723.8 157.4 %reduce-scatter.18.cloned.1.call-done = bf16[512,4096]{1,0:T(8,128)(2,1)} async-done(((bf16[2048,4096]{1,0:T(8,128)(2,1)}), bf16[512,4096]{1,0:T(8,128)(2,1)}) %reduce-scatter.18.cloned.1.call-update) | async-done | bytes 4194320 | tf_op jit(solution)/shard_map/reduce_scatter | solution.py:415
  2908.0 23.5 all-reduce.6
  2935.6 887.2 %all-reduce.12.cloned.1.call-done = (bf16[512,4096]{1,0:T(8,128)(2,1)}, bf16[512,512]{1,0:T(8,128)(2,1)}, bf16[512,512]{1,0:T(8,128)(2,1)}, bf16[512,4096]{1,0:T...) async-done(((bf16[512,4096]{1,0:T(8,128)(2,1)}, bf16[512,512]{1,0:T(8,128)(2,1)}, ...) | async-done | bytes 47185936 | tf_op jit(solution)/shard_map/psum | solution.py:433
  (430 shorter events, 573.8 us)
Async XLA Ops:
  7.2 39.1 %all-gather.15.cloned.1.call-start = ((), (), s32[]{:S(2)}) async-start(), calls=%async_computation.9 | async-start | bytes 2621440 | tf_op jit(solution)/shard_map/all_gather | solution.py:89
  7.9 75.6 %all-gather.21.cloned.1.call-start = ((), (), s32[]{:S(2)}) async-start(), calls=%async_computation.12 | async-start | bytes 2621440 | tf_op jit(solution)/shard_map/all_gather | solution.py:90
  8.7 117.3 %all-gather.17.cloned.1.call-start = ((), (), s32[]{:S(2)}) async-start(), calls=%async_computation.10 | async-start | bytes 1179648 | tf_op jit(solution)/shard_map/all_gather | solution.py:137
  54.4 213.5 %all-gather.19.cloned.1.call-start = ((), (), s32[]{:S(2)}) async-start(), calls=%async_computation.11 | async-start | bytes 20971520 | tf_op jit(solution)/shard_map/all_gather | solution.py:88
  55.0 246.9 %all-gather.23.cloned.1.call-start = ((), (), s32[]{:S(2)}) async-start(), calls=%async_computation.13 | async-start | bytes 1179648 | tf_op jit(solution)/shard_map/all_gather | solution.py:138
  86.3 364.6 %all-gather.25.cloned.1.call-start = ((), (), s32[]{:S(2)}) async-start(), calls=%async_computation.14 | async-start | bytes 20971520 | tf_op jit(solution)/shard_map/all_gather | solution.py:91
  86.9 803.8 %all-gather.27.cloned.1.call-start = ((), (), s32[]{:S(2)}) async-start(), calls=%async_computation.15 | async-start | bytes 62914560 | tf_op jit(solution)/shard_map/all_gather | solution.py:98
  87.6 1242.8 %all-gather.29.cloned.1.call-start = ((), (), s32[]{:S(2)}) async-start(), calls=%async_computation.16 | async-start | bytes 62914560 | tf_op jit(solution)/shard_map/all_gather | solution.py:99
  88.4 1681.8 %all-gather.31.cloned.1.call-start = ((), (), s32[]{:S(2)}) async-start(), calls=%async_computation.17 | async-start | bytes 62914560 | tf_op jit(solution)/shard_map/all_gather | solution.py:100
  89.2 1912.6 %reduce-scatter.22.cloned.1.call-start = ((), (), s32[]{:S(2)}) async-start(), calls=%async_computation.27 | async-start | bytes 1179648
  97.0 365.9 %copy-start.50 = (f32[4,1,512]{2,1,0:T(1,128)}, f32[4,1,512]{2,1,0:T(1,128)S(1)}, u32[]{:S(2)}) copy-start(f32[4,1,512]{2,1,0:T(1,128)S(1)} %convert_element_type.334) | copy-start | bytes 24580
  125.4 377.1 %copy-start.37 = (bf16[2048,16]{0,1:T(8,128)(2,1)}, bf16[2048,16]{0,1:T(8,128)(2,1)S(1)}, u32[]{:S(2)}) copy-start(bf16[2048,16]{0,1:T(8,128)(2,1)S(1)} %all_gather.75) | copy-start | bytes 196612
  1965.1 69.8 %reduce-scatter.10.cloned.1.call-start = ((), (), s32[]{:S(2)}) async-start(), calls=%async_computation.18 | async-start | bytes 1179648 | tf_op jit(solution)/shard_map/reduce_scatter | solution.py:365
  1965.9 384.4 %all-gather.33.cloned.1.call-start = ((), (), s32[]{:S(2)}) async-start(), calls=%async_computation.24 | async-start | bytes 11796480 | tf_op jit(solution)/shard_map/all_gather | solution.py:242
  1966.5 425.6 %all-gather.35.cloned.1.call-start = ((), (), s32[]{:S(2)}) async-start(), calls=%async_computation.25 | async-start | bytes 11796480 | tf_op jit(solution)/shard_map/all_gather | solution.py:243
  1967.2 523.0 %all-gather.37.cloned.1.call-start = ((), (), s32[]{:S(2)}) async-start(), calls=%async_computation.26 | async-start | bytes 11796480 | tf_op jit(solution)/shard_map/all_gather | solution.py:244
  1967.8 560.4 %reduce-scatter.14.cloned.1.call-start = ((), (), s32[]{:S(2)}) async-start(), calls=%async_computation.20 | async-start | bytes 2621440 | tf_op jit(solution)/shard_map/reduce_scatter | solution.py:409
  2005.5 561.0 %reduce-scatter.16.cloned.1.call-start = ((), (), s32[]{:S(2)}) async-start(), calls=%async_computation.21 | async-start | bytes 2621440 | tf_op jit(solution)/shard_map/reduce_scatter | solution.py:412
  2038.1 685.7 %reduce-scatter.12.cloned.1.call-start = ((), (), s32[]{:S(2)}) async-start(), calls=%async_computation.19 | async-start | bytes 20971520 | tf_op jit(solution)/shard_map/reduce_scatter | solution.py:406
  2054.8 826.3 %reduce-scatter.18.cloned.1.call-start = ((), (), s32[]{:S(2)}) async-start(), calls=%async_computation.22 | async-start | bytes 20971520 | tf_op jit(solution)/shard_map/reduce_scatter | solution.py:415
  2064.9 136.8 %all-to-all-start = ((bf16[16,96,2048]{1,0,2:T(8,128)(2,1)}), bf16[16,96,2048]{1,0,2:T(8,128)(2,1)}, u32[]{:S(2)}, u32[]{:S(2)}) async-start(bf16[16,96,2048]{1,0,2:T(8,128)(2,1)} %broadcast_select_fusion), calls=%async_computation.6 | async-start | bytes 16777216 | tf_op jit(solution)/shard_map/all_to_all | solution.py:238
  2201.7 129.0 %all-to-all-start.1 = ((bf16[16,96,2048]{1,0,2:T(8,128)(2,1)}), bf16[16,96,2048]{1,0,2:T(8,128)(2,1)}, u32[]{:S(2)}, u32[]{:S(2)}) async-start(bf16[16,96,2048]{1,0,2:T(8,128)(2,1)} %copy.241), calls=%async_computation.7 | async-start | bytes 16777216 | tf_op jit(solution)/shard_map/all_to_all | solution.py:239
  2207.4 700.5 %reduce-scatter.20.cloned.1.call-start = ((), (), s32[]{:S(2)}) async-start(), calls=%async_computation.23 | async-start | bytes 81920 | tf_op jit(solution)/shard_map/reduce_scatter | solution.py:427
  2350.3 1472.6 %all-reduce.12.cloned.1.call-start = ((), (), s32[]{:S(2)}) async-start(), calls=%async_computation.28 | async-start | bytes 94371840 | tf_op jit(solution)/shard_map/psum | solution.py:433
  (93 other events, 2879.2 us)
Sparse Core Ops, SparseCore 0:
  9.9 36.4 all-gather.14
  48.2 35.2 all-gather.20
  85.7 22.9 all-gather.16
  110.4 157.4 all-gather.18
  270.0 22.0 all-gather.22
  293.8 157.0 all-gather.24
  452.7 437.8 all-gather.26
  892.5 437.8 all-gather.28
  1332.3 437.8 all-gather.30
  1965.3 36.4 reduce-scatter.21
  2004.1 30.7 reduce-scatter.9
  2036.6 235.2 all-gather.32
  2273.8 118.2 all-gather.34
  2393.8 96.3 all-gather.36
  2493.0 35.1 reduce-scatter.13
  2531.3 35.1 reduce-scatter.15
  2570.0 153.7 reduce-scatter.11
  2727.3 153.8 reduce-scatter.17
  2884.5 23.4 reduce-scatter.19
  2912.3 910.4 all-reduce.11
where the time goes:
time: 3890 us; the launch traced here: 3880 us
  waiting for transfers between devices  3170 us (81%)
  matrix products  306 us (8%)
  local copies, waits for them, and re-layouts  191 us (5%)
  other arithmetic  116 us (3%)
  blocking collectives  56.4 us (1%)
    psum x1, waiting for transfers between devices, per_device(): lax.psum(attn_shares[1].astype(jnp.bfloat16), 'ctx').astype(jnp.float32)  887 us
    all_gather x1, waiting for transfers between devices, per_device(): lax.all_gather(down_weight, 'group', axis=1, tiled=True)  410 us
    all_gather x1, waiting for transfers between devices, per_device(): lax.all_gather(up_weight, 'group', axis=1, tiled=True)  409 us
    all_gather x1, waiting for transfers between devices, per_device(): lax.all_gather(gate_weight, 'group', axis=1, tiled=True)  373 us
    reduce_scatter x1, waiting for transfers between devices, per_device(): lax.psum_scatter(output_partial.astype(jnp.bfloat16), 'group', scatter_di...  157 us
    reduce_scatter x1, waiting for transfers between devices, per_device(): lax.psum_scatter(query_partial.astype(jnp.bfloat16), 'group', scatter_dim...  157 us
    all_gather x1, waiting for transfers between devices, per_device(): lax.all_gather(query_weight, 'group', axis=0, tiled=True)  140 us
    all_gather x1, waiting for transfers between devices, per_device(): lax.all_gather(output_weight, 'group', axis=0, tiled=True)  127 us
  transfers between devices with their start and end apart: 22, of which 19 were waited for; matrix products, arithmetic and copies ran while one was open for 10% of the time, Pallas kernels for 0%

commit v1 on v0

v1 whole, which is shorter than its diff:
```python
import functools

import jax
import jax.numpy as jnp
from jax import lax
from jax.experimental import pallas as pl
from jax.experimental.pallas import tpu as pltpu
from jax.sharding import PartitionSpec as P

D = 2048
HQ = 32
HK = 4
HD = 128
F = 768
TOPK = 8
EXPERTS = 16
PAD = 128

EPS = 1e-06
ROPE_BASE = 1000000.0
FLOOR = -1e30
F32 = jnp.float32
BF16 = jnp.bfloat16


def rms_parts(values, gains):
    factor = lax.rsqrt(jnp.mean(values * values, axis=-1, keepdims=True) + EPS)
    return (values * factor * gains, factor)


def rms_back(values, factor, gains, gradient):
    weighted = gradient * gains
    inner = jnp.mean(weighted * values, axis=-1, keepdims=True)
    grad_values = factor * weighted - values * (factor * factor * factor) * inner
    return (grad_values, gradient * values * factor)


def dot(left, right):
    return jnp.dot(left, right, preferred_element_type=F32)


def dot_nt(left, right):
    return lax.dot_general(left, right, (((1,), (1,)), ((), ())), preferred_element_type=F32)


def dot_tn(left, right):
    return lax.dot_general(left, right, (((0,), (0,)), ((), ())), preferred_element_type=F32)


def rope_tables(position_row):
    frequency = ROPE_BASE ** (-2.0 * jnp.arange(HD // 2, dtype=F32) / HD)
    angles = position_row.astype(F32)[:, None] * frequency[None, :]
    cosine, sine = jnp.cos(angles), jnp.sin(angles)
    return (
        jnp.concatenate([cosine, cosine], axis=-1),
        jnp.concatenate([-sine, sine], axis=-1),
    )


def turn(values):
    return pltpu.roll(values, HD // 2, 1)


def normed_rope(raw, gains, cosine, sine):
    normed, factor = rms_parts(raw, gains)
    return (normed * cosine + turn(normed) * sine, factor)


def masked_scores(query, key, doc_start, first_row, columns):
    scores = dot_nt(query, key) * (HD**-0.5)
    rows = query.shape[0]
    row_index = first_row + lax.broadcasted_iota(jnp.int32, (rows, columns), 0)
    key_index = lax.broadcasted_iota(jnp.int32, (rows, columns), 1)
    allowed = (key_index <= row_index) & (key_index >= doc_start)
    return jnp.where(allowed, scores, FLOOR)


def attend_kernel(
    block, q_ref, kv_ref, doc_ref, cos_ref, sin_ref, qg_ref, kg_ref, out_ref, key_ref, val_ref
):
    length = kv_ref.shape[0]
    head, part = pl.program_id(0), pl.program_id(1)

    @pl.when((head == 0) & (part == 0))
    def _():
        key, unused = normed_rope(kv_ref[:, :HD], kg_ref[...], cos_ref[...], sin_ref[...])
        key_ref[...] = key.astype(BF16)
        val_ref[...] = kv_ref[:, HD:].astype(BF16)

    for number in range(length // block):

        @pl.when(part == number)
        def _():
            rows = pl.ds(number * block, block)
            columns = (number + 1) * block
            query, unused = normed_rope(q_ref[...], qg_ref[...], cos_ref[rows, :], sin_ref[rows, :])
            masked = masked_scores(
                query.astype(BF16), key_ref[:columns, :], doc_ref[...], number * block, columns
            )
            weights = jnp.exp(masked - jnp.max(masked, axis=-1, keepdims=True))
            total = jnp.sum(weights, axis=-1, keepdims=True)
            mixed = dot(weights.astype(BF16), val_ref[:columns, :])
            out_ref[...] = (mixed / total).astype(BF16)


def attend_back_kernel(
    block,
    q_ref,
    kv_ref,
    doc_ref,
    cos_ref,
    sin_ref,
    qg_ref,
    kg_ref,
    dm_ref,
    dq_ref,
    dkv_ref,
    qt_ref,
    kt_ref,
    key_ref,
    val_ref,
    dk_ref,
    dv_ref,
):
    length = kv_ref.shape[0]
    head, part = pl.program_id(0), pl.program_id(1)
    scaling = HD**-0.5

    @pl.when((head == 0) & (part == 0))
    def _():
        key, unused = normed_rope(kv_ref[:, :HD], kg_ref[...], cos_ref[...], sin_ref[...])
        key_ref[...] = key.astype(BF16)
        val_ref[...] = kv_ref[:, HD:].astype(BF16)
        dk_ref[...] = jnp.zeros_like(dk_ref)
        dv_ref[...] = jnp.zeros_like(dv_ref)
        qt_ref[...] = jnp.zeros_like(qt_ref)

    for number in range(length // block):

        @pl.when(part == number)
        def _():
            rows = pl.ds(number * block, block)
            columns = (number + 1) * block
            cosine, sine = cos_ref[rows, :], sin_ref[rows, :]
            raw = q_ref[...]
            query, factor = normed_rope(raw, qg_ref[...], cosine, sine)
            query = query.astype(BF16)
            key, value = key_ref[:columns, :], val_ref[:columns, :]
            upstream = dm_ref[...]
            masked = masked_scores(query, key, doc_ref[...], number * block, columns)
            weights = jnp.exp(masked - jnp.max(masked, axis=-1, keepdims=True))
            probs = weights / jnp.sum(weights, axis=-1, keepdims=True)
            prob_grad = dot_nt(upstream, value)
            delta = jnp.sum(probs * prob_grad, axis=-1, keepdims=True)
            score_grad = (probs * (prob_grad - delta)).astype(BF16)
            dk_ref[:columns, :] += dot_tn(score_grad, query)
            dv_ref[:columns, :] += dot_tn(probs.astype(BF16), upstream)
            rotated = dot(score_grad, key) * scaling
            query_grad = rotated * cosine - turn(rotated) * sine
            raw_grad, terms = rms_back(raw, factor, qg_ref[...], query_grad)
            dq_ref[...] = raw_grad.astype(BF16)
            qt_ref[...] += jnp.sum(terms, axis=0, keepdims=True)

    @pl.when((head == pl.num_programs(0) - 1) & (part == pl.num_programs(1) - 1))
    def _():
        raw = kv_ref[:, :HD]
        cosine, sine = cos_ref[...], sin_ref[...]
        unused, factor = rms_parts(raw, kg_ref[...])
        rotated = dk_ref[...] * scaling
        key_grad = rotated * cosine - turn(rotated) * sine
        raw_grad, terms = rms_back(raw, factor, kg_ref[...], key_grad)
        dkv_ref[:, :HD] = raw_grad
        dkv_ref[:, HD:] = dv_ref[...]
        kt_ref[...] = jnp.sum(terms, axis=0, keepdims=True)


def attention_specs(length, block):
    whole = lambda h, b: (0, 0)
    return [
        pl.BlockSpec((block, HD), lambda h, b: (b, h)),
        pl.BlockSpec((length, 2 * HD), whole),
        pl.BlockSpec((block, 1), lambda h, b: (b, 0)),
        pl.BlockSpec((length, HD), whole),
        pl.BlockSpec((length, HD), whole),
        pl.BlockSpec((1, HD), whole),
        pl.BlockSpec((1, HD), whole),
    ]


def attend(query_raw, kv_raw, doc_start, cosine, sine, query_gain, key_gain):
    length, width = query_raw.shape
    block = 256
    return pl.pallas_call(
        functools.partial(attend_kernel, block),
        out_shape=jax.ShapeDtypeStruct((length, width), BF16),
        grid_spec=pltpu.PrefetchScalarGridSpec(
            num_scalar_prefetch=0,
            grid=(width // HD, length // block),
            in_specs=attention_specs(length, block),
            out_specs=pl.BlockSpec((block, HD), lambda h, b: (b, h)),
            scratch_shapes=[pltpu.VMEM((length, HD), BF16), pltpu.VMEM((length, HD), BF16)],
        ),
        cost_estimate=pl.CostEstimate(
            flops=3 * length * length * width,
            bytes_accessed=length * width * 6,
            transcendentals=length * length * width // HD // 2,
        ),
        name="attend",
    )(query_raw, kv_raw, doc_start, cosine, sine, query_gain, key_gain)


def attend_back(query_raw, kv_raw, doc_start, cosine, sine, query_gain, key_gain, upstream):
    length, width = query_raw.shape
    block = 256
    whole = lambda h, b: (0, 0)
    return pl.pallas_call(
        functools.partial(attend_back_kernel, block),
        out_shape=(
            jax.ShapeDtypeStruct((length, width), BF16),
            jax.ShapeDtypeStruct((length, 2 * HD), F32),
            jax.ShapeDtypeStruct((1, HD), F32),
            jax.ShapeDtypeStruct((1, HD), F32),
        ),
        grid_spec=pltpu.PrefetchScalarGridSpec(
            num_scalar_prefetch=0,
            grid=(width // HD, length // block),
            in_specs=attention_specs(length, block)
            + [pl.BlockSpec((block, HD), lambda h, b: (b, h))],
            out_specs=(
                pl.BlockSpec((block, HD), lambda h, b: (b, h)),
                pl.BlockSpec((length, 2 * HD), whole),
                pl.BlockSpec((1, HD), whole),
                pl.BlockSpec((1, HD), whole),
            ),
            scratch_shapes=[
                pltpu.VMEM((length, HD), BF16),
                pltpu.VMEM((length, HD), BF16),
                pltpu.VMEM((length, HD), F32),
                pltpu.VMEM((length, HD), F32),
            ],
        ),
        cost_estimate=pl.CostEstimate(
            flops=7 * length * length * width,
            bytes_accessed=length * width * 8,
            transcendentals=length * length * width // HD // 2,
        ),
        name="attend_back",
    )(query_raw, kv_raw, doc_start, cosine, sine, query_gain, key_gain, upstream)


def ctx_place():
    here = lax.axis_index("ctx")
    return (here // 2, lax.rem(here, 2))


def peer(chip, core):
    return {"ctx": 2 * chip + core}


def greet(chips, owners=1):
    chip, core = ctx_place()
    group = lax.axis_index("group")
    barrier = pltpu.get_barrier_semaphore()
    pl.semaphore_signal(barrier, inc=1, device_id=peer(chip, 1 - core))

    @pl.when(chip > 0)
    def _():
        pl.semaphore_signal(barrier, inc=1, device_id=peer(chip - 1, core))

    @pl.when(chip < chips - 1)
    def _():
        pl.semaphore_signal(barrier, inc=1, device_id=peer(chip + 1, core))

    bits = owners.bit_length() - 1
    for bit in range(bits):
        pl.semaphore_signal(barrier, inc=1, device_id={"group": group ^ (1 << bit)})
    count = 1 + bits + (chip > 0).astype(jnp.int32) + (chip < chips - 1).astype(jnp.int32)
    pl.semaphore_wait(barrier, count)


class Gather:
    def __init__(self, chips, source, target, sems):
        self.chips, self.source, self.target = chips, source, target
        self.up, self.down, self.side, self.near, self.cross, self.local = sems
        self.chip, self.core = ctx_place()
        self.rows = source.shape[0]

    def block(self, chip, core):
        start = pl.multiple_of((2 * chip + core) * self.rows, self.rows)
        return self.target.at[pl.ds(start, self.rows)]

    def hop(self, origin, sem, arrive, device, own=False):
        return pltpu.make_async_remote_copy(
            src_ref=self.source if own else self.block(origin, self.core),
            dst_ref=self.block(origin, self.core),
            send_sem=sem.at[origin],
            recv_sem=arrive.at[origin],
            device_id=device,
        )

    def to_up(self, origin, own=False):
        return self.hop(origin, self.up, self.near, peer(self.chip + 1, self.core), own)

    def to_down(self, origin, own=False):
        return self.hop(origin, self.down, self.near, peer(self.chip - 1, self.core), own)

    def to_side(self, origin, own=False):
        return self.hop(origin, self.side, self.cross, peer(self.chip, 1 - self.core), own)

    def mine(self):
        return pltpu.make_async_copy(self.source, self.block(self.chip, self.core), self.local)

    def start(self):
        @pl.when(self.chip < self.chips - 1)
        def _():
            self.to_up(self.chip, True).start()

        @pl.when(self.chip > 0)
        def _():
            self.to_down(self.chip, True).start()

        self.to_side(self.chip, True).start()
        self.mine().start()

    def step(self, distance):
        below, above = self.chip - distance, self.chip + distance

        @pl.when(below >= 0)
        def _():
            self.to_up(below).wait_recv()

            @pl.when(self.chip < self.chips - 1)
            def _():
                self.to_up(below).start()

            self.to_side(below).start()

        @pl.when(above < self.chips)
        def _():
            self.to_down(above).wait_recv()

            @pl.when(self.chip > 0)
            def _():
                self.to_down(above).start()

            self.to_side(above).start()

    def finish(self):
        self.mine().wait()
        for origin in range(self.chips):
            pltpu.make_async_remote_copy(
                src_ref=self.source,
                dst_ref=self.block(origin, 1 - self.core),
                send_sem=self.side.at[origin],
                recv_sem=self.cross.at[origin],
                device_id=peer(self.chip, 1 - self.core),
            ).wait_recv()
            self.to_side(origin).wait_send()

            @pl.when((origin <= self.chip) & (self.chip < self.chips - 1))
            def _():
                self.to_up(origin).wait_send()

            @pl.when((origin >= self.chip) & (self.chip > 0))
            def _():
                self.to_down(origin).wait_send()


def gather_sems(chips):
    return [pltpu.SemaphoreType.DMA((chips,))] * 5 + [pltpu.SemaphoreType.DMA]


class Scatter:
    def __init__(self, chips, tile, refs):
        self.chips, self.tile = chips, tile
        self.give, self.take, self.send, self.low, self.high, *self.sems = refs
        self.chip, self.core = ctx_place()

    def side(self, target):
        return pltpu.make_async_remote_copy(
            src_ref=self.give.at[target],
            dst_ref=self.take.at[target],
            send_sem=self.sems[0].at[target],
            recv_sem=self.sems[1].at[target],
            device_id=peer(self.chip, 1 - self.core),
        )

    def up(self, target):
        return pltpu.make_async_remote_copy(
            src_ref=self.send.at[target],
            dst_ref=self.low.at[target],
            send_sem=self.sems[2].at[target],
            recv_sem=self.sems[3].at[target],
            device_id=peer(self.chip + 1, self.core),
        )

    def down(self, target):
        return pltpu.make_async_remote_copy(
            src_ref=self.send.at[target],
            dst_ref=self.high.at[target],
            send_sem=self.sems[2].at[target],
            recv_sem=self.sems[4].at[target],
            device_id=peer(self.chip - 1, self.core),
        )

    def start(self):
        last = self.chips - 1
        for target in sorted(range(self.chips), key=lambda t: min(t, last - t)):
            self.give[target] = self.tile(2 * target + 1 - self.core).astype(BF16)
            self.side(target).start()

    def pairs(self, out):
        last = self.chips - 1
        for target in sorted(range(self.chips), key=lambda t: min(t, last - t)):
            value = self.tile(2 * target + self.core)
            self.side(target).wait_recv()
            value = value + self.take[target].astype(F32)
            self.send[target] = value.astype(BF16)

            @pl.when(self.chip == target)
            def _():
                out[...] = value

            if target == last:

                @pl.when(self.chip == 0)
                def _():
                    self.up(target).start()

            if target == 0:

                @pl.when(self.chip == last)
                def _():
                    self.down(target).start()

    def step(self, number):
        first, final = number, self.chips - 1 - number

        @pl.when(final > self.chip)
        def _():
            @pl.when(self.chip > 0)
            def _():
                self.up(final).wait_recv()
                self.send[final] = (
                    self.send[final].astype(F32) + self.low[final].astype(F32)
                ).astype(BF16)

            @pl.when((self.chip > 0) | (number > 0))
            def _():
                self.up(final).start()

        @pl.when(first < self.chip)
        def _():
            @pl.when(self.chip < self.chips - 1)
            def _():
                self.down(first).wait_recv()
                self.send[first] = (
                    self.send[first].astype(F32) + self.high[first].astype(F32)
                ).astype(BF16)

            @pl.when((self.chip < self.chips - 1) | (number > 0))
            def _():
                self.down(first).start()

    def finish(self, out):
        for target in range(self.chips):

            @pl.when(self.chip == target)
            def _():
                if target > 0:
                    self.up(target).wait_recv()
                    out[...] += self.low[target].astype(F32)
                if target < self.chips - 1:
                    self.down(target).wait_recv()
                    out[...] += self.high[target].astype(F32)

        for target in range(self.chips):
            self.side(target).wait_send()

            @pl.when(self.chip != target)
            def _():
                self.up(target).wait_send()


def scatter_scratch(chips, rows, width):
    return [pltpu.VMEM((chips, rows, width), BF16)] * 5 + [pltpu.SemaphoreType.DMA((chips,))] * 5


def row_block(ref, block, rows):
    return ref[pl.ds(pl.multiple_of(block * rows, rows), rows), :]


class GroupGather:
    def __init__(self, owners, source, target, sems):
        self.owners, self.source, self.target = owners, source, target
        self.sent, self.got, self.local = sems
        self.group = lax.axis_index("group")
        self.rows = source.shape[0]
        self.bits = list(range(owners.bit_length() - 1))
        self.orders = (self.bits, self.bits[::-1])

    def piece(self, mask, half):
        start = (self.group ^ mask) * self.rows + half * (self.rows // 2)
        return self.target.at[pl.ds(pl.multiple_of(start, self.rows // 2), self.rows // 2)]

    def held(self, half, stage):
        masks = [0]
        for bit in self.orders[half][:stage]:
            masks += [mask | 1 << bit for mask in masks]
        return masks

    def hop(self, half, stage, mask):
        bit = self.orders[half][stage]
        source = self.piece(mask, half)
        if mask == 0:
            source = self.source.at[pl.ds(half * (self.rows // 2), self.rows // 2)]
        return pltpu.make_async_remote_copy(
            src_ref=source,
            dst_ref=self.piece(mask, half),
            send_sem=self.sent.at[half, stage * self.owners + mask],
            recv_sem=self.got.at[half, mask | 1 << bit],
            device_id={"group": self.group ^ (1 << bit)},
        )

    def mine(self):
        start = pl.multiple_of(self.group * self.rows, self.rows)
        return pltpu.make_async_copy(
            self.source, self.target.at[pl.ds(start, self.rows)], self.local
        )

    def start(self):
        for half in range(2):
            self.hop(half, 0, 0).start()
        self.mine().start()

    def step(self, stage):
        for half in range(2):
            for mask in self.held(half, stage):
                self.hop(half, stage, mask).wait_recv()
            if stage + 1 < len(self.bits):
                for mask in self.held(half, stage + 1):
                    self.hop(half, stage + 1, mask).start()

    def finish(self):
        self.mine().wait()
        for half in range(2):
            for stage in self.bits:
                for mask in self.held(half, stage):
                    self.hop(half, stage, mask).wait_send()


def group_gather_sems(owners):
    bits = owners.bit_length() - 1
    return [
        pltpu.SemaphoreType.DMA((2, bits * owners)),
        pltpu.SemaphoreType.DMA((2, owners)),
        pltpu.SemaphoreType.DMA,
    ]


class GroupScatter:
    def __init__(self, owners, part, out, refs):
        self.owners, self.part, self.out = owners, part, out
        self.land, (self.sent, self.got) = refs[:-2], refs[-2:]
        self.group = lax.axis_index("group")
        self.bits = list(range(owners.bit_length() - 1))
        self.orders = (self.bits, self.bits[::-1])
        self.rows, self.columns = out.shape[0], out.shape[1] // 2

    def kept(self, half, stage):
        done = self.orders[half][: stage + 1]
        return [r for r in range(self.owners) if not any(r >> bit & 1 for bit in done)]

    def place(self, half, stage, piece):
        if stage == 0:
            start = pl.multiple_of((self.group ^ piece) * self.rows, self.rows)
            return self.part.at[pl.ds(start, self.rows), pl.ds(half * self.columns, self.columns)]
        return self.land[stage - 1].at[half, self.kept(half, stage - 1).index(piece)]

    def hop(self, half, stage, piece):
        bit = self.orders[half][stage]
        at = self.kept(half, stage).index(piece)
        return pltpu.make_async_remote_copy(
            src_ref=self.place(half, stage, piece | 1 << bit),
            dst_ref=self.land[stage].at[half, at],
            send_sem=self.sent.at[half, stage * self.owners + piece],
            recv_sem=self.got.at[half, stage * self.owners + piece],
            device_id={"group": self.group ^ (1 << bit)},
        )

    def begin(self, half, stage):
        for piece in self.kept(half, stage):
            self.hop(half, stage, piece).start()

    def start(self):
        for half in range(2):
            self.begin(half, 0)

    def step(self, stage):
        for half in range(2):
            for piece in self.kept(half, stage):
                self.hop(half, stage, piece).wait_recv()
                mine = self.place(half, stage, piece)
                theirs = self.land[stage].at[half, self.kept(half, stage).index(piece)]
                final = stage + 1 == len(self.bits)
                chunk = min(64, self.rows)

                @pl.loop(0, self.rows // chunk)
                def _(number):
                    rows = pl.ds(pl.multiple_of(number * chunk, chunk), chunk)
                    value = (mine[rows, :].astype(F32) + theirs[rows, :].astype(F32)).astype(BF16)
                    if final:
                        self.out[rows, half * self.columns : (half + 1) * self.columns] = value
                    else:
                        theirs[rows, :] = value

            if stage + 1 < len(self.bits):
                self.begin(half, stage + 1)

    def finish(self):
        for half in range(2):
            for stage in self.bits:
                for piece in self.kept(half, stage):
                    self.hop(half, stage, piece).wait_send()


def group_scatter_scratch(owners, rows, width):
    bits = owners.bit_length() - 1
    return [
        pltpu.VMEM((2, owners >> stage + 1, rows, width // 2), BF16) for stage in range(bits)
    ] + [pltpu.SemaphoreType.DMA((2, bits * owners))] * 2


def comm_kernel(plan, chips, owners, counts, *refs):
    refs = list(refs)

    def pop(count):
        taken = refs[:count]
        del refs[:count]
        return taken

    scatter_ins = pop(counts["scatter_ins"])
    gather_ins = pop(counts["gather"])
    group_gather_ins = pop(counts["group_gather"])
    group_scatter_ins = pop(counts["group_scatter"])
    scatter_outs = pop(counts["scatter"])
    gather_outs = pop(counts["gather"])
    group_gather_outs = pop(counts["group_gather"])
    group_scatter_outs = pop(counts["group_scatter"])
    chained_outs = pop(counts["chained"])
    bits = owners.bit_length() - 1
    transfers = {"out": scatter_outs}
    if counts["scatter"]:
        rows = scatter_outs[0].shape[0]
        left, weight = scatter_ins[0], scatter_ins[1] if len(scatter_ins) > 1 else None

        def tile(block):
            value = row_block(left, block, rows)
            return value.astype(F32) if weight is None else dot_nt(value, weight[...])

        transfers["scatter"] = Scatter(chips, tile, pop(10))
    transfers["gather"] = [
        Gather(chips, i, o, pop(6)) for i, o in zip(gather_ins, gather_outs, strict=True)
    ]
    transfers["group_gather"] = [
        GroupGather(owners, i, o, pop(3))
        for i, o in zip(group_gather_ins, group_gather_outs, strict=True)
    ]
    transfers["group_scatter"] = [
        GroupScatter(owners, i, o, pop(bits + 2))
        for i, o in zip(group_scatter_ins, group_scatter_outs, strict=True)
    ]
    transfers["chained"] = [
        Gather(chips, group_scatter_outs[i], o, pop(6)) for i, o in enumerate(chained_outs)
    ]
    greet(chips, owners if group_gather_ins or group_scatter_ins else 1)
    plan(transfers, chips, bits)


def comm_call(
    plan,
    number,
    name,
    parts,
    owners,
    micros,
    scatter=(),
    gather=(),
    group_gather=(),
    group_scatter=(),
    chained=0,
):
    chips = parts // 2
    operands = [*scatter, *gather, *group_gather, *group_scatter]
    in_specs = (
        [VMEM] * len(scatter)
        + [ANY] * (len(gather) + len(group_gather))
        + [VMEM] * len(group_scatter)
    )
    shapes, out_specs, scratch = [], [], []
    if scatter:
        rows = scatter[0].shape[0] // parts
        width = scatter[0].shape[1] if len(scatter) == 1 else scatter[1].shape[0]
        shapes.append(jax.ShapeDtypeStruct((rows, width), F32))
        out_specs.append(VMEM)
        scratch += scatter_scratch(chips, rows, width)
    for array in gather:
        shapes.append(jax.ShapeDtypeStruct((parts * array.shape[0], array.shape[1]), array.dtype))
        out_specs.append(ANY)
        scratch += gather_sems(chips)
    for array in group_gather:
        shapes.append(jax.ShapeDtypeStruct((owners * array.shape[0], array.shape[1]), array.dtype))
        out_specs.append(ANY)
        scratch += group_gather_sems(owners)
    for array in group_scatter:
        rows, width = array.shape[0] // owners, array.shape[1]
        shapes.append(jax.ShapeDtypeStruct((rows, width), BF16))
        out_specs.append(VMEM)
        scratch += group_scatter_scratch(owners, rows, width)
    for array in group_scatter[:chained]:
        rows, width = array.shape[0] // owners, array.shape[1]
        shapes.append(jax.ShapeDtypeStruct((parts * rows, width), BF16))
        out_specs.append(ANY)
        scratch += gather_sems(chips)
    counts = {
        "scatter_ins": len(scatter),
        "scatter": 1 if scatter else 0,
        "gather": len(gather),
        "group_gather": len(group_gather),
        "group_scatter": len(group_scatter),
        "chained": chained,
    }
    return pl.pallas_call(
        functools.partial(comm_kernel, plan, chips, owners, counts),
        out_shape=tuple(shapes),
        in_specs=in_specs,
        out_specs=tuple(out_specs),
        scratch_shapes=scratch,
        compiler_params=comm_params(number),
        cost_estimate=comm_cost(micros),
        name=name,
    )(*operands)


def plan_gather(transfers, chips, bits):
    for one in transfers["gather"] + transfers["group_gather"]:
        one.start()
    for number in range(max(chips - 1, bits)):
        if number < bits:
            for one in transfers["group_gather"]:
                one.step(number)
        if number < chips - 1:
            for one in transfers["gather"]:
                one.step(number + 1)
    for one in transfers["gather"] + transfers["group_gather"]:
        one.finish()


def plan_scatter(transfers, chips, bits):
    scatter, out = transfers["scatter"], transfers["out"][0]
    for one in transfers["group_scatter"]:
        one.start()
    scatter.start()
    scatter.pairs(out)
    for one in transfers["gather"]:
        one.start()
    for number in range(max(chips - 1, bits)):
        if number < chips - 1:
            scatter.step(number)
            for one in transfers["gather"]:
                one.step(number + 1)
        if number < bits:
            for one in transfers["group_scatter"]:
                one.step(number)
    scatter.finish(out)
    for one in transfers["gather"] + transfers["group_scatter"]:
        one.finish()


def plan_finish(transfers, chips, bits):
    scatters, chained = transfers["group_scatter"], transfers["chained"]
    for one in transfers["gather"] + scatters:
        one.start()
    for stage in range(bits):
        for one in scatters:
            one.step(stage)
    for one in chained:
        one.start()
    for number in range(1, chips):
        for one in transfers["gather"] + chained:
            one.step(number)
    for one in transfers["gather"] + chained + scatters:
        one.finish()


def plan_group_scatter(transfers, chips, bits):
    scatters, chained = transfers["group_scatter"], transfers["chained"]
    steps = [(one, stage) for one in scatters for stage in range(bits)]
    for one in scatters[:2]:
        one.start()
    waiting = list(scatters[2:])
    hops = []
    for one, stage in steps:
        one.step(stage)
        if stage == 0 and waiting:
            waiting.pop(0).start()
        at = scatters.index(one)
        if hops:
            hops.pop(0)()
        if stage == bits - 1 and at < len(chained):
            chained[at].start()
            hops += [functools.partial(chained[at].step, d) for d in range(1, chips)]
    for hop in hops:
        hop()
    for one in chained + scatters:
        one.finish()


def comm_params(number, limit=48):
    return pltpu.CompilerParams(
        collective_id=number, has_side_effects=True, vmem_limit_bytes=limit * 2**20
    )


def comm_cost(micros):
    return pl.CostEstimate(flops=0, bytes_accessed=int(micros * 3.4e6), transcendentals=0)


ANY = pl.BlockSpec(memory_space=pl.ANY)
VMEM = pl.BlockSpec(memory_space=pltpu.VMEM)


def widen_kernel(counts, *refs):
    sources, targets = refs[: len(counts)], refs[-sum(counts) :]
    at = 0
    for source, count in zip(sources, counts, strict=True):
        for number in range(count):
            targets[at][0, 0] = source[0, number].astype(F32)
            at += 1


def widen(packs, number, experts, previous=()):
    parts, unused, shard, width = packs[0].shape
    counts = [pack.shape[1] for pack in packs]
    total = sum(counts)
    shape = jax.ShapeDtypeStruct((parts, experts, shard, width), F32)
    block = pl.BlockSpec((1, 1, shard // 2, width), lambda c, h: (c, number, h, 0))
    return pl.pallas_call(
        functools.partial(widen_kernel, counts),
        out_shape=(shape,) * total,
        grid=(parts, 2),
        in_specs=[
            pl.BlockSpec((1, count, shard // 2, width), lambda c, h: (c, 0, h, 0))
            for count in counts
        ]
        + [ANY] * len(previous),
        out_specs=(block,) * total,
        input_output_aliases={len(packs) + i: i for i in range(len(previous))},
        cost_estimate=pl.CostEstimate(
            flops=0, bytes_accessed=sum(p.size for p in packs) * 6, transcendentals=0
        ),
        name="widen",
    )(*packs, *previous)


def finish_attention_kernel(sharers, packed_ref, q_ref, k_ref, v_ref, o_ref, sums_ref):
    width = o_ref.shape[1]
    share = 2 * HD // sharers
    at = pl.program_id(0)
    o_ref[...] = packed_ref[0, :, :width].astype(F32)
    q_ref[...] = packed_ref[0, :, width : 2 * width].astype(F32)
    for number in range(sharers):

        @pl.when(lax.rem(at, sharers) == number)
        def _():
            piece = packed_ref[0, :, 2 * width : 2 * width + share].astype(F32)
            start = number * share
            if start < HD:
                k_ref[:, start : start + share] = piece
            else:
                v_ref[:, start - HD : start - HD + share] = piece

    @pl.when(at == 0)
    def _():
        sums_ref[...] = jnp.zeros_like(sums_ref)

    sums_ref[...] += packed_ref[0, :, 2 * width + share :].astype(F32)


def finish_attention(packed, width, sharers):
    parts, shard, total = packed.shape
    spare = total - 2 * width - 2 * HD // sharers
    head = lambda c: (0, c // sharers)
    return pl.pallas_call(
        functools.partial(finish_attention_kernel, sharers),
        out_shape=(
            jax.ShapeDtypeStruct((shard, width * parts), F32),
            jax.ShapeDtypeStruct((shard, HK * HD), F32),
            jax.ShapeDtypeStruct((shard, HK * HD), F32),
            jax.ShapeDtypeStruct((shard, width * parts), F32),
            jax.ShapeDtypeStruct((shard, spare), F32),
        ),
        grid=(parts,),
        in_specs=[pl.BlockSpec((1, shard, total), lambda c: (c, 0, 0))],
        out_specs=(
            pl.BlockSpec((shard, width), lambda c: (0, c)),
            pl.BlockSpec((shard, HD), head),
            pl.BlockSpec((shard, HD), head),
            pl.BlockSpec((shard, width), lambda c: (0, c)),
            pl.BlockSpec((shard, spare), lambda c: (0, 0)),
        ),
        cost_estimate=pl.CostEstimate(flops=0, bytes_accessed=packed.size * 6, transcendentals=0),
        name="finish_attention",
    )(packed)


def per_device(
    tokens,
    positions,
    expert_ids,
    cotangent,
    attention_gain,
    query_weight,
    key_weight,
    value_weight,
    output_weight,
    query_gain,
    key_gain,
    mixture_gain,
    router_weight,
    gate_weight,
    up_weight,
    down_weight,
):
    parts, owners = lax.axis_size("ctx"), lax.axis_size("group")
    here, group = lax.axis_index("ctx"), lax.axis_index("group")
    rows = tokens.shape[1]
    length = rows * parts
    shard = query_weight.shape[0]
    width = HQ * HD // parts
    experts = EXPERTS // parts
    sharers = parts // HK
    key_head = here // sharers
    share = 2 * HD // sharers
    share_at = (here % sharers) * share

    gather_group = lambda v: lax.all_gather(v, "group", axis=0, tiled=True)

    def column(vector):
        return jnp.pad(vector, (0, shard - vector.shape[0]))[:, None]

    def columns(array, start, count):
        return lax.dynamic_slice_in_dim(array, start, count, 1)

    extras = jnp.concatenate(
        [
            router_weight,
            attention_gain[:, None],
            mixture_gain[:, None],
            column(query_gain),
            column(key_gain),
            jnp.zeros((shard, PAD - EXPERTS - 4), BF16),
        ],
        axis=1,
    )
    comm = lambda plan, number, name, micros, **transfers: comm_call(
        plan, number, name, parts, owners, micros, **transfers
    )
    inputs_all, positions_all, wqkv, wout = comm(
        plan_gather,
        0,
        "gather_tokens",
        45,
        gather=(tokens[0], jnp.broadcast_to(positions, (8, rows))),
        group_gather=(
            jnp.concatenate(
                [
                    columns(query_weight, here * width, width),
                    columns(key_weight, key_head * HD, HD),
                    columns(value_weight, key_head * HD, HD),
                    extras,
                ],
                axis=1,
            ),
            columns(output_weight, here * width, width),
        ),
    )
    at = width + 2 * HD
    extras = wqkv[:, at:]
    wqkv = wqkv[:, :at]
    router = extras[:, :EXPERTS]
    attention_gains = extras[:, EXPERTS].astype(F32)
    mixture_gains = extras[:, EXPERTS + 1].astype(F32)
    head_gain = (
        lambda col: extras[:, col]
        .reshape(owners, shard)[:, : HD // owners]
        .reshape(1, HD)
        .astype(F32)
    )
    query_gains, key_gains = head_gain(EXPERTS + 2), head_gain(EXPERTS + 3)

    def expert_pack(number, index):
        take = lambda w: lax.dynamic_index_in_dim(w, index * experts + number, 0, keepdims=False)
        return jnp.concatenate([take(gate_weight), take(up_weight), take(down_weight)], axis=1)

    later = lax.optimization_barrier((positions_all, here))[1]
    expert_weights = [gather_group(expert_pack(number, later)) for number in range(experts)]
    positions_all = positions_all.reshape(parts, 8, rows)[:, 0].reshape(length)
    doc_start = (jnp.arange(length, dtype=jnp.int32) - positions_all)[:, None]
    cosine, sine = rope_tables(positions_all)
    inputs = tokens[0].astype(F32)
    unused, attn_factor = rms_parts(inputs, attention_gains)
    normed_all = rms_parts(inputs_all.astype(F32), attention_gains)[0].astype(BF16)
    qkv_raw = dot(normed_all, wqkv)
    query_raw, kv_raw = qkv_raw[:, :width], qkv_raw[:, width:]
    tables = (query_raw, kv_raw, doc_start, cosine, sine, query_gains, key_gains)
    mixed_low = attend(*tables)
    attn_out, upstream_all = comm(
        plan_scatter,
        1,
        "scatter_attention",
        50,
        scatter=(mixed_low, wout),
        gather=(cotangent[0],),
    )
    hidden = inputs + attn_out
    moe_normed, moe_factor = rms_parts(hidden, mixture_gains)
    moe_low = moe_normed.astype(BF16)
    logits = dot(moe_low, router)
    onehot = (
        expert_ids[0][:, :, None] == jnp.arange(EXPERTS, dtype=jnp.int32)[None, None, :]
    ).astype(F32)
    chosen = jnp.sum(onehot * logits[:, None, :], axis=-1)
    expo = jnp.exp(chosen - jnp.max(chosen, axis=-1, keepdims=True))
    gates = expo / jnp.sum(expo, axis=-1, keepdims=True)
    combine = jnp.sum(gates[:, :, None] * onehot, axis=1)
    moe_all, combine_all = comm(
        plan_gather,
        2,
        "gather_mixture",
        45,
        gather=(moe_low, jnp.pad(combine, ((0, 0), (0, PAD - EXPERTS)))),
    )
    combine_all = columns(combine_all, here * experts, experts)

    layer_part = jnp.zeros((length, D), F32)
    moe_part = jnp.zeros((length, D), F32)
    combine_grads = []
    first_pieces, last_grads = [], []
    for number in range(experts):
        pack = expert_weights[number]
        if first_pieces:
            pack = lax.optimization_barrier((pack, *first_pieces[-1]))[0]
        gate_up, down = pack[:, : 2 * F], pack[:, 2 * F :]
        weight = combine_all[:, number : number + 1]
        gate_up_all = dot(moe_all, gate_up)
        gate_all, up_all = gate_up_all[:, :F], gate_up_all[:, F:]
        back_all = dot(upstream_all, down)
        sigmoid = lax.logistic(gate_all)
        act_low = (gate_all * sigmoid * up_all).astype(BF16)
        act = act_low.astype(F32)
        combine_grads.append(jnp.sum(act * back_all, axis=-1, keepdims=True))
        act_grad = weight * back_all
        gate_grad = (act_grad * up_all * sigmoid * (1.0 + gate_all * (1.0 - sigmoid))).astype(BF16)
        up_grad = (act_grad * gate_all * sigmoid).astype(BF16)
        weighted = (weight * act).astype(BF16)
        grads = (
            dot_tn(upstream_all, weighted).astype(BF16),
            dot_tn(moe_all, gate_grad).astype(BF16),
            dot_tn(moe_all, up_grad).astype(BF16),
        )
        if number < experts - 1:
            first_pieces.append(
                comm(
                    plan_group_scatter,
                    10 + number,
                    "scatter_expert",
                    80,
                    group_scatter=grads,
                    chained=1,
                )
            )
        else:
            last_grads = grads
        layer_part = layer_part + dot_nt(weighted, down)
        moe_part = moe_part + dot_nt(jnp.concatenate([gate_grad, up_grad], axis=1), gate_up)
    combine_grad = jnp.concatenate(combine_grads, axis=1)
    high = combine_grad.astype(BF16)
    low = (combine_grad - high.astype(F32)).astype(BF16)
    place = lambda v: lax.dynamic_update_slice_in_dim(
        jnp.zeros((length, EXPERTS), BF16), v, here * experts, 1
    )
    moe_pack = jnp.concatenate(
        [
            moe_part.astype(BF16),
            place(high),
            place(low),
            jnp.zeros((length, PAD - 2 * EXPERTS), BF16),
        ],
        axis=1,
    )
    moe_sum, *last_pieces = comm(
        plan_scatter,
        3,
        "scatter_mixture",
        80,
        scatter=(moe_pack,),
        group_scatter=last_grads,
    )
    stack_shape = lambda v: v.reshape(parts, -1, shard, F)
    expert_packs = [
        (stack_shape(pieces[3]), lax.all_gather(jnp.stack(pieces[1:3]), "ctx"))
        for pieces in first_pieces
    ] + [(lax.all_gather(jnp.stack(last_pieces), "ctx"),)]

    dcombine = moe_sum[:, D : D + EXPERTS] + moe_sum[:, D + EXPERTS : D + 2 * EXPERTS]
    gates_grad = jnp.sum(onehot * dcombine[:, None, :], axis=-1)
    chosen_grad = gates * (gates_grad - jnp.sum(gates * gates_grad, axis=-1, keepdims=True))
    logit_grad_low = jnp.sum(chosen_grad[:, :, None] * onehot, axis=1).astype(BF16)
    router_partial = dot_tn(moe_low, logit_grad_low)
    moe_grad = moe_sum[:, :D] + dot_nt(logit_grad_low, router)
    hidden_part, mixture_terms = rms_back(hidden, moe_factor, mixture_gains, moe_grad)
    mixture_partial = jnp.sum(mixture_terms, axis=0)
    hidden_grad = cotangent[0].astype(F32) + hidden_part

    layer_sum, attn_grad_all = comm(
        plan_scatter,
        4,
        "scatter_layer",
        60,
        scatter=(layer_part.astype(BF16),),
        gather=(hidden_grad.astype(BF16),),
    )
    layer_out = (hidden + layer_sum).astype(BF16)[None]
    mixed_grad = dot(attn_grad_all, wout).astype(BF16)
    output_partial = dot_tn(attn_grad_all, mixed_low).astype(BF16)
    query_low, kv_part, query_terms, key_terms = attend_back(*tables, mixed_grad)
    step = 1
    while step < sharers:
        kv_part = kv_part + lax.ppermute(kv_part, "ctx", [(i, i ^ step) for i in range(parts)])
        step *= 2
    kv_low = columns(kv_part.astype(BF16), share_at, share)
    qkv_low = jnp.concatenate([query_low, kv_low], axis=1)
    wqkv_share = jnp.concatenate(
        [wqkv[:, :width], columns(wqkv[:, width:], share_at, share)], axis=1
    )
    def head_column(terms):
        spread = terms.reshape(owners, HD // owners)
        return jnp.pad(spread, ((0, 0), (0, shard - HD // owners))).reshape(D, 1)

    spare = next(n for n in range(EXPERTS + 3, 1024) if (width + share + n) % 256 == 0)
    qkv_partial = jnp.concatenate(
        [
            dot_tn(normed_all, qkv_low),
            router_partial,
            mixture_partial[:, None],
            head_column(query_terms),
            head_column(key_terms),
            jnp.zeros((D, spare - EXPERTS - 3), F32),
        ],
        axis=1,
    ).astype(BF16)
    normed_grad, output_piece, qkv_piece = comm(
        plan_scatter,
        5,
        "scatter_normed",
        60,
        scatter=(qkv_low, wqkv_share),
        group_scatter=(output_partial, qkv_partial),
    )
    input_part, attention_terms = rms_back(inputs, attn_factor, attention_gains, normed_grad)
    tokens_grad = (hidden_grad + input_part).astype(BF16)[None]
    attention_partial = jnp.sum(attention_terms, axis=0)
    gain_rows = jnp.pad(attention_partial.reshape(owners, shard), ((0, 0), (0, D - shard)))
    attn_grads, unused, gain_parts = comm(
        plan_finish,
        6,
        "gather_grads",
        90,
        gather=(jnp.concatenate([output_piece, qkv_piece], axis=1),),
        group_scatter=(gain_rows.reshape(owners * 8, D // 8).astype(BF16),),
        chained=1,
    )
    attention_gain_grad = jnp.sum(gain_parts.reshape(parts, D)[:, :shard].astype(F32), axis=0)
    query_grad, key_grad, value_grad, output_grad, sums = finish_attention(
        attn_grads.reshape(parts, shard, -1), width, sharers
    )
    finished = ()
    for number in range(experts):
        finished = widen(expert_packs[number], number, experts, finished)
    whole = lambda v: v.reshape(EXPERTS, shard, F)
    return (
        layer_out,
        tokens_grad,
        attention_gain_grad,
        query_grad,
        key_grad,
        value_grad,
        output_grad,
        sums[: HD // owners, EXPERTS + 1],
        sums[: HD // owners, EXPERTS + 2],
        sums[:, EXPERTS],
        sums[:, :EXPERTS],
        whole(finished[1]),
        whole(finished[2]),
        whole(finished[0]),
    )


def solution(mesh):
    return jax.shard_map(
        per_device,
        mesh=mesh,
        in_specs=(
            P("group", "ctx", None),
            P("group", "ctx"),
            P("group", "ctx", None),
            P("group", "ctx", None),
            P("group"),
            P("group", None),
            P("group", None),
            P("group", None),
            P("group", None),
            P("group"),
            P("group"),
            P("group"),
            P("group", None),
            P(None, "group", None),
            P(None, "group", None),
            P(None, "group", None),
        ),
        out_specs=(
            P("group", "ctx", None),
            P("group", "ctx", None),
            P("group"),
            P("group", None),
            P("group", None),
            P("group", None),
            P("group", None),
            P("group"),
            P("group"),
            P("group"),
            P("group", None),
            P(None, "group", None),
            P(None, "group", None),
            P(None, "group", None),
        ),
        check_vma=False,
    )
```

time: 3890 us -> 1100 us (0.28)
  waiting for transfers between devices: 3170 us -> 0.11 us
  Pallas kernels: 0 us -> 832 us
  matrix products: 306 us -> 125 us
  local copies, waits for them, and re-layouts: 191 us -> 73.7 us
  other arithmetic: 116 us -> 30.2 us
  blocking collectives: 56.4 us -> 0 us
    all_gather x12 -> x4, waiting for transfers between devices: 1610 us -> 0.04 us  [the longest x2 0.04 us: per_device(): gather_group = lambda v: lax.all_gather(v, 'group', axis=0, tiled=True)]
    psum x1 -> x0, waiting for transfers between devices: 887 us -> none  [per_device(): lax.psum(attn_shares[1].astype(jnp.bfloat16), 'ctx').astype(jnp.float32)]
    pallas_call x0 -> x13, Pallas kernels: none -> 832 us  [the longest x8 733 us: comm_call(): pl.pallas_call(functools.partial(comm_kernel, plan, chips, owners, counts...]
    reduce_scatter x6 -> x0, waiting for transfers between devices: 406 us -> none  [the longest x1 157 us: per_device(): lax.psum_scatter(output_partial.astype(jnp.bfloat16), 'group', scatter_di...]
    all_to_all x2 -> x0, waiting for transfers between devices: 224 us -> none  [the longest x1 119 us: per_device(): lax.all_to_all(expert_rows, 'group', split_axis=2, concat_axis=1, tiled=T...]
    dot_general x31 -> x21, matrix products: 306 us -> 125 us  [the longest x7 45.4 us: dot(): return jnp.dot(left, right, preferred_element_type=F32)]
    convert_element_type x26 -> x9, other arithmetic: 63.9 us -> 3.73 us  [the longest x1 2.1 us: per_device(): mixture_gains = extras[:, EXPERTS + 1].astype(F32)]
    gather x5 -> x0, local copies, waits for them, and re-layouts: 55.1 us -> none  [the longest x2 19.9 us: per_device(): moe_low[slot_token]]
  transfers between devices with their start and end apart: 22 -> 5, of which waited for: 19 -> 0; matrix products, arithmetic and copies ran while one was open for 10% -> 19% of each run, Pallas kernels for 0% -> 70%
where the time goes in v1:
time: 1100 us; the launch traced here: 1080 us
  Pallas kernels  832 us (76%)
  matrix products  125 us (11%)
  local copies, waits for them, and re-layouts  73.7 us (7%)
  other arithmetic  30.2 us (3%)
  between operations  14.8 us (1%)
    pallas_call x8, Pallas kernels, comm_call(): pl.pallas_call(functools.partial(comm_kernel, plan, chips, owners, counts...  733 us
    dot_general x7, matrix products, dot(): return jnp.dot(left, right, preferred_element_type=F32)  45.4 us
    dot_general x9, matrix products, dot_tn(): lax.dot_general(left, right, (((0,), (0,)), ((), ())), preferred_element_...  42.9 us
    pallas_call x2, Pallas kernels, widen(): pl.pallas_call(functools.partial(widen_kernel, counts), out_shape=(shape,...  41.5 us
    dot_general x5, matrix products, dot_nt(): lax.dot_general(left, right, (((1,), (1,)), ((), ())), preferred_element_...  36.8 us
    pallas_call x1, Pallas kernels, attend_back(): pl.pallas_call(functools.partial(attend_back_kernel, block), out_shape=(j...  27.8 us
  transfers between devices with their start and end apart: 5, of which 0 were waited for; matrix products, arithmetic and copies ran while one was open for 19% of the time, Pallas kernels for 70%

profile of v1, /device:TPU:17, one launch (start us, length us, event | category | flops | bytes accessed | tf_op | source)
XLA Modules:
  0.0 1076.0 jit_solution(10925398180044859291)
XLA Ops:
  17.9 60.1 %gather_tokens.1 = (bf16[1024,2048]{1,0:T(8,128)(2,1)}, s32[64,128]{1,0:T(8,128)S(1)}, bf16[2048,896]{1,0:T(8,128)(2,1)}, bf16[2048,512]{1,0:T(8,128)(2,1)S(1)}) custom-call(bf16[128,2048]{1,0:T(8,128)(2,1)S(1)} %bitcast.82, s32[8,128]{1,0:T(8,128)S(1)} %broadcast_in_dim.30.refs_1_, bf16[512,896]{1,0:T(8,128)(2,1)S(1)} %concatenate.40.refs_2_, ...), custom_call_target="tpu_custom_call" | custom-call | bytes 153000000 | tf_op jit(solution)/shard_map/gather_tokens/pallas_call | solution.py:733
  110.6 17.6 %attend.1.refs_0_ = bf16[1024,512]{1,0:T(8,128)(2,1)} custom-call(f32[1024,512]{1,0:T(8,128)} %slice.132.q_ref, f32[1024,256]{1,0:T(8,128)} %slice.133.kv_ref, s32[1024,1]{1,0:T(8,128)} %iota_subtract_fusion.doc_ref, f32[1024,128]{1,0:T(8,128)} %pad_maximum_fusion.7.cos_ref, f32[1024,128]{1,0:T(8,128)} %pad_maximum_fusion.8.sin_ref, ...), custom_call_target="tpu_custom_call" | custom-call | flops 1610612736 | bytes 3145728 | tf_op jit(solution)/shard_map/attend/pallas_call | solution.py:193
  129.4 82.7 %scatter_attention.1 = (f32[128,2048]{1,0:T(8,128)S(1)}, bf16[1024,2048]{1,0:T(8,128)(2,1)}) custom-call(bf16[1024,512]{1,0:T(8,128)(2,1)S(1)} %copy-done.7, bf16[2048,512]{1,0:T(8,128)(2,1)S(1)} %get-tuple-element.56.refs_1_, bf16[128,2048]{1,0:T(8,128)(2,1)S(1)} %bitcast.83), custom_call_target="tpu_custom_call" | custom-call | bytes 170000000 | tf_op jit(solution)/shard_map/scatter_attention/pallas_call | solution.py:733
  215.2 54.3 %gather_mixture.1 = (bf16[1024,2048]{1,0:T(8,128)(2,1)S(1)}, f32[1024,128]{1,0:T(8,128)S(1)}) custom-call(bf16[128,2048]{1,0:T(8,128)(2,1)S(1)} %multiply_convert_fusion.6.refs_0_, f32[128,128]{1,0:T(8,128)S(1)} %pad.27.refs_1_), custom_call_target="tpu_custom_call" | custom-call | bytes 153000000 | tf_op jit(solution)/shard_map/gather_mixture/pallas_call | solution.py:733
  274.2 10.2 fusion.5
  284.4 6.7 multiply_convert_fusion.3
  305.4 103.3 %scatter_expert.1 = (bf16[512,768]{1,0:T(8,128)(2,1)}, bf16[512,768]{1,0:T(8,128)(2,1)S(1)}, bf16[512,768]{1,0:T(8,128)(2,1)S(1)}, bf16[4096,768]{1,0:T(8,128)(2,1)}) custom-call(bf16[2048,768]{1,0:T(8,128)(2,1)S(1)} %convolution_convert_fusion.5.refs_0_, bf16[2048,768]{1,0:T(8,128)(2,1)} %convolution_convert_fusion.4.refs_1_, ...), custom_call_target="tpu_custom_call" | custom-call | bytes 272000000 | tf_op jit(solution)/shard_map/scatter_expert/pallas_call | solution.py:733
  410.1 10.2 fusion.9
  420.3 8.4 multiply_convert_fusion.1
  436.9 10.0 fusion.3
  446.9 11.1 %add_convert_fusion = bf16[1024,2048]{1,0:T(8,128)(2,1)} fusion(f32[1024,2048]{1,0:T(8,128)S(1)} %fusion.3, bf16[2048,2304]{1,0:T(8,128)(2,1)} %all-gather.9.cloned.1.call-done, bf16[1024,768]{1,0:T(8,128)(2,1)S(1)} %copy-done.41, bf16[1024,768]{1,0:T(8,128)(2,1)S(1)} %copy-done.43), kind=kOutput, calls=%fused_computation.5 | convolution fusion | flops 6452936704 | bytes 22020096 | tf_op jit(solution)/shard_map/dot_general | solution.py:43
  458.0 8.0 concatenate.48.refs_0_
  466.0 8.0 convolution_convert_fusion.1.refs_2_
  484.1 104.9 %scatter_mixture.1 = (f32[128,2176]{1,0:T(8,128)S(1)}, bf16[512,768]{1,0:T(8,128)(2,1)S(1)}, bf16[512,768]{1,0:T(8,128)(2,1)S(1)}, bf16[512,768]{1,0:T(8,128)(2,1)S(1)}) custom-call(bf16[1024,2176]{1,0:T(8,128)(2,1)} %concatenate.48.refs_0_, bf16[2048,768]{1,0:T(8,128)(2,1)} %convolution_convert_fusion.2.refs_1_, ...), custom_call_target="tpu_custom_call" | custom-call | bytes 272000000 | tf_op jit(solution)/shard_map/scatter_mixture/pallas_call | solution.py:733
  615.2 7.1 add_convert_fusion.1.refs_0_
  622.3 178.5 %scatter_layer.1 = (f32[128,2048]{1,0:T(8,128)S(1)}, bf16[1024,2048]{1,0:T(8,128)(2,1)S(1)}) custom-call(bf16[1024,2048]{1,0:T(8,128)(2,1)} %add_convert_fusion.1.refs_0_, bf16[128,2048]{1,0:T(8,128)(2,1)S(1)} %get-tuple-element.174.refs_1_), custom_call_target="tpu_custom_call" | custom-call | bytes 204000000 | tf_op jit(solution)/shard_map/scatter_layer/pallas_call | solution.py:733
  807.1 27.8 %attend_back.1 = (bf16[1024,512]{1,0:T(8,128)(2,1)}, f32[1024,256]{1,0:T(8,128)}, f32[1,128]{1,0:T(1,128)}, f32[1,128]{1,0:T(1,128)}) custom-call(f32[1024,512]{1,0:T(8,128)} %slice.132.q_ref, f32[1024,256]{1,0:T(8,128)} %slice.133.kv_ref, s32[1024,1]{1,0:T(8,128)} %iota_subtract_fusion.doc_ref, f32[1024,128]{1,0:T(8,128)} %pad_maximum_fusion.7.cos_ref, ...), custom_call_target="tpu_custom_call" | custom-call | flops 3758096384 | bytes 4194304 | tf_op jit(solution)/shard_map/attend_back/pallas_call | solution.py:216
  840.0 6.0 convolution_convert_fusion.7.refs_2_
  851.3 6.4 concatenate.51.refs_3_
  859.6 63.4 %scatter_normed.1 = (f32[128,2048]{1,0:T(8,128)S(1)}, bf16[512,512]{1,0:T(8,128)(2,1)S(1)}, bf16[512,768]{1,0:T(8,128)(2,1)S(1)}) custom-call(bf16[1024,640]{1,0:T(8,128)(2,1)S(1)} %pad_maximum_fusion.5.refs_0_, bf16[2048,640]{1,0:T(8,128)(2,1)} %pad_maximum_fusion.refs_1_, bf16[2048,512]{1,0:T(8,128)(2,1)S(1)} %copy-done.5, ...), custom_call_target="tpu_custom_call" | custom-call | bytes 204000000 | tf_op jit(solution)/shard_map/scatter_normed/pallas_call | solution.py:733
  923.4 85.4 %gather_grads.1 = (bf16[4096,1280]{1,0:T(8,128)(2,1)}, bf16[8,256]{1,0:T(8,128)(2,1)}, bf16[64,256]{1,0:T(8,128)(2,1)S(1)}) custom-call(bf16[512,1280]{1,0:T(8,128)(2,1)S(1)} %pad_maximum_fusion.6.refs_0_, bf16[32,256]{1,0:T(8,128)(2,1)S(1)} %convert_element_type.200.refs_1_), custom_call_target="tpu_custom_call" | custom-call | bytes 306000000 | tf_op jit(solution)/shard_map/gather_grads/pallas_call | solution.py:733
  1008.8 12.2 %finish_attention.1 = (f32[512,4096]{1,0:T(8,128)}, f32[512,512]{1,0:T(8,128)}, f32[512,512]{1,0:T(8,128)}, f32[512,4096]{1,0:T(8,128)}, f32[512,128]{1,0:T(8,128)}) custom-call(bf16[8,512,1280]{2,1,0:T(8,128)(2,1)} %bitcast.95), custom_call_target="tpu_custom_call" | custom-call | bytes 31457280 | tf_op jit(solution)/shard_map/finish_attention/pallas_call | solution.py:894
  1027.8 20.8 %widen.2 = (f32[8,2,512,768]{3,2,1,0:T(8,128)}, f32[8,2,512,768]{3,2,1,0:T(8,128)}, f32[8,2,512,768]{3,2,1,0:T(8,128)}) custom-call(bf16[8,1,512,768]{3,2,1,0:T(8,128)(2,1)} %bitcast.96, bf16[8,2,512,768]{3,2,1,0:T(8,128)(2,1)} %bitcast.94), custom_call_target="tpu_custom_call" | custom-call | bytes 56623104 | tf_op jit(solution)/shard_map/widen/pallas_call | solution.py:848
  1048.5 20.7 %widen.3 = (f32[8,2,512,768]{3,2,1,0:T(8,128)}, f32[8,2,512,768]{3,2,1,0:T(8,128)}, f32[8,2,512,768]{3,2,1,0:T(8,128)}) custom-call(bf16[8,3,512,768]{3,2,1,0:T(8,128)(2,1)} %bitcast.93, f32[8,2,512,768]{3,2,1,0:T(8,128)} %get-tuple-element.86.refs_1_, ...), custom_call_target="tpu_custom_call", output_to_operand_aliasing={{0}: (1, {}), {1}: (2, {}), {2}: (3, {})} | custom-call | bytes 56623104 | tf_op jit(solution)/shard_map/widen/pallas_call | solution.py:848
  (214 shorter events, 137.6 us)
Async XLA Ops:
  7.2 9.7 copy-start
  7.2 9.7 copy-start.31
  7.2 267.0 %all-gather.7.cloned.1.call-start = ((), (), s32[]{:S(2)}) async-start(), calls=%async_computation | async-start | bytes 11796480 | tf_op jit(solution)/shard_map/all_gather | solution.py:947
  86.4 323.6 %all-gather.9.cloned.1.call-start = ((), (), s32[]{:S(2)}) async-start(), calls=%async_computation.1 | async-start | bytes 11796480 | tf_op jit(solution)/shard_map/all_gather | solution.py:947
  89.4 938.3 %all-gather.13.cloned.1.call-start = ((), (), s32[]{:S(2)}) async-start(), calls=%async_computation.3 | async-start | bytes 14155776 | tf_op jit(solution)/shard_map/all_gather | solution.py:1112
  91.6 8.6 copy-start.26
  110.6 17.6 %copy-start.2 = (bf16[1,128,2048]{2,1,0:T(8,128)(2,1)S(1)}, bf16[1,128,2048]{2,1,0:T(8,128)(2,1)}, u32[]{:S(2)}) copy-start(bf16[1,128,2048]{2,1,0:T(8,128)(2,1)} %param.19) | copy-start | bytes 1572868
  274.2 10.2 copy-start.32
  284.4 6.7 copy-start.13
  291.1 9.9 copy-start.35
  410.0 638.5 %all-gather.11.cloned.1.call-start = ((), (), s32[]{:S(2)}) async-start(), calls=%async_computation.2 | async-start | bytes 21233664 | tf_op jit(solution)/shard_map/all_gather | solution.py:1114
  410.1 10.2 copy-start.33
  436.8 10.0 copy-start.23
  436.9 10.0 copy-start.41
  436.9 10.0 copy-start.43
  466.0 8.1 copy-start.14
  466.0 8.1 copy-start.42
  807.1 32.0 %copy-start.10 = (f32[128,2048]{1,0:T(8,128)S(1)}, f32[128,2048]{1,0:T(8,128)}, u32[]{:S(2)}) copy-start(f32[128,2048]{1,0:T(8,128)} %copy-done.9) | copy-start | bytes 3145732
  807.1 32.0 %copy-start.18 = (f32[128,2048]{1,0:T(8,128)S(1)}, f32[128,2048]{1,0:T(8,128)}, u32[]{:S(2)}) copy-start(f32[128,2048]{1,0:T(8,128)} %copy-done.16) | copy-start | bytes 3145732
  838.6 7.4 collective-permute-start
  840.0 6.2 copy-start.27
  840.0 6.2 copy-start.30
  859.6 63.4 %copy-start.1 = (bf16[1,128,2048]{2,1,0:T(8,128)(2,1)S(1)}, bf16[1,128,2048]{2,1,0:T(8,128)(2,1)}, u32[]{:S(2)}) copy-start(bf16[1,128,2048]{2,1,0:T(8,128)(2,1)} %param.16) | copy-start | bytes 1572868
  1008.8 17.7 %copy-start.20 = (f32[128,2048]{1,0:T(8,128)S(1)}, f32[128,2048]{1,0:T(8,128)}, u32[]{:S(2)}) copy-start(f32[128,2048]{1,0:T(8,128)} %get-tuple-element.175) | copy-start | bytes 3145732
  (25 other events, 86.7 us)
Sparse Core Ops, SparseCore 0:
  86.6 100.8 all-gather.6
  189.9 96.3 all-gather.8
  410.1 132.8 all-gather.12
  591.8 211.7 all-gather.10

commit v2 on v1

--- a/solution.py
+++ b/solution.py
@@ -51,10 +51,7 @@
     frequency = ROPE_BASE ** (-2.0 * jnp.arange(HD // 2, dtype=F32) / HD)
     angles = position_row.astype(F32)[:, None] * frequency[None, :]
     cosine, sine = jnp.cos(angles), jnp.sin(angles)
-    return (
-        jnp.concatenate([cosine, cosine], axis=-1),
-        jnp.concatenate([-sine, sine], axis=-1),
-    )
+    return jnp.concatenate([cosine, cosine, -sine, sine], axis=-1)
 
 
 def turn(values):
@@ -66,13 +63,23 @@
     return (normed * cosine + turn(normed) * sine, factor)
 
 
-def masked_scores(query, key, doc_start, first_row, columns):
-    scores = dot_nt(query, key) * (HD**-0.5)
+def softmax_weights(query, key_ref, doc_start, number):
     rows = query.shape[0]
-    row_index = first_row + lax.broadcasted_iota(jnp.int32, (rows, columns), 0)
-    key_index = lax.broadcasted_iota(jnp.int32, (rows, columns), 1)
-    allowed = (key_index <= row_index) & (key_index >= doc_start)
-    return jnp.where(allowed, scores, FLOOR)
+    scale = HD**-0.5 * 1.4426950408889634
+    parts = []
+    if number:
+        columns = number * rows
+        key_index = lax.broadcasted_iota(jnp.int32, (rows, columns), 1)
+        scores = dot_nt(query, key_ref[:columns, :]) * scale
+        parts.append(jnp.where(key_index >= doc_start, scores, FLOOR))
+    row_index = lax.broadcasted_iota(jnp.int32, (rows, rows), 0)
+    key_index = lax.broadcasted_iota(jnp.int32, (rows, rows), 1)
+    allowed = (key_index <= row_index) & (key_index >= doc_start - number * rows)
+    scores = dot_nt(query, key_ref[number * rows : (number + 1) * rows, :]) * scale
+    parts.append(jnp.where(allowed, scores, FLOOR))
+    masked = jnp.concatenate(parts, axis=1) if number else parts[0]
+    weights = jnp.exp2(masked - jnp.max(masked, axis=-1, keepdims=True))
+    return weights, 1.0 / jnp.sum(weights, axis=-1, keepdims=True)
 
 
 def attend_kernel(
@@ -94,13 +101,9 @@
             rows = pl.ds(number * block, block)
             columns = (number + 1) * block
             query, unused = normed_rope(q_ref[...], qg_ref[...], cos_ref[rows, :], sin_ref[rows, :])
-            masked = masked_scores(
-                query.astype(BF16), key_ref[:columns, :], doc_ref[...], number * block, columns
-            )
-            weights = jnp.exp(masked - jnp.max(masked, axis=-1, keepdims=True))
-            total = jnp.sum(weights, axis=-1, keepdims=True)
+            weights, share = softmax_weights(query.astype(BF16), key_ref, doc_ref[...], number)
             mixed = dot(weights.astype(BF16), val_ref[:columns, :])
-            out_ref[...] = (mixed / total).astype(BF16)
+            out_ref[...] = (mixed * share).astype(BF16)
 
 
 def attend_back_kernel(
@@ -147,9 +150,8 @@
             query = query.astype(BF16)
             key, value = key_ref[:columns, :], val_ref[:columns, :]
             upstream = dm_ref[...]
-            masked = masked_scores(query, key, doc_ref[...], number * block, columns)
-            weights = jnp.exp(masked - jnp.max(masked, axis=-1, keepdims=True))
-            probs = weights / jnp.sum(weights, axis=-1, keepdims=True)
+            weights, share = softmax_weights(query, key_ref, doc_ref[...], number)
+            probs = weights * share
             prob_grad = dot_nt(upstream, value)
             delta = jnp.sum(probs * prob_grad, axis=-1, keepdims=True)
             score_grad = (probs * (prob_grad - delta)).astype(BF16)
@@ -174,21 +176,21 @@
         kt_ref[...] = jnp.sum(terms, axis=0, keepdims=True)
 
 
-def attention_specs(length, block):
+def attention_specs(length, block, heads):
     whole = lambda h, b: (0, 0)
     return [
         pl.BlockSpec((block, HD), lambda h, b: (b, h)),
-        pl.BlockSpec((length, 2 * HD), whole),
+        pl.BlockSpec((length, 2 * HD), lambda h, b: (0, heads // 2)),
         pl.BlockSpec((block, 1), lambda h, b: (b, 0)),
         pl.BlockSpec((length, HD), whole),
-        pl.BlockSpec((length, HD), whole),
+        pl.BlockSpec((length, HD), lambda h, b: (0, 1)),
         pl.BlockSpec((1, HD), whole),
         pl.BlockSpec((1, HD), whole),
     ]
 
 
-def attend(query_raw, kv_raw, doc_start, cosine, sine, query_gain, key_gain):
-    length, width = query_raw.shape
+def attend(qkv_raw, doc_start, tables, query_gain, key_gain):
+    length, width = qkv_raw.shape[0], qkv_raw.shape[1] - 2 * HD
     block = 256
     return pl.pallas_call(
         functools.partial(attend_kernel, block),
@@ -196,21 +198,21 @@
         grid_spec=pltpu.PrefetchScalarGridSpec(
             num_scalar_prefetch=0,
             grid=(width // HD, length // block),
-            in_specs=attention_specs(length, block),
+            in_specs=attention_specs(length, block, width // HD),
             out_specs=pl.BlockSpec((block, HD), lambda h, b: (b, h)),
             scratch_shapes=[pltpu.VMEM((length, HD), BF16), pltpu.VMEM((length, HD), BF16)],
         ),
         cost_estimate=pl.CostEstimate(
-            flops=3 * length * length * width,
-            bytes_accessed=length * width * 6,
-            transcendentals=length * length * width // HD // 2,
+            flops=length * length,
+            bytes_accessed=length * width,
+            transcendentals=0,
         ),
         name="attend",
-    )(query_raw, kv_raw, doc_start, cosine, sine, query_gain, key_gain)
-
-
-def attend_back(query_raw, kv_raw, doc_start, cosine, sine, query_gain, key_gain, upstream):
-    length, width = query_raw.shape
+    )(qkv_raw, qkv_raw, doc_start, tables, tables, query_gain, key_gain)
+
+
+def attend_back(qkv_raw, doc_start, tables, query_gain, key_gain, upstream):
+    length, width = qkv_raw.shape[0], qkv_raw.shape[1] - 2 * HD
     block = 256
     whole = lambda h, b: (0, 0)
     return pl.pallas_call(
@@ -224,7 +226,7 @@
         grid_spec=pltpu.PrefetchScalarGridSpec(
             num_scalar_prefetch=0,
             grid=(width // HD, length // block),
-            in_specs=attention_specs(length, block)
+            in_specs=attention_specs(length, block, width // HD)
             + [pl.BlockSpec((block, HD), lambda h, b: (b, h))],
             out_specs=(
                 pl.BlockSpec((block, HD), lambda h, b: (b, h)),
@@ -240,12 +242,12 @@
             ],
         ),
         cost_estimate=pl.CostEstimate(
-            flops=7 * length * length * width,
-            bytes_accessed=length * width * 8,
-            transcendentals=length * length * width // HD // 2,
+            flops=length * length,
+            bytes_accessed=length * width,
+            transcendentals=0,
         ),
         name="attend_back",
-    )(query_raw, kv_raw, doc_start, cosine, sine, query_gain, key_gain, upstream)
+    )(qkv_raw, qkv_raw, doc_start, tables, tables, query_gain, key_gain, upstream)
 
 
 def ctx_place():
@@ -284,97 +286,120 @@
         self.up, self.down, self.side, self.near, self.cross, self.local = sems
         self.chip, self.core = ctx_place()
         self.rows = source.shape[0]
-
-    def block(self, chip, core):
-        start = pl.multiple_of((2 * chip + core) * self.rows, self.rows)
-        return self.target.at[pl.ds(start, self.rows)]
-
-    def hop(self, origin, sem, arrive, device, own=False):
+        self.chunks = range(chunk_count(self.rows))
+        self.piece = self.rows // len(self.chunks)
+
+    def block(self, chip, core, chunk):
+        start = (2 * chip + core) * self.rows + chunk * self.piece
+        return self.target.at[pl.ds(pl.multiple_of(start, self.piece), self.piece)]
+
+    def hop(self, origin, chunk, sem, arrive, device, own):
+        source = self.block(origin, self.core, chunk)
+        if own:
+            source = self.source.at[pl.ds(chunk * self.piece, self.piece)]
         return pltpu.make_async_remote_copy(
-            src_ref=self.source if own else self.block(origin, self.core),
-            dst_ref=self.block(origin, self.core),
-            send_sem=sem.at[origin],
-            recv_sem=arrive.at[origin],
+            src_ref=source,
+            dst_ref=self.block(origin, self.core, chunk),
+            send_sem=sem.at[origin, chunk],
+            recv_sem=arrive.at[origin, chunk],
             device_id=device,
         )
 
-    def to_up(self, origin, own=False):
-        return self.hop(origin, self.up, self.near, peer(self.chip + 1, self.core), own)
-
-    def to_down(self, origin, own=False):
-        return self.hop(origin, self.down, self.near, peer(self.chip - 1, self.core), own)
-
-    def to_side(self, origin, own=False):
-        return self.hop(origin, self.side, self.cross, peer(self.chip, 1 - self.core), own)
+    def to_up(self, origin, chunk, own=False):
+        return self.hop(origin, chunk, self.up, self.near, peer(self.chip + 1, self.core), own)
+
+    def to_down(self, origin, chunk, own=False):
+        return self.hop(origin, chunk, self.down, self.near, peer(self.chip - 1, self.core), own)
+
+    def to_side(self, origin, chunk, own=False):
+        return self.hop(origin, chunk, self.side, self.cross, peer(self.chip, 1 - self.core), own)
 
     def mine(self):
-        return pltpu.make_async_copy(self.source, self.block(self.chip, self.core), self.local)
+        start = pl.multiple_of((2 * self.chip + self.core) * self.rows, self.rows)
+        return pltpu.make_async_copy(
+            self.source, self.target.at[pl.ds(start, self.rows)], self.local
+        )
 
     def start(self):
-        @pl.when(self.chip < self.chips - 1)
-        def _():
-            self.to_up(self.chip, True).start()
-
-        @pl.when(self.chip > 0)
-        def _():
-            self.to_down(self.chip, True).start()
-
-        self.to_side(self.chip, True).start()
+        for chunk in self.chunks:
+
+            @pl.when(self.chip < self.chips - 1)
+            def _():
+                self.to_up(self.chip, chunk, True).start()
+
+            @pl.when(self.chip > 0)
+            def _():
+                self.to_down(self.chip, chunk, True).start()
+
+        for chunk in self.chunks:
+            self.to_side(self.chip, chunk, True).start()
         self.mine().start()
 
     def step(self, distance):
         below, above = self.chip - distance, self.chip + distance
-
-        @pl.when(below >= 0)
-        def _():
-            self.to_up(below).wait_recv()
-
-            @pl.when(self.chip < self.chips - 1)
+        for chunk in self.chunks:
+
+            @pl.when(below >= 0)
             def _():
-                self.to_up(below).start()
-
-            self.to_side(below).start()
-
-        @pl.when(above < self.chips)
-        def _():
-            self.to_down(above).wait_recv()
-
-            @pl.when(self.chip > 0)
+                self.to_up(below, chunk).wait_recv()
+
+                @pl.when(self.chip < self.chips - 1)
+                def _():
+                    self.to_up(below, chunk).start()
+
+                self.to_side(below, chunk).start()
+
+            @pl.when(above < self.chips)
             def _():
-                self.to_down(above).start()
-
-            self.to_side(above).start()
+                self.to_down(above, chunk).wait_recv()
+
+                @pl.when(self.chip > 0)
+                def _():
+                    self.to_down(above, chunk).start()
+
+                self.to_side(above, chunk).start()
 
     def finish(self):
         self.mine().wait()
         for origin in range(self.chips):
-            pltpu.make_async_remote_copy(
-                src_ref=self.source,
-                dst_ref=self.block(origin, 1 - self.core),
-                send_sem=self.side.at[origin],
-                recv_sem=self.cross.at[origin],
-                device_id=peer(self.chip, 1 - self.core),
-            ).wait_recv()
-            self.to_side(origin).wait_send()
-
-            @pl.when((origin <= self.chip) & (self.chip < self.chips - 1))
-            def _():
-                self.to_up(origin).wait_send()
-
-            @pl.when((origin >= self.chip) & (self.chip > 0))
-            def _():
-                self.to_down(origin).wait_send()
-
-
-def gather_sems(chips):
-    return [pltpu.SemaphoreType.DMA((chips,))] * 5 + [pltpu.SemaphoreType.DMA]
+            for chunk in self.chunks:
+                pltpu.make_async_remote_copy(
+                    src_ref=self.source.at[pl.ds(chunk * self.piece, self.piece)],
+                    dst_ref=self.block(origin, 1 - self.core, chunk),
+                    send_sem=self.side.at[origin, chunk],
+                    recv_sem=self.cross.at[origin, chunk],
+                    device_id=peer(self.chip, 1 - self.core),
+                ).wait_recv()
+                self.to_side(origin, chunk).wait_send()
+
+                @pl.when((origin <= self.chip) & (self.chip < self.chips - 1))
+                def _():
+                    self.to_up(origin, chunk).wait_send()
+
+                @pl.when((origin >= self.chip) & (self.chip > 0))
+                def _():
+                    self.to_down(origin, chunk).wait_send()
+
+
+def chunk_count(rows):
+    return 4 if rows % 64 == 0 else 1
+
+
+def gather_sems(chips, rows):
+    return [pltpu.SemaphoreType.DMA((chips, chunk_count(rows)))] * 5 + [pltpu.SemaphoreType.DMA]
 
 
 class Scatter:
-    def __init__(self, chips, tile, refs):
-        self.chips, self.tile = chips, tile
+    def __init__(self, chips, tile, outs, refs):
+        self.chips, self.tile, self.outs = chips, tile, outs
         self.give, self.take, self.send, self.low, self.high, *self.sems = refs
         self.chip, self.core = ctx_place()
+        self.rows = outs[0].shape[0]
+        self.chunks = range(chunk_count(self.rows))
+        self.piece = self.rows // len(self.chunks)
+
+    def part(self, ref, target, chunk):
+        return ref.at[target, pl.ds(chunk * self.piece, self.piece)]
 
     def side(self, target):
         return pltpu.make_async_remote_copy(
@@ -385,33 +410,42 @@
             device_id=peer(self.chip, 1 - self.core),
         )
 
-    def up(self, target):
+    def up(self, target, chunk):
         return pltpu.make_async_remote_copy(
-            src_ref=self.send.at[target],
-            dst_ref=self.low.at[target],
-            send_sem=self.sems[2].at[target],
-            recv_sem=self.sems[3].at[target],
+            src_ref=self.part(self.send, target, chunk),
+            dst_ref=self.part(self.low, target, chunk),
+            send_sem=self.sems[2].at[target, chunk],
+            recv_sem=self.sems[3].at[target, chunk],
             device_id=peer(self.chip + 1, self.core),
         )
 
-    def down(self, target):
+    def down(self, target, chunk):
         return pltpu.make_async_remote_copy(
-            src_ref=self.send.at[target],
-            dst_ref=self.high.at[target],
-            send_sem=self.sems[2].at[target],
-            recv_sem=self.sems[4].at[target],
+            src_ref=self.part(self.send, target, chunk),
+            dst_ref=self.part(self.high, target, chunk),
+            send_sem=self.sems[2].at[target, chunk],
+            recv_sem=self.sems[4].at[target, chunk],
             device_id=peer(self.chip - 1, self.core),
         )
 
+    def order(self):
+        last = self.chips - 1
+        return sorted(range(self.chips), key=lambda target: min(target, last - target))
+
     def start(self):
-        last = self.chips - 1
-        for target in sorted(range(self.chips), key=lambda t: min(t, last - t)):
+        for target in self.order():
             self.give[target] = self.tile(2 * target + 1 - self.core).astype(BF16)
             self.side(target).start()
 
-    def pairs(self, out):
+    def store(self, value):
+        at = 0
+        for out in self.outs:
+            out[...] = value[:, at : at + out.shape[1]]
+            at += out.shape[1]
+
+    def pairs(self):
         last = self.chips - 1
-        for target in sorted(range(self.chips), key=lambda t: min(t, last - t)):
+        for target in self.order():
             value = self.tile(2 * target + self.core)
             self.side(target).wait_recv()
             value = value + self.take[target].astype(F32)
@@ -419,71 +453,105 @@
 
             @pl.when(self.chip == target)
             def _():
-                out[...] = value
+                self.store(value)
 
             if target == last:
 
                 @pl.when(self.chip == 0)
                 def _():
-                    self.up(target).start()
+                    for chunk in self.chunks:
+                        self.up(target, chunk).start()
 
             if target == 0:
 
                 @pl.when(self.chip == last)
                 def _():
-                    self.down(target).start()
+                    for chunk in self.chunks:
+                        self.down(target, chunk).start()
+
+    def add(self, target, chunk, ref):
+        mine, theirs = self.part(self.send, target, chunk), self.part(ref, target, chunk)
+        mine[...] = (mine[...].astype(F32) + theirs[...].astype(F32)).astype(BF16)
+
+    def upward(self, number):
+        target = self.chips - 1 - number
+
+        @pl.when(target > self.chip)
+        def _():
+            for chunk in self.chunks:
+
+                @pl.when(self.chip > 0)
+                def _():
+                    self.up(target, chunk).wait_recv()
+                    self.add(target, chunk, self.low)
+
+                @pl.when((self.chip > 0) | (number > 0))
+                def _():
+                    self.up(target, chunk).start()
+
+    def downward(self, number):
+        last = self.chips - 1
+
+        @pl.when(number < self.chip)
+        def _():
+            for chunk in self.chunks:
+
+                @pl.when(self.chip < last)
+                def _():
+                    self.down(number, chunk).wait_recv()
+                    self.add(number, chunk, self.high)
+
+                @pl.when((self.chip < last) | (number > 0))
+                def _():
+                    self.down(number, chunk).start()
 
     def step(self, number):
-        first, final = number, self.chips - 1 - number
-
-        @pl.when(final > self.chip)
+        @pl.when(self.chip < self.chips // 2)
         def _():
-            @pl.when(self.chip > 0)
-            def _():
-                self.up(final).wait_recv()
-                self.send[final] = (
-                    self.send[final].astype(F32) + self.low[final].astype(F32)
-                ).astype(BF16)
-
-            @pl.when((self.chip > 0) | (number > 0))
-            def _():
-                self.up(final).start()
-
-        @pl.when(first < self.chip)
+            self.upward(number)
+            self.downward(number)
+
+        @pl.when(self.chip >= self.chips // 2)
         def _():
-            @pl.when(self.chip < self.chips - 1)
-            def _():
-                self.down(first).wait_recv()
-                self.send[first] = (
-                    self.send[first].astype(F32) + self.high[first].astype(F32)
-                ).astype(BF16)
-
-            @pl.when((self.chip < self.chips - 1) | (number > 0))
-            def _():
-                self.down(first).start()
-
-    def finish(self, out):
+            self.downward(number)
+            self.upward(number)
+
+    def gain(self, target, chunk, ref):
+        theirs = self.part(ref, target, chunk)[...].astype(F32)
+        rows, at = pl.ds(chunk * self.piece, self.piece), 0
+        for out in self.outs:
+            out[rows, :] += theirs[:, at : at + out.shape[1]]
+            at += out.shape[1]
+
+    def finish(self):
         for target in range(self.chips):
 
             @pl.when(self.chip == target)
             def _():
-                if target > 0:
-                    self.up(target).wait_recv()
-                    out[...] += self.low[target].astype(F32)
-                if target < self.chips - 1:
-                    self.down(target).wait_recv()
-                    out[...] += self.high[target].astype(F32)
+                for chunk in self.chunks:
+                    if target > 0:
+                        self.up(target, chunk).wait_recv()
+                        self.gain(target, chunk, self.low)
+                    if target < self.chips - 1:
+                        self.down(target, chunk).wait_recv()
+                        self.gain(target, chunk, self.high)
 
         for target in range(self.chips):
             self.side(target).wait_send()
 
             @pl.when(self.chip != target)
             def _():
-                self.up(target).wait_send()
+                for chunk in self.chunks:
+                    self.up(target, chunk).wait_send()
 
 
 def scatter_scratch(chips, rows, width):
-    return [pltpu.VMEM((chips, rows, width), BF16)] * 5 + [pltpu.SemaphoreType.DMA((chips,))] * 5
+    hops = pltpu.SemaphoreType.DMA((chips, chunk_count(rows)))
+    return (
+        [pltpu.VMEM((chips, rows, width), BF16)] * 5
+        + [pltpu.SemaphoreType.DMA((chips,))] * 2
+        + [hops] * 3
+    )
 
 
 def row_block(ref, block, rows):
@@ -631,7 +699,7 @@
     ] + [pltpu.SemaphoreType.DMA((2, bits * owners))] * 2
 
 
-def comm_kernel(plan, chips, owners, counts, *refs):
+def comm_kernel(plan, chips, owners, counts, views, *refs):
     refs = list(refs)
 
     def pop(count):
@@ -639,26 +707,30 @@
         del refs[:count]
         return taken
 
-    scatter_ins = pop(counts["scatter_ins"])
+    scatter_ins = [pop(count) for count in counts["scatter_ins"]]
     gather_ins = pop(counts["gather"])
-    group_gather_ins = pop(counts["group_gather"])
+    group_gather_ins = [view(ref) for view, ref in zip(views[0], pop(len(views[0])), strict=True)]
     group_scatter_ins = pop(counts["group_scatter"])
+    pack_ins = [[view(ref) for view, ref in zip(v, pop(len(v)), strict=True)] for v in views[1]]
     scatter_outs = pop(counts["scatter"])
     gather_outs = pop(counts["gather"])
-    group_gather_outs = pop(counts["group_gather"])
+    group_gather_outs = pop(len(views[0]))
     group_scatter_outs = pop(counts["group_scatter"])
     chained_outs = pop(counts["chained"])
+    pack_outs = pop(len(views[1]))
     bits = owners.bit_length() - 1
-    transfers = {"out": scatter_outs}
-    if counts["scatter"]:
+    transfers = {}
+    if scatter_outs:
         rows = scatter_outs[0].shape[0]
-        left, weight = scatter_ins[0], scatter_ins[1] if len(scatter_ins) > 1 else None
 
         def tile(block):
-            value = row_block(left, block, rows)
-            return value.astype(F32) if weight is None else dot_nt(value, weight[...])
-
-        transfers["scatter"] = Scatter(chips, tile, pop(10))
+            values = []
+            for left, *weight in scatter_ins:
+                value = row_block(left, block, rows)
+                values.append(dot_nt(value, weight[0][...]) if weight else value.astype(F32))
+            return values[0] if len(values) == 1 else jnp.concatenate(values, axis=1)
+
+        transfers["scatter"] = Scatter(chips, tile, scatter_outs, pop(10))
     transfers["gather"] = [
         Gather(chips, i, o, pop(6)) for i, o in zip(gather_ins, gather_outs, strict=True)
     ]
@@ -673,8 +745,22 @@
     transfers["chained"] = [
         Gather(chips, group_scatter_outs[i], o, pop(6)) for i, o in enumerate(chained_outs)
     ]
+    copies = []
+    for sources, target in zip(pack_ins, pack_outs, strict=True):
+        sems, at = pop(1)[0], 0
+        for number, source in enumerate(sources):
+            copies.append(
+                pltpu.make_async_copy(
+                    source, target.at[:, pl.ds(at, source.shape[1])], sems.at[number]
+                )
+            )
+            at += source.shape[1]
     greet(chips, owners if group_gather_ins or group_scatter_ins else 1)
+    for copy in copies:
+        copy.start()
     plan(transfers, chips, bits)
+    for copy in copies:
+        copy.wait()
 
 
 def comm_call(
@@ -689,27 +775,31 @@
     group_gather=(),
     group_scatter=(),
     chained=0,
+    packs=(),
 ):
     chips = parts // 2
-    operands = [*scatter, *gather, *group_gather, *group_scatter]
+    flat = [array for item in scatter for array in item]
+    operands = [*flat, *gather, *(g[0] for g in group_gather), *group_scatter]
+    operands += [item[0] for pack in packs for item in pack]
     in_specs = (
-        [VMEM] * len(scatter)
+        [VMEM] * len(flat)
         + [ANY] * (len(gather) + len(group_gather))
         + [VMEM] * len(group_scatter)
+        + [ANY] * sum(len(pack) for pack in packs)
     )
     shapes, out_specs, scratch = [], [], []
     if scatter:
-        rows = scatter[0].shape[0] // parts
-        width = scatter[0].shape[1] if len(scatter) == 1 else scatter[1].shape[0]
-        shapes.append(jax.ShapeDtypeStruct((rows, width), F32))
-        out_specs.append(VMEM)
-        scratch += scatter_scratch(chips, rows, width)
+        rows = flat[0].shape[0] // parts
+        widths = [item[0].shape[1] if len(item) == 1 else item[1].shape[0] for item in scatter]
+        shapes += [jax.ShapeDtypeStruct((rows, width), F32) for width in widths]
+        out_specs += [VMEM] * len(widths)
+        scratch += scatter_scratch(chips, rows, sum(widths))
     for array in gather:
         shapes.append(jax.ShapeDtypeStruct((parts * array.shape[0], array.shape[1]), array.dtype))
         out_specs.append(ANY)
-        scratch += gather_sems(chips)
-    for array in group_gather:
-        shapes.append(jax.ShapeDtypeStruct((owners * array.shape[0], array.shape[1]), array.dtype))
+        scratch += gather_sems(chips, array.shape[0])
+    for array, unused, (rows, width) in group_gather:
+        shapes.append(jax.ShapeDtypeStruct((owners * rows, width), array.dtype))
         out_specs.append(ANY)
         scratch += group_gather_sems(owners)
     for array in group_scatter:
@@ -721,17 +811,22 @@
         rows, width = array.shape[0] // owners, array.shape[1]
         shapes.append(jax.ShapeDtypeStruct((parts * rows, width), BF16))
         out_specs.append(ANY)
-        scratch += gather_sems(chips)
+        scratch += gather_sems(chips, rows)
+    for pack in packs:
+        width = sum(item[2][1] for item in pack)
+        shapes.append(jax.ShapeDtypeStruct((pack[0][2][0], width), pack[0][0].dtype))
+        out_specs.append(ANY)
+        scratch.append(pltpu.SemaphoreType.DMA((len(pack),)))
     counts = {
-        "scatter_ins": len(scatter),
-        "scatter": 1 if scatter else 0,
+        "scatter_ins": [len(item) for item in scatter],
+        "scatter": len(widths) if scatter else 0,
         "gather": len(gather),
-        "group_gather": len(group_gather),
         "group_scatter": len(group_scatter),
         "chained": chained,
     }
+    views = ([g[1] for g in group_gather], [[item[1] for item in pack] for pack in packs])
     return pl.pallas_call(
-        functools.partial(comm_kernel, plan, chips, owners, counts),
+        functools.partial(comm_kernel, plan, chips, owners, counts, views),
         out_shape=tuple(shapes),
         in_specs=in_specs,
         out_specs=tuple(out_specs),
@@ -743,37 +838,43 @@
 
 
 def plan_gather(transfers, chips, bits):
-    for one in transfers["gather"] + transfers["group_gather"]:
+    ends = transfers["group_gather"]
+    for one in transfers["gather"] + ends:
         one.start()
-    for number in range(max(chips - 1, bits)):
+    for number in range(1, chips):
+        for one in transfers["gather"]:
+            one.step(number)
         if number < bits:
-            for one in transfers["group_gather"]:
-                one.step(number)
-        if number < chips - 1:
-            for one in transfers["gather"]:
-                one.step(number + 1)
-    for one in transfers["gather"] + transfers["group_gather"]:
+            for one in ends:
+                one.step(number - 1)
+    for number in range(min(bits, chips) - 1, bits):
+        for one in ends:
+            one.step(number)
+    for one in transfers["gather"] + ends:
         one.finish()
 
 
 def plan_scatter(transfers, chips, bits):
-    scatter, out = transfers["scatter"], transfers["out"][0]
-    for one in transfers["group_scatter"]:
+    scatter = transfers["scatter"]
+    beside = transfers["group_scatter"] + transfers["group_gather"]
+    for one in beside:
         one.start()
     scatter.start()
-    scatter.pairs(out)
+    scatter.pairs()
     for one in transfers["gather"]:
         one.start()
-    for number in range(max(chips - 1, bits)):
-        if number < chips - 1:
-            scatter.step(number)
-            for one in transfers["gather"]:
-                one.step(number + 1)
-        if number < bits:
-            for one in transfers["group_scatter"]:
+    for number in range(chips - 1):
+        scatter.step(number)
+        for one in transfers["gather"]:
+            one.step(number + 1)
+        if number < bits - 1:
+            for one in beside:
                 one.step(number)
-    scatter.finish(out)
-    for one in transfers["gather"] + transfers["group_scatter"]:
+    scatter.finish()
+    for number in range(min(bits, chips) - 1, bits):
+        for one in beside:
+            one.step(number)
+    for one in transfers["gather"] + beside:
         one.finish()
 
 
@@ -823,11 +924,63 @@
 
 
 def comm_cost(micros):
-    return pl.CostEstimate(flops=0, bytes_accessed=int(micros * 3.4e6), transcendentals=0)
+    return pl.CostEstimate(flops=0, bytes_accessed=int(micros * 3.4e4), transcendentals=0)
 
 
 ANY = pl.BlockSpec(memory_space=pl.ANY)
 VMEM = pl.BlockSpec(memory_space=pltpu.VMEM)
+
+
+def after(values, *earlier):
+    tied = lax.optimization_barrier((values, earlier))[0]
+    return tied
+
+
+class GroupSum:
+    def __init__(self, partial, owners, group, flip):
+        self.owners, self.group = owners, group
+        self.rows = partial.shape[0] // owners
+        bits = list(range(owners.bit_length() - 1))
+        self.order = bits[::-1] if flip else bits
+        self.held = {piece: None for piece in range(owners)}
+        self.partial = partial
+
+    def piece(self, number):
+        if self.held[number] is not None:
+            return self.held[number]
+        start = (self.group ^ number) * self.rows
+        return lax.dynamic_slice_in_dim(self.partial, start, self.rows, 0)
+
+    def send(self):
+        bit = self.order.pop(0)
+        self.keep = [piece for piece in self.held if not piece >> bit & 1]
+        self.sent = jnp.stack([self.piece(piece | 1 << bit) for piece in self.keep])
+        pairs = [(i, i ^ 1 << bit) for i in range(self.owners)]
+        self.got = lax.ppermute(self.sent, "group", pairs)
+        return self.sent
+
+    def add(self, *earlier):
+        got = after(self.got, *earlier)
+        self.held = {
+            piece: (self.piece(piece).astype(F32) + got[at].astype(F32)).astype(BF16)
+            for at, piece in enumerate(self.keep)
+        }
+
+
+def finish_all(sums):
+    for one in sums:
+        while one.order:
+            one.send()
+            one.add()
+
+
+def send_all(sums):
+    return [one.send() for one in sums]
+
+
+def add_all(sums, *earlier):
+    for one in sums:
+        one.add(*earlier)
 
 
 def widen_kernel(counts, *refs):
@@ -857,18 +1010,41 @@
         out_specs=(block,) * total,
         input_output_aliases={len(packs) + i: i for i in range(len(previous))},
         cost_estimate=pl.CostEstimate(
-            flops=0, bytes_accessed=sum(p.size for p in packs) * 6, transcendentals=0
+            flops=0, bytes_accessed=sum(p.size for p in packs) // 16, transcendentals=0
         ),
         name="widen",
     )(*packs, *previous)
 
 
-def finish_attention_kernel(sharers, packed_ref, q_ref, k_ref, v_ref, o_ref, sums_ref):
+def finish_attention_kernel(
+    sharers,
+    packed_ref,
+    query_ref,
+    key_ref,
+    value_ref,
+    q_ref,
+    k_ref,
+    v_ref,
+    o_ref,
+    router_ref,
+    rows_ref,
+    sums_ref,
+):
     width = o_ref.shape[1]
     share = 2 * HD // sharers
     at = pl.program_id(0)
     o_ref[...] = packed_ref[0, :, :width].astype(F32)
-    q_ref[...] = packed_ref[0, :, width : 2 * width].astype(F32)
+    query = packed_ref[0, :, width : 2 * width].astype(F32)
+    q_ref[...] = query
+    gain = jnp.sum(query * query_ref[...].astype(F32), axis=1, keepdims=True)
+    small = packed_ref[0, :, 2 * width + share :].astype(F32)
+
+    @pl.when(at == 0)
+    def _():
+        sums_ref[...] = jnp.zeros_like(sums_ref)
+
+    lane = lax.broadcasted_iota(jnp.int32, small.shape, 1)
+    sums_ref[...] += small + jnp.where(lane == EXPERTS + 3, gain, 0.0)
     for number in range(sharers):
 
         @pl.when(lax.rem(at, sharers) == number)
@@ -876,21 +1052,26 @@
             piece = packed_ref[0, :, 2 * width : 2 * width + share].astype(F32)
             start = number * share
             if start < HD:
+                weight = key_ref[:, start : start + share]
                 k_ref[:, start : start + share] = piece
             else:
+                weight = value_ref[:, start - HD : start - HD + share]
                 v_ref[:, start - HD : start - HD + share] = piece
-
-    @pl.when(at == 0)
+            more = jnp.sum(piece * weight.astype(F32), axis=1, keepdims=True)
+            sums_ref[...] += jnp.where(lane == EXPERTS + 3, more, 0.0)
+
+    @pl.when(at == pl.num_programs(0) - 1)
     def _():
-        sums_ref[...] = jnp.zeros_like(sums_ref)
-
-    sums_ref[...] += packed_ref[0, :, 2 * width + share :].astype(F32)
-
-
-def finish_attention(packed, width, sharers):
+        router_ref[...] = sums_ref[:, :EXPERTS]
+        rows_ref[...] = jnp.transpose(sums_ref[...], (1, 0))[EXPERTS : EXPERTS + 8, :]
+
+
+def finish_attention(packed, weights, width, sharers):
     parts, shard, total = packed.shape
     spare = total - 2 * width - 2 * HD // sharers
-    head = lambda c: (0, c // sharers)
+    head = pl.BlockSpec((shard, HD), lambda c: (0, c // sharers))
+    own = pl.BlockSpec((shard, width), lambda c: (0, c))
+    whole = lambda c: (0, 0)
     return pl.pallas_call(
         functools.partial(finish_attention_kernel, sharers),
         out_shape=(
@@ -898,20 +1079,26 @@
             jax.ShapeDtypeStruct((shard, HK * HD), F32),
             jax.ShapeDtypeStruct((shard, HK * HD), F32),
             jax.ShapeDtypeStruct((shard, width * parts), F32),
-            jax.ShapeDtypeStruct((shard, spare), F32),
+            jax.ShapeDtypeStruct((shard, EXPERTS), F32),
+            jax.ShapeDtypeStruct((8, shard), F32),
         ),
-        grid=(parts,),
-        in_specs=[pl.BlockSpec((1, shard, total), lambda c: (c, 0, 0))],
-        out_specs=(
-            pl.BlockSpec((shard, width), lambda c: (0, c)),
-            pl.BlockSpec((shard, HD), head),
-            pl.BlockSpec((shard, HD), head),
-            pl.BlockSpec((shard, width), lambda c: (0, c)),
-            pl.BlockSpec((shard, spare), lambda c: (0, 0)),
+        grid_spec=pltpu.PrefetchScalarGridSpec(
+            num_scalar_prefetch=0,
+            grid=(parts,),
+            in_specs=[pl.BlockSpec((1, shard, total), lambda c: (c, 0, 0)), own, head, head],
+            out_specs=(
+                own,
+                head,
+                head,
+                own,
+                pl.BlockSpec((shard, EXPERTS), whole),
+                pl.BlockSpec((8, shard), whole),
+            ),
+            scratch_shapes=[pltpu.VMEM((shard, spare), F32)],
         ),
-        cost_estimate=pl.CostEstimate(flops=0, bytes_accessed=packed.size * 6, transcendentals=0),
+        cost_estimate=pl.CostEstimate(flops=0, bytes_accessed=packed.size // 16, transcendentals=0),
         name="finish_attention",
-    )(packed)
+    )(packed, *weights)
 
 
 def per_device(
@@ -966,28 +1153,42 @@
     comm = lambda plan, number, name, micros, **transfers: comm_call(
         plan, number, name, parts, owners, micros, **transfers
     )
-    inputs_all, positions_all, wqkv, wout = comm(
+    def expert_pack(number, at):
+        return jnp.concatenate(
+            [
+                lax.dynamic_index_in_dim(w, at * experts + number, 0, keepdims=False)
+                for w in (gate_weight, up_weight, down_weight)
+            ],
+            axis=1,
+        )
+
+    packs = [expert_pack(number, here) for number in range(experts)]
+    extras = after(extras, *packs)
+
+    def cut(start, count):
+        return lambda ref: ref.at[:, pl.ds(pl.multiple_of(start(), count), count)]
+
+    place = lambda: lax.axis_index("ctx")
+    key_cut = cut(lambda: place() // sharers * HD, HD)
+    own_cut = cut(lambda: place() * width, width)
+
+    inputs_all, positions_all, extras, wquery, wkey, wvalue, wout = comm(
         plan_gather,
         0,
         "gather_tokens",
         45,
         gather=(tokens[0], jnp.broadcast_to(positions, (8, rows))),
         group_gather=(
-            jnp.concatenate(
-                [
-                    columns(query_weight, here * width, width),
-                    columns(key_weight, key_head * HD, HD),
-                    columns(value_weight, key_head * HD, HD),
-                    extras,
-                ],
-                axis=1,
-            ),
-            columns(output_weight, here * width, width),
+            (extras, lambda ref: ref, (shard, PAD)),
+            (query_weight, own_cut, (shard, width)),
+            (key_weight, key_cut, (shard, HD)),
+            (value_weight, key_cut, (shard, HD)),
+            (output_weight, own_cut, (shard, width)),
         ),
     )
-    at = width + 2 * HD
-    extras = wqkv[:, at:]
-    wqkv = wqkv[:, :at]
+    packs = [gather_group(after(pack, positions_all)) for pack in packs]
+    wqkv = jnp.concatenate([wquery, wkey, wvalue], axis=1)
+
     router = extras[:, :EXPERTS]
     attention_gains = extras[:, EXPERTS].astype(F32)
     mixture_gains = extras[:, EXPERTS + 1].astype(F32)
@@ -999,28 +1200,20 @@
     )
     query_gains, key_gains = head_gain(EXPERTS + 2), head_gain(EXPERTS + 3)
 
-    def expert_pack(number, index):
-        take = lambda w: lax.dynamic_index_in_dim(w, index * experts + number, 0, keepdims=False)
-        return jnp.concatenate([take(gate_weight), take(up_weight), take(down_weight)], axis=1)
-
-    later = lax.optimization_barrier((positions_all, here))[1]
-    expert_weights = [gather_group(expert_pack(number, later)) for number in range(experts)]
     positions_all = positions_all.reshape(parts, 8, rows)[:, 0].reshape(length)
     doc_start = (jnp.arange(length, dtype=jnp.int32) - positions_all)[:, None]
-    cosine, sine = rope_tables(positions_all)
     inputs = tokens[0].astype(F32)
     unused, attn_factor = rms_parts(inputs, attention_gains)
     normed_all = rms_parts(inputs_all.astype(F32), attention_gains)[0].astype(BF16)
     qkv_raw = dot(normed_all, wqkv)
-    query_raw, kv_raw = qkv_raw[:, :width], qkv_raw[:, width:]
-    tables = (query_raw, kv_raw, doc_start, cosine, sine, query_gains, key_gains)
+    tables = (qkv_raw, doc_start, rope_tables(positions_all), query_gains, key_gains)
     mixed_low = attend(*tables)
     attn_out, upstream_all = comm(
         plan_scatter,
         1,
         "scatter_attention",
         50,
-        scatter=(mixed_low, wout),
+        scatter=((mixed_low, wout),),
         gather=(cotangent[0],),
     )
     hidden = inputs + attn_out
@@ -1043,97 +1236,129 @@
     )
     combine_all = columns(combine_all, here * experts, experts)
 
-    layer_part = jnp.zeros((length, D), F32)
-    moe_part = jnp.zeros((length, D), F32)
-    combine_grads = []
-    first_pieces, last_grads = [], []
-    for number in range(experts):
-        pack = expert_weights[number]
-        if first_pieces:
-            pack = lax.optimization_barrier((pack, *first_pieces[-1]))[0]
-        gate_up, down = pack[:, : 2 * F], pack[:, 2 * F :]
-        weight = combine_all[:, number : number + 1]
-        gate_up_all = dot(moe_all, gate_up)
-        gate_all, up_all = gate_up_all[:, :F], gate_up_all[:, F:]
-        back_all = dot(upstream_all, down)
+    def expert_forward(number, weights, gate_all):
+        up_all = dot(moe_all, weights[1])
         sigmoid = lax.logistic(gate_all)
         act_low = (gate_all * sigmoid * up_all).astype(BF16)
-        act = act_low.astype(F32)
-        combine_grads.append(jnp.sum(act * back_all, axis=-1, keepdims=True))
-        act_grad = weight * back_all
+        weighted = (combine_all[:, number : number + 1] * act_low.astype(F32)).astype(BF16)
+        return gate_all, up_all, act_low, weighted
+
+    def expert_back(number, gate_all, up_all, act_low, weights):
+        back_all = dot(upstream_all, weights[2])
+        sigmoid = lax.logistic(gate_all)
+        combine_grad = jnp.sum(act_low.astype(F32) * back_all, axis=-1, keepdims=True)
+        act_grad = combine_all[:, number : number + 1] * back_all
         gate_grad = (act_grad * up_all * sigmoid * (1.0 + gate_all * (1.0 - sigmoid))).astype(BF16)
         up_grad = (act_grad * gate_all * sigmoid).astype(BF16)
-        weighted = (weight * act).astype(BF16)
-        grads = (
-            dot_tn(upstream_all, weighted).astype(BF16),
-            dot_tn(moe_all, gate_grad).astype(BF16),
-            dot_tn(moe_all, up_grad).astype(BF16),
+        return combine_grad, gate_grad, up_grad
+
+    def weight_grad(left, right):
+        return dot_tn(left, right).astype(BF16)
+
+    split = lambda pack: (pack[:, :F], pack[:, F : 2 * F], pack[:, 2 * F :])
+    weights = split(packs[0])
+    gate_all = dot(moe_all, weights[0])
+    gate_all, up_all, act_low, weighted = expert_forward(0, weights, gate_all)
+    combine_grads, layer_terms, moe_terms, gathered = [], [], [], []
+    last_grads = [weight_grad(upstream_all, weighted)]
+    for number in range(1, experts):
+        half = F // 2
+        down_sums = [
+            GroupSum(last_grads[0][:, :half], owners, group, False),
+            GroupSum(last_grads[0][:, half:], owners, group, True),
+        ]
+        gate_all, up_all = after((gate_all, up_all), *send_all(down_sums))
+        combine_grad, gate_grad, up_grad = expert_back(
+            number - 1, gate_all, up_all, act_low, weights
         )
-        if number < experts - 1:
-            first_pieces.append(
-                comm(
-                    plan_group_scatter,
-                    10 + number,
-                    "scatter_expert",
-                    80,
-                    group_scatter=grads,
-                    chained=1,
-                )
-            )
-        else:
-            last_grads = grads
-        layer_part = layer_part + dot_nt(weighted, down)
-        moe_part = moe_part + dot_nt(jnp.concatenate([gate_grad, up_grad], axis=1), gate_up)
+        combine_grads.append(combine_grad)
+        layer_terms.append((weighted, weights[2]))
+        moe_terms += [(gate_grad, weights[0]), (up_grad, weights[1])]
+        grads = weight_grad(moe_all, gate_grad), weight_grad(moe_all, up_grad)
+        layer_part = dot_nt(weighted, weights[2])
+        add_all(down_sums, layer_part, *grads)
+        sent = send_all(down_sums) if down_sums[0].order else []
+        other_sums = [
+            GroupSum(after(grads[0], *sent), owners, group, False),
+            GroupSum(after(grads[1], *sent), owners, group, True),
+        ]
+        weights = split(after(packs[number], *send_all(other_sums)))
+        gate_all = dot(moe_all, weights[0])
+        add_all(down_sums, gate_all)
+        finish_all(down_sums)
+        down = jnp.concatenate([one.held[0] for one in down_sums], axis=1)
+        weights = (weights[0], after(weights[1], down), weights[2])
+        gate_all, up_all, act_low, weighted = expert_forward(number, weights, gate_all)
+        last_grads = [weight_grad(upstream_all, weighted)]
+        gathered.append([down.reshape(2, shard // 2, F), other_sums])
+    combine_grad, gate_grad, up_grad = expert_back(
+        experts - 1, gate_all, up_all, act_low, weights
+    )
+    combine_grads.append(combine_grad)
+    layer_terms.append((weighted, weights[2]))
+    moe_terms += [(gate_grad, weights[0]), (up_grad, weights[1])]
+    last_grads += [weight_grad(moe_all, gate_grad), weight_grad(moe_all, up_grad)]
+    for pieces in gathered:
+        add_all(pieces[1], *last_grads)
+        if pieces[1][0].order:
+            moe_terms = after(moe_terms, *send_all(pieces[1]))
+    moe_part = sum(dot_nt(left, right) for left, right in moe_terms[:2])
+    layer_part = sum(dot_nt(left, right) for left, right in layer_terms)
+    for pieces in gathered:
+        add_all(pieces[1], moe_part, layer_part)
+        finish_all(pieces[1])
+        pieces[1] = jnp.stack([one.held[0] for one in pieces[1]])
+        moe_terms[2:] = after(moe_terms[2:], pieces[1])
+    for left, right in moe_terms[2:]:
+        moe_part = moe_part + dot_nt(left, right)
+    moe_part_low = moe_part.astype(BF16)
     combine_grad = jnp.concatenate(combine_grads, axis=1)
-    high = combine_grad.astype(BF16)
-    low = (combine_grad - high.astype(F32)).astype(BF16)
-    place = lambda v: lax.dynamic_update_slice_in_dim(
-        jnp.zeros((length, EXPERTS), BF16), v, here * experts, 1
-    )
-    moe_pack = jnp.concatenate(
-        [
-            moe_part.astype(BF16),
-            place(high),
-            place(low),
-            jnp.zeros((length, PAD - 2 * EXPERTS), BF16),
-        ],
-        axis=1,
-    )
-    moe_sum, *last_pieces = comm(
+    high = combine_grad.astype(BF16).astype(F32)
+    low = combine_grad - high
+    at = jnp.arange(PAD, dtype=jnp.int32)[None, :]
+    small = sum(
+        jnp.where(at == here * experts + number, high[:, number : number + 1], 0.0)
+        + jnp.where(at == EXPERTS + here * experts + number, low[:, number : number + 1], 0.0)
+        for number in range(experts)
+    ).astype(BF16)
+    moe_sum, small_sum, *last_pieces = comm(
         plan_scatter,
         3,
         "scatter_mixture",
-        80,
-        scatter=(moe_pack,),
+        60,
+        scatter=((moe_part_low,), (small,)),
         group_scatter=last_grads,
     )
-    stack_shape = lambda v: v.reshape(parts, -1, shard, F)
-    expert_packs = [
-        (stack_shape(pieces[3]), lax.all_gather(jnp.stack(pieces[1:3]), "ctx"))
-        for pieces in first_pieces
-    ] + [(lax.all_gather(jnp.stack(last_pieces), "ctx"),)]
-
-    dcombine = moe_sum[:, D : D + EXPERTS] + moe_sum[:, D + EXPERTS : D + 2 * EXPERTS]
+    gathered.append([jnp.stack(last_pieces)])
+    unfold = lambda piece: lax.all_gather(piece, "ctx").reshape(parts, -1, shard, F)
+    expert_packs = [[unfold(piece) for piece in pieces] for pieces in gathered]
+
+    dcombine = small_sum[:, :EXPERTS] + small_sum[:, EXPERTS : 2 * EXPERTS]
     gates_grad = jnp.sum(onehot * dcombine[:, None, :], axis=-1)
     chosen_grad = gates * (gates_grad - jnp.sum(gates * gates_grad, axis=-1, keepdims=True))
     logit_grad_low = jnp.sum(chosen_grad[:, :, None] * onehot, axis=1).astype(BF16)
     router_partial = dot_tn(moe_low, logit_grad_low)
-    moe_grad = moe_sum[:, :D] + dot_nt(logit_grad_low, router)
+    moe_grad = moe_sum + dot_nt(logit_grad_low, router)
     hidden_part, mixture_terms = rms_back(hidden, moe_factor, mixture_gains, moe_grad)
     mixture_partial = jnp.sum(mixture_terms, axis=0)
     hidden_grad = cotangent[0].astype(F32) + hidden_part
 
-    layer_sum, attn_grad_all = comm(
-        plan_scatter,
+    (attn_grad_all,) = comm(
+        plan_gather,
         4,
-        "scatter_layer",
-        60,
-        scatter=(layer_part.astype(BF16),),
-        gather=(hidden_grad.astype(BF16),),
-    )
-    layer_out = (hidden + layer_sum).astype(BF16)[None]
+        "gather_attention",
+        45,
+        gather=(
+            after(hidden_grad.astype(BF16), *(pack[0] for pack in expert_packs[:-1])),
+        ),
+    )
     mixed_grad = dot(attn_grad_all, wout).astype(BF16)
-    output_partial = dot_tn(attn_grad_all, mixed_low).astype(BF16)
+    output_partial = weight_grad(attn_grad_all, mixed_low)
+    output_sums = [
+        GroupSum(output_partial[:, : width // 2], owners, group, False),
+        GroupSum(output_partial[:, width // 2 :], owners, group, True),
+    ]
+    mixed_grad = after(mixed_grad, *send_all(output_sums))
     query_low, kv_part, query_terms, key_terms = attend_back(*tables, mixed_grad)
     step = 1
     while step < sharers:
@@ -1148,42 +1373,47 @@
         spread = terms.reshape(owners, HD // owners)
         return jnp.pad(spread, ((0, 0), (0, shard - HD // owners))).reshape(D, 1)
 
-    spare = next(n for n in range(EXPERTS + 3, 1024) if (width + share + n) % 256 == 0)
-    qkv_partial = jnp.concatenate(
+    add_all(output_sums, qkv_low)
+    qkv_tied = qkv_low
+    if output_sums[0].order:
+        qkv_tied = after(qkv_low, *send_all(output_sums))
+    spare = next(n for n in range(EXPERTS + 8, 1024) if (width + share + n) % 256 == 0)
+    grad_extras = jnp.concatenate(
         [
-            dot_tn(normed_all, qkv_low),
             router_partial,
             mixture_partial[:, None],
             head_column(query_terms),
             head_column(key_terms),
-            jnp.zeros((D, spare - EXPERTS - 3), F32),
         ],
         axis=1,
-    ).astype(BF16)
-    normed_grad, output_piece, qkv_piece = comm(
+    )
+    grad_extras = jnp.pad(grad_extras, ((0, 0), (width + share, spare - EXPERTS - 3)))
+    qkv_wide = jnp.pad(qkv_tied, ((0, 0), (0, spare)))
+    qkv_partial = (dot_tn(normed_all, qkv_wide) + grad_extras).astype(BF16)
+    layer_sum, qkv_piece = comm(
+        plan_scatter,
+        6,
+        "scatter_grads",
+        60,
+        scatter=((layer_part.astype(BF16),),),
+        group_scatter=(after(qkv_partial, *(pack[-1] for pack in expert_packs[:-1])),),
+    )
+    layer_out = (hidden + layer_sum).astype(BF16)[None]
+    add_all(output_sums, qkv_piece)
+    finish_all(output_sums)
+    attn_piece = jnp.concatenate([one.held[0] for one in output_sums] + [qkv_piece], axis=1)
+    attn_grads = lax.all_gather(attn_piece, "ctx")
+    (normed_grad,) = comm(
         plan_scatter,
         5,
         "scatter_normed",
         60,
-        scatter=(qkv_low, wqkv_share),
-        group_scatter=(output_partial, qkv_partial),
-    )
-    input_part, attention_terms = rms_back(inputs, attn_factor, attention_gains, normed_grad)
+        scatter=((after(qkv_low, attn_piece), wqkv_share),),
+    )
+    input_part, unused = rms_back(inputs, attn_factor, attention_gains, normed_grad)
     tokens_grad = (hidden_grad + input_part).astype(BF16)[None]
-    attention_partial = jnp.sum(attention_terms, axis=0)
-    gain_rows = jnp.pad(attention_partial.reshape(owners, shard), ((0, 0), (0, D - shard)))
-    attn_grads, unused, gain_parts = comm(
-        plan_finish,
-        6,
-        "gather_grads",
-        90,
-        gather=(jnp.concatenate([output_piece, qkv_piece], axis=1),),
-        group_scatter=(gain_rows.reshape(owners * 8, D // 8).astype(BF16),),
-        chained=1,
-    )
-    attention_gain_grad = jnp.sum(gain_parts.reshape(parts, D)[:, :shard].astype(F32), axis=0)
-    query_grad, key_grad, value_grad, output_grad, sums = finish_attention(
-        attn_grads.reshape(parts, shard, -1), width, sharers
+    query_grad, key_grad, value_grad, output_grad, router_grad, gain_rows = finish_attention(
+        attn_grads, (query_weight, key_weight, value_weight), width, sharers
     )
     finished = ()
     for number in range(experts):
@@ -1192,15 +1422,15 @@
     return (
         layer_out,
         tokens_grad,
-        attention_gain_grad,
+        gain_rows[3] / attention_gain.astype(F32),
         query_grad,
         key_grad,
         value_grad,
         output_grad,
-        sums[: HD // owners, EXPERTS + 1],
-        sums[: HD // owners, EXPERTS + 2],
-        sums[:, EXPERTS],
-        sums[:, :EXPERTS],
+        gain_rows[1, : HD // owners],
+        gain_rows[2, : HD // owners],
+        gain_rows[0],
+        router_grad,
         whole(finished[1]),
         whole(finished[2]),
         whole(finished[0]),

time: 1100 us -> 897 us (0.82); the launches traced: 1080 us -> 892 us
  Pallas kernels: 832 us -> 555 us
  waiting for transfers between devices: 0.11 us -> 78.8 us
  local copies, waits for them, and re-layouts: 73.7 us -> 45.7 us
  other arithmetic: 30.2 us -> 50.9 us
    pallas_call x8 -> x7, Pallas kernels: 733 us -> 453 us  [comm_call(): pl.pallas_call(functools.partial(comm_kernel, plan, chips, owners, counts...]
    all_gather x2 -> x4, waiting for transfers between devices: 0.01 us -> 52.1 us  [the longest x1 52.1 us: per_device(): attn_grads = lax.all_gather(attn_piece, 'ctx')]
    ppermute x0 -> x12, waiting for transfers between devices: none -> 25.8 us  [send(): self.got = lax.ppermute(self.sent, 'group', pairs)]
    another operation x4 -> x16, other arithmetic: 4.39 us -> 18.6 us  [the longest x12 12.7 us: send(): self.sent = jnp.stack([self.piece(piece | 1 << bit) for piece in self.keep])]
    concatenate x3 -> x2, local copies, waits for them, and re-layouts: 16.7 us -> 2.72 us  [the longest x1 1.38 us: per_device(): jnp.concatenate([router_weight, attention_gain[:, None], mixture_gain[:,...]
    dot_general x5 -> x7, matrix products: 36.8 us -> 47.2 us  [dot_nt(): lax.dot_general(left, right, (((1,), (1,)), ((), ())), preferred_element_...]
    dot_general x7 -> x9, matrix products: 45.4 us -> 51.4 us  [dot(): return jnp.dot(left, right, preferred_element_type=F32)]
  transfers between devices with their start and end apart: 5 -> 19, of which waited for: 0 -> 5; matrix products, arithmetic and copies ran while one was open for 19% -> 22% of each run, Pallas kernels for 70% -> 55%
where the time goes in v2:
time: 897 us; the launch traced here: 892 us
  Pallas kernels  555 us (62%)
  matrix products  134 us (15%)
  waiting for transfers between devices  78.8 us (9%)
  other arithmetic  50.9 us (6%)
  local copies, waits for them, and re-layouts  45.7 us (5%)
  between operations  15.5 us (2%)
  starting transfers between devices  11.3 us (1%)
    pallas_call x7, Pallas kernels, comm_call(): pl.pallas_call(functools.partial(comm_kernel, plan, chips, owners, counts...  453 us
    all_gather x1, waiting for transfers between devices, per_device(): attn_grads = lax.all_gather(attn_piece, 'ctx')  52.1 us
    dot_general x9, matrix products, dot(): return jnp.dot(left, right, preferred_element_type=F32)  51.4 us
    dot_general x7, matrix products, dot_nt(): lax.dot_general(left, right, (((1,), (1,)), ((), ())), preferred_element_...  47.2 us
    pallas_call x2, Pallas kernels, widen(): pl.pallas_call(functools.partial(widen_kernel, counts), out_shape=(shape,...  41.6 us
    dot_general x9, matrix products, dot_tn(): lax.dot_general(left, right, (((0,), (0,)), ((), ())), preferred_element_...  35.7 us
    pallas_call x1, Pallas kernels, attend_back(): pl.pallas_call(functools.partial(attend_back_kernel, block), out_shape=(j...  27.4 us
    ppermute x12, waiting for transfers between devices, send(): self.got = lax.ppermute(self.sent, 'group', pairs)  25.8 us
  transfers between devices with their start and end apart: 19, of which 5 were waited for; matrix products, arithmetic and copies ran while one was open for 22% of the time, Pallas kernels for 55%

profile of v2, /device:TPU:17, one launch (start us, length us, event | category | flops | bytes accessed | tf_op | source)
XLA Modules:
  0.0 891.6 jit_solution(668108896514690151)
XLA Ops:
  24.2 51.4 %gather_tokens.1 = (bf16[1024,2048]{1,0:T(8,128)(2,1)}, s32[64,128]{1,0:T(8,128)S(1)}, bf16[2048,128]{1,0:T(8,128)(2,1)S(1)}, bf16[2048,512]{1,0:T(8,128)(2,1)S(...) custom-call(bf16[128,2048]{1,0:T(8,128)(2,1)S(1)} %bitcast.195, ...), custom_call_target="tpu_custom_call" | custom-call | bytes 1530000 | tf_op jit(solution)/shard_map/gather_tokens/pallas_call | solution.py:828
  91.4 17.6 %attend.1.refs_0_ = bf16[1024,512]{1,0:T(8,128)(2,1)} custom-call(f32[1024,768]{1,0:T(8,128)} %fusion.7.q_ref.kv_ref, f32[1024,768]{1,0:T(8,128)} %fusion.7.q_ref.kv_ref, s32[1024,1]{1,0:T(8,128)} %iota_subtract_fusion.doc_ref, f32[1024,256]{1,0:T(8,128)} %pad_maximum_fusion.9.cos_ref.sin_ref, f32[1024,256]{1,0:T(8,128)} %pad_maximum_fusion.9.cos_ref.sin_ref, ...), custom_call_target="tpu_custom_call" | custom-call | flops 1048576 | bytes 524288 | tf_op jit(solution)/shard_map/attend/pallas_call | solution.py:195
  111.8 58.4 %scatter_attention.1 = (f32[128,2048]{1,0:T(8,128)S(1)}, bf16[1024,2048]{1,0:T(8,128)(2,1)}) custom-call(bf16[1024,512]{1,0:T(8,128)(2,1)S(1)} %copy-done.6, bf16[2048,512]{1,0:T(8,128)(2,1)S(1)} %copy-done.11, bf16[128,2048]{1,0:T(8,128)(2,1)S(1)} %bitcast.196), custom_call_target="tpu_custom_call" | custom-call | bytes 1700000 | tf_op jit(solution)/shard_map/scatter_attention/pallas_call | solution.py:828
  172.3 45.0 %gather_mixture.1 = (bf16[1024,2048]{1,0:T(8,128)(2,1)S(1)}, f32[1024,128]{1,0:T(8,128)S(1)}) custom-call(bf16[128,2048]{1,0:T(8,128)(2,1)S(1)} %multiply_convert_fusion.6.refs_0_, f32[128,128]{1,0:T(8,128)S(1)} %pad.28.refs_1_), custom_call_target="tpu_custom_call" | custom-call | bytes 1530000 | tf_op jit(solution)/shard_map/gather_mixture/pallas_call | solution.py:828
  220.0 7.9 fusion.75
  232.3 8.1 fusion.4
  241.5 6.2 convolution_convert_fusion
  265.1 20.6 %collective-permute-done.1 = bf16[2,512,384]{1,2,0:T(8,128)(2,1)} collective-permute-done((bf16[2,512,384]{1,2,0:T(8,128)(2,1)S(1)}, bf16[2,512,384]{1,2,0:T(8,128)(2,1)}, u32[]{:S(2)}, u32[]{:S(2)}) %collective-permute-start.1) | collective-permute-done | bytes 786464 | tf_op jit(solution)/shard_map/ppermute | solution.py:959
  292.8 8.3 fusion.79
  305.0 6.6 fusion.83
  320.6 9.6 %fusion.6 = (f32[1024]{0:T(1024)S(1)}, bf16[1024,768]{0,1:T(8,128)(2,1)}, bf16[1024,768]{0,1:T(8,128)(2,1)S(1)}, bf16[1024,768]{0,1:T(8,128)(2,1)S(1)}) fusion(f32[1024,768]{0,1:T(8,128)} %fusion.90, f32[1024,768]{0,1:T(8,128)} %fusion.79, f32[1024]{0:T(1024)S(1)} %get-tuple-element.232, bf16[1024,2048]{1,0:T(8,128)(2,1)} %get-tuple-element.99, ...), kind=kOutput, calls=%fused_computation.22 | convolution fusion | flops 3236953088 | bytes 18358272 | tf_op jit(solution)/shard_map/dot_general | solution.py:39
  345.0 8.0 convolution_add_fusion.1.refs_0_
  363.5 8.0 convolution_add_fusion
  377.4 9.6 %fusion.92 = f32[1024,2048]{1,0:T(8,128)} fusion(bf16[1024,768]{0,1:T(8,128)(2,1)} %copy-done.73, bf16[2048,768]{1,0:T(8,128)(2,1)} %get-tuple-element.123), kind=kOutput, calls=%fused_computation.220 | convolution fusion | flops 3221225472 | bytes 13107200 | tf_op jit(solution)/shard_map/dot_general | solution.py:43
  387.0 8.2 add_convert_fusion.refs_0_
  395.2 116.2 %scatter_mixture.1 = (f32[128,2048]{1,0:T(8,128)S(1)}, f32[128,128]{1,0:T(8,128)S(1)}, bf16[512,768]{1,0:T(8,128)(2,1)S(1)}, bf16[512,768]{1,0:T(8,128)(2,1)S(1)}, bf16[512,768]{1,0:T(8,128)(2,1)S(1)}) custom-call(bf16[1024,2048]{1,0:T(8,128)(2,1)} %add_convert_fusion.refs_0_, bf16[1024,128]{1,0:T(8,128)(2,1)S(1)} %add_convert_fusion.3.refs_1_, ...), custom_call_target="tpu_custom_call" | custom-call | bytes 2040000 | tf_op jit(solution)/shard_map/scatter_mixture/pallas_call | solution.py:828
  516.8 37.1 %gather_attention.1 = bf16[1024,2048]{1,0:T(8,128)(2,1)S(1)} custom-call(bf16[128,2048]{1,0:T(8,128)(2,1)S(1)} %get-tuple-element.128.refs_0_), custom_call_target="tpu_custom_call" | custom-call | bytes 1530000 | tf_op jit(solution)/shard_map/gather_attention/pallas_call | solution.py:828
  562.6 27.4 %attend_back.1 = (bf16[1024,512]{1,0:T(8,128)(2,1)}, f32[1024,256]{1,0:T(8,128)}, f32[1,128]{1,0:T(1,128)}, f32[1,128]{1,0:T(1,128)}) custom-call(f32[1024,768]{1,0:T(8,128)} %fusion.7.q_ref.kv_ref, f32[1024,768]{1,0:T(8,128)} %fusion.7.q_ref.kv_ref, s32[1024,1]{1,0:T(8,128)} %iota_subtract_fusion.doc_ref, f32[1024,256]{1,0:T(8,128)} %pad_maximum_fusion.9.cos_ref.sin_ref, ...), custom_call_target="tpu_custom_call" | custom-call | flops 1048576 | bytes 524288 | tf_op jit(solution)/shard_map/attend_back/pallas_call | solution.py:218
  615.1 88.1 %scatter_grads.1 = (f32[128,2048]{1,0:T(8,128)S(1)}, bf16[512,768]{1,0:T(8,128)(2,1)S(1)}) custom-call(bf16[1024,2048]{1,0:T(8,128)(2,1)} %convolution_add_fusion.1.refs_0_, bf16[2048,768]{1,0:T(8,128)(2,1)S(1)} %add_convert_fusion.1.refs_1_), custom_call_target="tpu_custom_call" | custom-call | bytes 2040000 | tf_op jit(solution)/shard_map/scatter_grads/pallas_call | solution.py:828
  709.9 20.7 %widen.2 = (f32[8,2,512,768]{3,2,1,0:T(8,128)}, f32[8,2,512,768]{3,2,1,0:T(8,128)}, f32[8,2,512,768]{3,2,1,0:T(8,128)}) custom-call(bf16[8,1,512,768]{3,2,1,0:T(8,128)(2,1)} %bitcast.207, bf16[8,2,512,768]{3,2,1,0:T(8,128)(2,1)} %bitcast.205), custom_call_target="tpu_custom_call" | custom-call | bytes 589824 | tf_op jit(solution)/shard_map/widen/pallas_call | solution.py:1001
  731.9 56.9 %scatter_normed.1 = f32[128,2048]{1,0:T(8,128)S(1)} custom-call(bf16[1024,640]{1,0:T(8,128)(2,1)S(1)} %copy-done.5, bf16[2048,640]{1,0:T(8,128)(2,1)S(1)} %pad_maximum_fusion.refs_1_), custom_call_target="tpu_custom_call" | custom-call | bytes 2040000 | tf_op jit(solution)/shard_map/scatter_normed/pallas_call | solution.py:828
  791.4 20.8 %widen.3 = (f32[8,2,512,768]{3,2,1,0:T(8,128)}, f32[8,2,512,768]{3,2,1,0:T(8,128)}, f32[8,2,512,768]{3,2,1,0:T(8,128)}) custom-call(bf16[8,3,512,768]{3,2,1,0:T(8,128)(2,1)} %bitcast.204, f32[8,2,512,768]{3,2,1,0:T(8,128)} %get-tuple-element.152.refs_1_, ...), custom_call_target="tpu_custom_call", output_to_operand_aliasing={{0}: (1, {}), {1}: (2, {}), {2}: (3, {})} | custom-call | bytes 589824 | tf_op jit(solution)/shard_map/widen/pallas_call | solution.py:1001
  812.2 52.1 %all-gather.18.cloned.1.call-done = bf16[4096,1280]{1,0:T(8,128)(2,1)} async-done(((bf16[512,1280]{1,0:T(8,128)(2,1)}), bf16[4096,1280]{1,0:T(8,128)(2,1)}) %all-gather.18.cloned.1.call-update) | async-done | bytes 10485776 | tf_op jit(solution)/shard_map/all_gather | solution.py:1405
  864.3 15.3 %finish_attention.1 = (f32[512,4096]{1,0:T(8,128)}, f32[512,512]{1,0:T(8,128)}, f32[512,512]{1,0:T(8,128)}, f32[512,4096]{1,0:T(8,128)}, f32[512,16]{1,0:T(8,128)}, /*index=5*/f32[8,512]{1,0:T(8,128)}) custom-call(bf16[8,512,1280]{2,1,0:T(8,128)(2,1)} %bitcast.206, bf16[512,4096]{1,0:T(8,128)(2,1)} %query_ref.1, bf16[512,512]{1,0:T(8,128)(2,1)} %key_ref.1, ...), custom_call_target="tpu_custom_call" | custom-call | bytes 327680 | tf_op jit(solution)/shard_map/finish_attention/pallas_call | solution.py:1075
  (327 shorter events, 168.0 us)
Async XLA Ops:
  7.2 212.8 %all-gather.10.cloned.1.call-start = ((), (), s32[]{:S(2)}) async-start(), calls=%async_computation | async-start | bytes 11796480 | tf_op jit(solution)/shard_map/all_gather | solution.py:1134
  76.8 94.4 %copy-start = (bf16[2048,128]{1,0:T(8,128)(2,1)}, bf16[2048,128]{1,0:T(8,128)(2,1)S(1)}, u32[]{:S(2)}) copy-start(bf16[2048,128]{1,0:T(8,128)(2,1)S(1)} %get-tuple-element.88) | copy-start | bytes 1572868
  76.9 215.9 %all-gather.12.cloned.1.call-start = ((), (), s32[]{:S(2)}) async-start(), calls=%async_computation.1 | async-start | bytes 11796480 | tf_op jit(solution)/shard_map/all_gather | solution.py:1134
  77.6 439.2 %all-gather.14.cloned.1.call-start = ((), (), s32[]{:S(2)}) async-start(), calls=%async_computation.2 | async-start | bytes 7077888 | tf_op jit(solution)/shard_map/all_gather | solution.py:1333
  84.4 86.6 %copy-start.52 = (f32[2048]{0:T(1024)}, f32[2048]{0:T(1024)S(1)}, u32[]{:S(2)}) copy-start(f32[2048]{0:T(1024)S(1)} %get-tuple-element.234) | copy-start | bytes 24580
  248.2 37.5 %collective-permute-start = (bf16[2,512,384]{1,2,0:T(8,128)(2,1)S(1)}, bf16[2,512,384]{1,2,0:T(8,128)(2,1)S(1)}, u32[]{:S(2)}, u32[]{:S(2)}) collective-permute-start(bf16[2,512,384]{1,2,0:T(8,128)(2,1)S(1)} %pad_maximum_fusion.10), channel_id=1, source_target_pairs={{0,8},{8,0},{16,24},{24,16},{1,9},{9,1},{17,25},{25,17},{2,10},{10... | collective-permute-start | bytes 2359304 | tf_op jit(solution)/shard_map/ppermute | solution.py:959
  249.6 36.1 %collective-permute-start.1 = (bf16[2,512,384]{1,2,0:T(8,128)(2,1)S(1)}, bf16[2,512,384]{1,2,0:T(8,128)(2,1)}, u32[]{:S(2)}, u32[]{:S(2)}) collective-permute-start(bf16[2,512,384]{1,2,0:T(8,128)(2,1)S(1)} %pad_maximum_fusion.11), channel_id=1, source_target_pairs={{0,16},{8,24},{16,0},{24,8},{1,17},{9,25},{17,1},{25,9},{2,18},{10... | collective-permute-start | bytes 2359304 | tf_op jit(solution)/shard_map/ppermute | solution.py:959
  288.5 12.6 %collective-permute-start.3 = (bf16[1,512,384]{1,2,0:T(8,128)(2,1)}, bf16[1,512,384]{1,2,0:T(8,128)(2,1)}, u32[]{:S(2)}, u32[]{:S(2)}) collective-permute-start(bf16[1,512,384]{1,2,0:T(8,128)(2,1)} %fusion.63), channel_id=1, source_target_pairs={{0,8},{8,0},{16,24},{24,16},{1,9},{9,1},{17,25},{25,17},{2,10},{10... | collective-permute-start | bytes 1179656 | tf_op jit(solution)/shard_map/ppermute | solution.py:959
  288.7 12.3 %collective-permute-start.2 = (bf16[1,512,384]{1,2,0:T(8,128)(2,1)}, bf16[1,512,384]{1,2,0:T(8,128)(2,1)}, u32[]{:S(2)}, u32[]{:S(2)}) collective-permute-start(bf16[1,512,384]{1,2,0:T(8,128)(2,1)} %fusion.62), channel_id=1, source_target_pairs={{0,16},{8,24},{16,0},{24,8},{1,17},{9,25},{17,1},{25,9},{2,18},{10... | collective-permute-start | bytes 1179656 | tf_op jit(solution)/shard_map/ppermute | solution.py:959
  304.9 310.2 %all-gather.16.cloned.1.call-start = ((), (), s32[]{:S(2)}) async-start(), calls=%async_computation.3 | async-start | bytes 14155776 | tf_op jit(solution)/shard_map/all_gather | solution.py:1333
  311.6 41.4 %collective-permute-start.5 = (bf16[2,512,768]{2,1,0:T(8,128)(2,1)}, bf16[2,512,768]{2,1,0:T(8,128)(2,1)}, u32[]{:S(2)}, u32[]{:S(2)}) collective-permute-start(bf16[2,512,768]{2,1,0:T(8,128)(2,1)} %pad_maximum_fusion.5), channel_id=1, source_target_pairs={{0,16},{8,24},{16,0},{24,8},{1,17},{9,25},{17,1},{25,9},{2,18},{10... | collective-permute-start | bytes 4718600 | tf_op jit(solution)/shard_map/ppermute | solution.py:959
  311.9 41.1 %collective-permute-start.4 = (bf16[2,512,768]{2,1,0:T(8,128)(2,1)S(1)}, bf16[2,512,768]{2,1,0:T(8,128)(2,1)}, u32[]{:S(2)}, u32[]{:S(2)}) collective-permute-start(bf16[2,512,768]{2,1,0:T(8,128)(2,1)S(1)} %copy-done.44), channel_id=1, source_target_pairs={{0,8},{8,0},{16,24},{24,16},{1,9},{9,1},{17,25},{25,17},{2,10},{10... | collective-permute-start | bytes 4718600 | tf_op jit(solution)/shard_map/ppermute | solution.py:959
  354.5 16.9 %collective-permute-start.7 = (bf16[1,512,768]{2,1,0:T(8,128)(2,1)S(1)}, bf16[1,512,768]{2,1,0:T(8,128)(2,1)S(1)}, u32[]{:S(2)}, u32[]{:S(2)}) collective-permute-start(bf16[1,512,768]{2,1,0:T(8,128)(2,1)S(1)} %fusion.40), channel_id=1, source_target_pairs={{0,8},{8,0},{16,24},{24,16},{1,9},{9,1},{17,25},{25,17},{2,10},{10... | collective-permute-start | bytes 2359304 | tf_op jit(solution)/shard_map/ppermute | solution.py:959
  356.2 16.1 %collective-permute-start.6 = (bf16[1,512,768]{2,1,0:T(8,128)(2,1)S(1)}, bf16[1,512,768]{2,1,0:T(8,128)(2,1)S(1)}, u32[]{:S(2)}, u32[]{:S(2)}) collective-permute-start(bf16[1,512,768]{2,1,0:T(8,128)(2,1)S(1)} %fusion.39), channel_id=1, source_target_pairs={{0,16},{8,24},{16,0},{24,8},{1,17},{9,25},{17,1},{25,9},{2,18},{10... | collective-permute-start | bytes 2359304 | tf_op jit(solution)/shard_map/ppermute | solution.py:959
  376.6 414.8 %all-gather.20.cloned.1.call-start = ((), (), s32[]{:S(2)}) async-start(), calls=%async_computation.5 | async-start | bytes 21233664 | tf_op jit(solution)/shard_map/all_gather | solution.py:1333
  513.2 351.1 %all-gather.18.cloned.1.call-start = ((), (), s32[]{:S(2)}) async-start(), calls=%async_computation.4 | async-start | bytes 11796480 | tf_op jit(solution)/shard_map/all_gather | solution.py:1405
  590.1 7.7 collective-permute-start.8
  591.6 13.9 %collective-permute-start.9 = (bf16[2,512,256]{2,1,0:T(8,128)(2,1)}, bf16[2,512,256]{2,1,0:T(8,128)(2,1)}, u32[]{:S(2)}, u32[]{:S(2)}) collective-permute-start(bf16[2,512,256]{2,1,0:T(8,128)(2,1)} %pad_maximum_fusion.13), channel_id=1, source_target_pairs={{0,8},{8,0},{16,24},{24,16},{1,9},{9,1},{17,25},{25,17},{2,10},{10... | collective-permute-start | bytes 1572872 | tf_op jit(solution)/shard_map/ppermute | solution.py:959
  592.1 13.3 %collective-permute-start.10 = (bf16[2,512,256]{2,1,0:T(8,128)(2,1)S(1)}, bf16[2,512,256]{2,1,0:T(8,128)(2,1)}, u32[]{:S(2)}, u32[]{:S(2)}) collective-permute-start(bf16[2,512,256]{2,1,0:T(8,128)(2,1)S(1)} %pad_maximum_fusion.14), channel_id=1, source_target_pairs={{0,16},{8,24},{16,0},{24,8},{1,17},{9,25},{17,1},{25,9},{2,18},{10... | collective-permute-start | bytes 1572872 | tf_op jit(solution)/shard_map/ppermute | solution.py:959
  607.2 97.0 %collective-permute-start.12 = (bf16[1,512,256]{2,1,0:T(8,128)(2,1)}, bf16[1,512,256]{2,1,0:T(8,128)(2,1)S(1)}, u32[]{:S(2)}, u32[]{:S(2)}) collective-permute-start(bf16[1,512,256]{2,1,0:T(8,128)(2,1)} %fusion.65), channel_id=1, source_target_pairs={{0,8},{8,0},{16,24},{24,16},{1,9},{9,1},{17,25},{25,17},{2,10},{10... | collective-permute-start | bytes 786440 | tf_op jit(solution)/shard_map/ppermute | solution.py:959
  609.9 94.3 %collective-permute-start.11 = (bf16[1,512,256]{2,1,0:T(8,128)(2,1)}, bf16[1,512,256]{2,1,0:T(8,128)(2,1)}, u32[]{:S(2)}, u32[]{:S(2)}) collective-permute-start(bf16[1,512,256]{2,1,0:T(8,128)(2,1)} %fusion.64), channel_id=1, source_target_pairs={{0,16},{8,24},{16,0},{24,8},{1,17},{9,25},{17,1},{25,9},{2,18},{10... | collective-permute-start | bytes 786440 | tf_op jit(solution)/shard_map/ppermute | solution.py:959
  731.9 56.9 %copy-start.3 = (bf16[1,128,2048]{2,1,0:T(8,128)(2,1)S(1)}, bf16[1,128,2048]{2,1,0:T(8,128)(2,1)}, u32[]{:S(2)}) copy-start(bf16[1,128,2048]{2,1,0:T(8,128)(2,1)} %param.16) | copy-start | bytes 1572868
  731.9 57.2 %copy-start.16 = (f32[128,2048]{1,0:T(8,128)S(1)}, f32[128,2048]{1,0:T(8,128)}, u32[]{:S(2)}) copy-start(f32[128,2048]{1,0:T(8,128)} %copy-done.15) | copy-start | bytes 3145732
  731.9 57.2 %copy-start.26 = (f32[128,2048]{1,0:T(8,128)S(1)}, f32[128,2048]{1,0:T(8,128)}, u32[]{:S(2)}) copy-start(f32[128,2048]{1,0:T(8,128)} %copy-done.24) | copy-start | bytes 3145732
  (72 other events, 622.9 us)
Sparse Core Ops, SparseCore 0:
  77.0 97.1 all-gather.9
  176.6 113.2 all-gather.11
  305.0 66.8 all-gather.13
  376.7 166.4 all-gather.15
  545.3 204.9 all-gather.19
  751.7 112.5 all-gather.17

commit v3 on v2

--- a/solution.py
+++ b/solution.py
@@ -85,25 +85,18 @@
 def attend_kernel(
     block, q_ref, kv_ref, doc_ref, cos_ref, sin_ref, qg_ref, kg_ref, out_ref, key_ref, val_ref
 ):
-    length = kv_ref.shape[0]
-    head, part = pl.program_id(0), pl.program_id(1)
-
-    @pl.when((head == 0) & (part == 0))
+    @pl.when(pl.program_id(0) == 0)
     def _():
         key, unused = normed_rope(kv_ref[:, :HD], kg_ref[...], cos_ref[...], sin_ref[...])
         key_ref[...] = key.astype(BF16)
         val_ref[...] = kv_ref[:, HD:].astype(BF16)
 
-    for number in range(length // block):
-
-        @pl.when(part == number)
-        def _():
-            rows = pl.ds(number * block, block)
-            columns = (number + 1) * block
-            query, unused = normed_rope(q_ref[...], qg_ref[...], cos_ref[rows, :], sin_ref[rows, :])
-            weights, share = softmax_weights(query.astype(BF16), key_ref, doc_ref[...], number)
-            mixed = dot(weights.astype(BF16), val_ref[:columns, :])
-            out_ref[...] = (mixed * share).astype(BF16)
+    for number in range(kv_ref.shape[0] // block):
+        rows = pl.ds(number * block, block)
+        query, unused = normed_rope(q_ref[rows, :], qg_ref[...], cos_ref[rows, :], sin_ref[rows, :])
+        weights, share = softmax_weights(query.astype(BF16), key_ref, doc_ref[rows, :], number)
+        mixed = dot(weights.astype(BF16), val_ref[: (number + 1) * block, :])
+        out_ref[rows, :] = (mixed * share).astype(BF16)
 
 
 def attend_back_kernel(
@@ -125,11 +118,10 @@
     dk_ref,
     dv_ref,
 ):
-    length = kv_ref.shape[0]
-    head, part = pl.program_id(0), pl.program_id(1)
+    head = pl.program_id(0)
     scaling = HD**-0.5
 
-    @pl.when((head == 0) & (part == 0))
+    @pl.when(head == 0)
     def _():
         key, unused = normed_rope(kv_ref[:, :HD], kg_ref[...], cos_ref[...], sin_ref[...])
         key_ref[...] = key.astype(BF16)
@@ -138,32 +130,29 @@
         dv_ref[...] = jnp.zeros_like(dv_ref)
         qt_ref[...] = jnp.zeros_like(qt_ref)
 
-    for number in range(length // block):
-
-        @pl.when(part == number)
-        def _():
-            rows = pl.ds(number * block, block)
-            columns = (number + 1) * block
-            cosine, sine = cos_ref[rows, :], sin_ref[rows, :]
-            raw = q_ref[...]
-            query, factor = normed_rope(raw, qg_ref[...], cosine, sine)
-            query = query.astype(BF16)
-            key, value = key_ref[:columns, :], val_ref[:columns, :]
-            upstream = dm_ref[...]
-            weights, share = softmax_weights(query, key_ref, doc_ref[...], number)
-            probs = weights * share
-            prob_grad = dot_nt(upstream, value)
-            delta = jnp.sum(probs * prob_grad, axis=-1, keepdims=True)
-            score_grad = (probs * (prob_grad - delta)).astype(BF16)
-            dk_ref[:columns, :] += dot_tn(score_grad, query)
-            dv_ref[:columns, :] += dot_tn(probs.astype(BF16), upstream)
-            rotated = dot(score_grad, key) * scaling
-            query_grad = rotated * cosine - turn(rotated) * sine
-            raw_grad, terms = rms_back(raw, factor, qg_ref[...], query_grad)
-            dq_ref[...] = raw_grad.astype(BF16)
-            qt_ref[...] += jnp.sum(terms, axis=0, keepdims=True)
-
-    @pl.when((head == pl.num_programs(0) - 1) & (part == pl.num_programs(1) - 1))
+    for number in range(kv_ref.shape[0] // block):
+        rows = pl.ds(number * block, block)
+        columns = (number + 1) * block
+        cosine, sine = cos_ref[rows, :], sin_ref[rows, :]
+        raw = q_ref[rows, :]
+        query, factor = normed_rope(raw, qg_ref[...], cosine, sine)
+        query = query.astype(BF16)
+        key, value = key_ref[:columns, :], val_ref[:columns, :]
+        upstream = dm_ref[rows, :]
+        weights, share = softmax_weights(query, key_ref, doc_ref[rows, :], number)
+        probs = weights * share
+        prob_grad = dot_nt(upstream, value)
+        delta = jnp.sum(probs * prob_grad, axis=-1, keepdims=True)
+        score_grad = (probs * (prob_grad - delta)).astype(BF16)
+        dk_ref[:columns, :] += dot_tn(score_grad, query)
+        dv_ref[:columns, :] += dot_tn(probs.astype(BF16), upstream)
+        rotated = dot(score_grad, key) * scaling
+        query_grad = rotated * cosine - turn(rotated) * sine
+        raw_grad, terms = rms_back(raw, factor, qg_ref[...], query_grad)
+        dq_ref[rows, :] = raw_grad.astype(BF16)
+        qt_ref[...] += jnp.sum(terms, axis=0, keepdims=True)
+
+    @pl.when(head == pl.num_programs(0) - 1)
     def _():
         raw = kv_ref[:, :HD]
         cosine, sine = cos_ref[...], sin_ref[...]
@@ -176,14 +165,14 @@
         kt_ref[...] = jnp.sum(terms, axis=0, keepdims=True)
 
 
-def attention_specs(length, block, heads):
-    whole = lambda h, b: (0, 0)
+def attention_specs(length, heads):
+    whole = lambda h: (0, 0)
     return [
-        pl.BlockSpec((block, HD), lambda h, b: (b, h)),
-        pl.BlockSpec((length, 2 * HD), lambda h, b: (0, heads // 2)),
-        pl.BlockSpec((block, 1), lambda h, b: (b, 0)),
+        pl.BlockSpec((length, HD), lambda h: (0, h)),
+        pl.BlockSpec((length, 2 * HD), lambda h: (0, heads // 2)),
+        pl.BlockSpec((length, 1), whole),
         pl.BlockSpec((length, HD), whole),
-        pl.BlockSpec((length, HD), lambda h, b: (0, 1)),
+        pl.BlockSpec((length, HD), lambda h: (0, 1)),
         pl.BlockSpec((1, HD), whole),
         pl.BlockSpec((1, HD), whole),
     ]
@@ -191,21 +180,19 @@
 
 def attend(qkv_raw, doc_start, tables, query_gain, key_gain):
     length, width = qkv_raw.shape[0], qkv_raw.shape[1] - 2 * HD
-    block = 256
     return pl.pallas_call(
-        functools.partial(attend_kernel, block),
+        functools.partial(attend_kernel, 256),
         out_shape=jax.ShapeDtypeStruct((length, width), BF16),
         grid_spec=pltpu.PrefetchScalarGridSpec(
             num_scalar_prefetch=0,
-            grid=(width // HD, length // block),
-            in_specs=attention_specs(length, block, width // HD),
-            out_specs=pl.BlockSpec((block, HD), lambda h, b: (b, h)),
+            grid=(width // HD,),
+            in_specs=attention_specs(length, width // HD),
+            out_specs=pl.BlockSpec((length, HD), lambda h: (0, h)),
             scratch_shapes=[pltpu.VMEM((length, HD), BF16), pltpu.VMEM((length, HD), BF16)],
         ),
+        compiler_params=pltpu.CompilerParams(vmem_limit_bytes=40 * 2**20),
         cost_estimate=pl.CostEstimate(
-            flops=length * length,
-            bytes_accessed=length * width,
-            transcendentals=0,
+            flops=length * length, bytes_accessed=length * width, transcendentals=0
         ),
         name="attend",
     )(qkv_raw, qkv_raw, doc_start, tables, tables, query_gain, key_gain)
@@ -213,10 +200,9 @@
 
 def attend_back(qkv_raw, doc_start, tables, query_gain, key_gain, upstream):
     length, width = qkv_raw.shape[0], qkv_raw.shape[1] - 2 * HD
-    block = 256
-    whole = lambda h, b: (0, 0)
+    whole = lambda h: (0, 0)
     return pl.pallas_call(
-        functools.partial(attend_back_kernel, block),
+        functools.partial(attend_back_kernel, 256),
         out_shape=(
             jax.ShapeDtypeStruct((length, width), BF16),
             jax.ShapeDtypeStruct((length, 2 * HD), F32),
@@ -225,11 +211,11 @@
         ),
         grid_spec=pltpu.PrefetchScalarGridSpec(
             num_scalar_prefetch=0,
-            grid=(width // HD, length // block),
-            in_specs=attention_specs(length, block, width // HD)
-            + [pl.BlockSpec((block, HD), lambda h, b: (b, h))],
+            grid=(width // HD,),
+            in_specs=attention_specs(length, width // HD)
+            + [pl.BlockSpec((length, HD), lambda h: (0, h))],
             out_specs=(
-                pl.BlockSpec((block, HD), lambda h, b: (b, h)),
+                pl.BlockSpec((length, HD), lambda h: (0, h)),
                 pl.BlockSpec((length, 2 * HD), whole),
                 pl.BlockSpec((1, HD), whole),
                 pl.BlockSpec((1, HD), whole),
@@ -241,10 +227,9 @@
                 pltpu.VMEM((length, HD), F32),
             ],
         ),
+        compiler_params=pltpu.CompilerParams(vmem_limit_bytes=40 * 2**20),
         cost_estimate=pl.CostEstimate(
-            flops=length * length,
-            bytes_accessed=length * width,
-            transcendentals=0,
+            flops=length * length, bytes_accessed=length * width, transcendentals=0
         ),
         name="attend_back",
     )(qkv_raw, qkv_raw, doc_start, tables, tables, query_gain, key_gain, upstream)
@@ -937,19 +922,20 @@
 
 
 class GroupSum:
-    def __init__(self, partial, owners, group, flip):
+    def __init__(self, partials, owners, group, flip):
         self.owners, self.group = owners, group
-        self.rows = partial.shape[0] // owners
+        self.partials = partials if isinstance(partials, list) else [partials]
+        self.rows = self.partials[0].shape[0] // owners
         bits = list(range(owners.bit_length() - 1))
         self.order = bits[::-1] if flip else bits
         self.held = {piece: None for piece in range(owners)}
-        self.partial = partial
 
     def piece(self, number):
         if self.held[number] is not None:
             return self.held[number]
         start = (self.group ^ number) * self.rows
-        return lax.dynamic_slice_in_dim(self.partial, start, self.rows, 0)
+        slices = [lax.dynamic_slice_in_dim(p, start, self.rows, 0) for p in self.partials]
+        return slices[0] if len(slices) == 1 else jnp.concatenate(slices, axis=1)
 
     def send(self):
         bit = self.order.pop(0)
@@ -1022,12 +1008,16 @@
     query_ref,
     key_ref,
     value_ref,
+    gain_ref,
     q_ref,
     k_ref,
     v_ref,
     o_ref,
     router_ref,
-    rows_ref,
+    attention_ref,
+    mixture_ref,
+    qg_ref,
+    kg_ref,
     sums_ref,
 ):
     width = o_ref.shape[1]
@@ -1062,8 +1052,12 @@
 
     @pl.when(at == pl.num_programs(0) - 1)
     def _():
-        router_ref[...] = sums_ref[:, :EXPERTS]
-        rows_ref[...] = jnp.transpose(sums_ref[...], (1, 0))[EXPERTS : EXPERTS + 8, :]
+        rows = jnp.transpose(sums_ref[...], (1, 0))
+        router_ref[...] = rows[:EXPERTS, :]
+        mixture_ref[...] = rows[EXPERTS : EXPERTS + 1, :]
+        qg_ref[...] = rows[EXPERTS + 1 : EXPERTS + 2, :]
+        kg_ref[...] = rows[EXPERTS + 2 : EXPERTS + 3, :]
+        attention_ref[...] = rows[EXPERTS + 3 : EXPERTS + 4, :] / gain_ref[...]
 
 
 def finish_attention(packed, weights, width, sharers):
@@ -1079,21 +1073,27 @@
             jax.ShapeDtypeStruct((shard, HK * HD), F32),
             jax.ShapeDtypeStruct((shard, HK * HD), F32),
             jax.ShapeDtypeStruct((shard, width * parts), F32),
-            jax.ShapeDtypeStruct((shard, EXPERTS), F32),
-            jax.ShapeDtypeStruct((8, shard), F32),
-        ),
+            jax.ShapeDtypeStruct((EXPERTS, shard), F32),
+        )
+        + (jax.ShapeDtypeStruct((1, shard), F32),) * 4,
         grid_spec=pltpu.PrefetchScalarGridSpec(
             num_scalar_prefetch=0,
             grid=(parts,),
-            in_specs=[pl.BlockSpec((1, shard, total), lambda c: (c, 0, 0)), own, head, head],
+            in_specs=[
+                pl.BlockSpec((1, shard, total), lambda c: (c, 0, 0)),
+                own,
+                head,
+                head,
+                pl.BlockSpec((1, shard), whole),
+            ],
             out_specs=(
                 own,
                 head,
                 head,
                 own,
-                pl.BlockSpec((shard, EXPERTS), whole),
-                pl.BlockSpec((8, shard), whole),
-            ),
+                pl.BlockSpec((EXPERTS, shard), whole),
+            )
+            + (pl.BlockSpec((1, shard), whole),) * 4,
             scratch_shapes=[pltpu.VMEM((shard, spare), F32)],
         ),
         cost_estimate=pl.CostEstimate(flops=0, bytes_accessed=packed.size // 16, transcendentals=0),
@@ -1133,23 +1133,19 @@
 
     gather_group = lambda v: lax.all_gather(v, "group", axis=0, tiled=True)
 
-    def column(vector):
-        return jnp.pad(vector, (0, shard - vector.shape[0]))[:, None]
-
     def columns(array, start, count):
         return lax.dynamic_slice_in_dim(array, start, count, 1)
 
-    extras = jnp.concatenate(
+    spread = lambda vector: jnp.pad(vector, (0, shard - vector.shape[0]))
+    gain_rows = jnp.concatenate(
         [
-            router_weight,
-            attention_gain[:, None],
-            mixture_gain[:, None],
-            column(query_gain),
-            column(key_gain),
-            jnp.zeros((shard, PAD - EXPERTS - 4), BF16),
-        ],
-        axis=1,
-    )
+            attention_gain,
+            mixture_gain,
+            spread(query_gain),
+            spread(key_gain),
+            jnp.zeros((12 * shard,), BF16),
+        ]
+    ).reshape(16, shard)
     comm = lambda plan, number, name, micros, **transfers: comm_call(
         plan, number, name, parts, owners, micros, **transfers
     )
@@ -1157,13 +1153,13 @@
         return jnp.concatenate(
             [
                 lax.dynamic_index_in_dim(w, at * experts + number, 0, keepdims=False)
-                for w in (gate_weight, up_weight, down_weight)
+                for w in (up_weight, down_weight)
             ],
             axis=1,
         )
 
     packs = [expert_pack(number, here) for number in range(experts)]
-    extras = after(extras, *packs)
+    gain_rows = after(gain_rows, *packs)
 
     def cut(start, count):
         return lambda ref: ref.at[:, pl.ds(pl.multiple_of(start(), count), count)]
@@ -1172,14 +1168,19 @@
     key_cut = cut(lambda: place() // sharers * HD, HD)
     own_cut = cut(lambda: place() * width, width)
 
-    inputs_all, positions_all, extras, wquery, wkey, wvalue, wout = comm(
+    def gate_item(number):
+        return (gate_weight, lambda ref: ref.at[place() * experts + number], (shard, F))
+
+
+    inputs_all, positions_all, gain_rows, router, wquery, wkey, wvalue, wout = comm(
         plan_gather,
         0,
         "gather_tokens",
         45,
         gather=(tokens[0], jnp.broadcast_to(positions, (8, rows))),
         group_gather=(
-            (extras, lambda ref: ref, (shard, PAD)),
+            (gain_rows, lambda ref: ref, (16, shard)),
+            (router_weight, lambda ref: ref, (shard, EXPERTS)),
             (query_weight, own_cut, (shard, width)),
             (key_weight, key_cut, (shard, HD)),
             (value_weight, key_cut, (shard, HD)),
@@ -1189,16 +1190,10 @@
     packs = [gather_group(after(pack, positions_all)) for pack in packs]
     wqkv = jnp.concatenate([wquery, wkey, wvalue], axis=1)
 
-    router = extras[:, :EXPERTS]
-    attention_gains = extras[:, EXPERTS].astype(F32)
-    mixture_gains = extras[:, EXPERTS + 1].astype(F32)
-    head_gain = (
-        lambda col: extras[:, col]
-        .reshape(owners, shard)[:, : HD // owners]
-        .reshape(1, HD)
-        .astype(F32)
-    )
-    query_gains, key_gains = head_gain(EXPERTS + 2), head_gain(EXPERTS + 3)
+    gain_rows = gain_rows.reshape(owners, 16, shard).astype(F32)
+    attention_gains, mixture_gains = gain_rows[:, 0].reshape(D), gain_rows[:, 1].reshape(D)
+    query_gains = gain_rows[:, 2, : HD // owners].reshape(1, HD)
+    key_gains = gain_rows[:, 3, : HD // owners].reshape(1, HD)
 
     positions_all = positions_all.reshape(parts, 8, rows)[:, 0].reshape(length)
     doc_start = (jnp.arange(length, dtype=jnp.int32) - positions_all)[:, None]
@@ -1208,13 +1203,14 @@
     qkv_raw = dot(normed_all, wqkv)
     tables = (qkv_raw, doc_start, rope_tables(positions_all), query_gains, key_gains)
     mixed_low = attend(*tables)
-    attn_out, upstream_all = comm(
+    attn_out, upstream_all, first_gate = comm(
         plan_scatter,
         1,
         "scatter_attention",
         50,
         scatter=((mixed_low, wout),),
         gather=(cotangent[0],),
+        group_gather=(gate_item(0),),
     )
     hidden = inputs + attn_out
     moe_normed, moe_factor = rms_parts(hidden, mixture_gains)
@@ -1227,13 +1223,15 @@
     expo = jnp.exp(chosen - jnp.max(chosen, axis=-1, keepdims=True))
     gates = expo / jnp.sum(expo, axis=-1, keepdims=True)
     combine = jnp.sum(gates[:, :, None] * onehot, axis=1)
-    moe_all, combine_all = comm(
+    moe_all, combine_all, *gates_all = comm(
         plan_gather,
         2,
         "gather_mixture",
         45,
         gather=(moe_low, jnp.pad(combine, ((0, 0), (0, PAD - EXPERTS)))),
-    )
+        group_gather=[gate_item(number) for number in range(1, experts)],
+    )
+    gates_all = [first_gate, *gates_all]
     combine_all = columns(combine_all, here * experts, experts)
 
     def expert_forward(number, weights, gate_all):
@@ -1255,8 +1253,8 @@
     def weight_grad(left, right):
         return dot_tn(left, right).astype(BF16)
 
-    split = lambda pack: (pack[:, :F], pack[:, F : 2 * F], pack[:, 2 * F :])
-    weights = split(packs[0])
+    split = lambda number, pack: (gates_all[number], pack[:, :F], pack[:, F:])
+    weights = split(0, packs[0])
     gate_all = dot(moe_all, weights[0])
     gate_all, up_all, act_low, weighted = expert_forward(0, weights, gate_all)
     combine_grads, layer_terms, moe_terms, gathered = [], [], [], []
@@ -1282,7 +1280,7 @@
             GroupSum(after(grads[0], *sent), owners, group, False),
             GroupSum(after(grads[1], *sent), owners, group, True),
         ]
-        weights = split(after(packs[number], *send_all(other_sums)))
+        weights = split(number, after(packs[number], *send_all(other_sums)))
         gate_all = dot(moe_all, weights[0])
         add_all(down_sums, gate_all)
         finish_all(down_sums)
@@ -1297,21 +1295,30 @@
     combine_grads.append(combine_grad)
     layer_terms.append((weighted, weights[2]))
     moe_terms += [(gate_grad, weights[0]), (up_grad, weights[1])]
+    for pieces in gathered:
+        add_all(pieces[1], gate_grad, up_grad)
+        if pieces[1][0].order:
+            gate_grad, up_grad = after((gate_grad, up_grad), *send_all(pieces[1]))
     last_grads += [weight_grad(moe_all, gate_grad), weight_grad(moe_all, up_grad)]
     for pieces in gathered:
         add_all(pieces[1], *last_grads)
-        if pieces[1][0].order:
-            moe_terms = after(moe_terms, *send_all(pieces[1]))
+        finish_all(pieces[1])
+        pieces[1] = jnp.stack([one.held[0] for one in pieces[1]])
+        last_grads = list(after(last_grads, pieces[1]))
+    half = F // 2
+    last_sums = [
+        GroupSum([last_grads[0][:, :half], last_grads[1]], owners, group, False),
+        GroupSum([last_grads[0][:, half:], last_grads[2]], owners, group, True),
+    ]
+    moe_terms = after(moe_terms, *send_all(last_sums))
     moe_part = sum(dot_nt(left, right) for left, right in moe_terms[:2])
     layer_part = sum(dot_nt(left, right) for left, right in layer_terms)
-    for pieces in gathered:
-        add_all(pieces[1], moe_part, layer_part)
-        finish_all(pieces[1])
-        pieces[1] = jnp.stack([one.held[0] for one in pieces[1]])
-        moe_terms[2:] = after(moe_terms[2:], pieces[1])
     for left, right in moe_terms[2:]:
         moe_part = moe_part + dot_nt(left, right)
     moe_part_low = moe_part.astype(BF16)
+    add_all(last_sums, moe_part_low)
+    if last_sums[0].order:
+        moe_part_low = after(moe_part_low, *send_all(last_sums))
     combine_grad = jnp.concatenate(combine_grads, axis=1)
     high = combine_grad.astype(BF16).astype(F32)
     low = combine_grad - high
@@ -1321,15 +1328,14 @@
         + jnp.where(at == EXPERTS + here * experts + number, low[:, number : number + 1], 0.0)
         for number in range(experts)
     ).astype(BF16)
-    moe_sum, small_sum, *last_pieces = comm(
-        plan_scatter,
-        3,
-        "scatter_mixture",
-        60,
-        scatter=((moe_part_low,), (small,)),
-        group_scatter=last_grads,
-    )
-    gathered.append([jnp.stack(last_pieces)])
+    moe_sum, small_sum = comm(
+        plan_scatter, 3, "scatter_mixture", 60, scatter=((moe_part_low,), (small,))
+    )
+    add_all(last_sums, moe_sum)
+    finish_all(last_sums)
+    ends = [one.held[0] for one in last_sums]
+    down = jnp.concatenate([end[:, :half] for end in ends], axis=1)
+    gathered.append([jnp.stack([down] + [end[:, half:] for end in ends])])
     unfold = lambda piece: lax.all_gather(piece, "ctx").reshape(parts, -1, shard, F)
     expert_packs = [[unfold(piece) for piece in pieces] for pieces in gathered]
 
@@ -1412,8 +1418,11 @@
     )
     input_part, unused = rms_back(inputs, attn_factor, attention_gains, normed_grad)
     tokens_grad = (hidden_grad + input_part).astype(BF16)[None]
-    query_grad, key_grad, value_grad, output_grad, router_grad, gain_rows = finish_attention(
-        attn_grads, (query_weight, key_weight, value_weight), width, sharers
+    query_grad, key_grad, value_grad, output_grad, router_grad, *gain_grads = finish_attention(
+        attn_grads,
+        (query_weight, key_weight, value_weight, attention_gain.astype(F32).reshape(1, shard)),
+        width,
+        sharers,
     )
     finished = ()
     for number in range(experts):
@@ -1422,15 +1431,15 @@
     return (
         layer_out,
         tokens_grad,
-        gain_rows[3] / attention_gain.astype(F32),
+        gain_grads[0].reshape(shard),
         query_grad,
         key_grad,
         value_grad,
         output_grad,
-        gain_rows[1, : HD // owners],
-        gain_rows[2, : HD // owners],
-        gain_rows[0],
-        router_grad,
+        gain_grads[2][0, : HD // owners],
+        gain_grads[3][0, : HD // owners],
+        gain_grads[1].reshape(shard),
+        router_grad.T,
         whole(finished[1]),
         whole(finished[2]),
         whole(finished[0]),

time: 897 us -> 864 us (0.963)
  waiting for transfers between devices: 78.8 us -> 48.4 us
    all_gather x1, waiting for transfers between devices: 52.1 us -> 3.93 us  [per_device(): attn_grads = lax.all_gather(attn_piece, 'ctx')]
    ppermute x12 -> x16, waiting for transfers between devices: 25.8 us -> 43.7 us  [send(): self.got = lax.ppermute(self.sent, 'group', pairs)]
    pallas_call x7, Pallas kernels: 453 us -> 471 us  [comm_call(): pl.pallas_call(functools.partial(comm_kernel, plan, chips, owners, counts...]
    pallas_call x2, Pallas kernels: 45.1 us -> 30.5 us  [the longest x1 19.1 us: attend_back(): pl.pallas_call(functools.partial(attend_back_kernel, 256), out_shape=(jax...]
  transfers between devices with their start and end apart: 19 -> 23, of which waited for: 5 -> 12; matrix products, arithmetic and copies ran while one was open for 22% -> 23% of each run, Pallas kernels for 55% -> 57%
where the time goes in v3:
time: 864 us; the launch traced here: 859 us
  Pallas kernels  558 us (65%)
  matrix products  133 us (15%)
  other arithmetic  55 us (6%)
  waiting for transfers between devices  48.4 us (6%)
  local copies, waits for them, and re-layouts  36.9 us (4%)
  between operations  15.9 us (2%)
  starting transfers between devices  11.7 us (1%)
    pallas_call x7, Pallas kernels, comm_call(): pl.pallas_call(functools.partial(comm_kernel, plan, chips, owners, counts...  471 us
    dot_general x9, matrix products, dot(): return jnp.dot(left, right, preferred_element_type=F32)  48.4 us
    dot_general x7, matrix products, dot_nt(): lax.dot_general(left, right, (((1,), (1,)), ((), ())), preferred_element_...  46 us
    ppermute x16, waiting for transfers between devices, send(): self.got = lax.ppermute(self.sent, 'group', pairs)  43.7 us
    pallas_call x2, Pallas kernels, widen(): pl.pallas_call(functools.partial(widen_kernel, counts), out_shape=(shape,...  41.7 us
    dot_general x9, matrix products, dot_tn(): lax.dot_general(left, right, (((0,), (0,)), ((), ())), preferred_element_...  38.1 us
    pallas_call x1, Pallas kernels, attend_back(): pl.pallas_call(functools.partial(attend_back_kernel, 256), out_shape=(jax...  19.1 us
    unnamed x203, local copies, waits for them, and re-layouts  17.5 us
  transfers between devices with their start and end apart: 23, of which 12 were waited for; matrix products, arithmetic and copies ran while one was open for 23% of the time, Pallas kernels for 57%

profile of v3, /device:TPU:17, one launch (start us, length us, event | category | flops | bytes accessed | tf_op | source)
XLA Modules:
  0.0 858.9 jit_solution(3107083827938101310)
XLA Ops:
  18.2 52.1 %gather_tokens.1 = (bf16[1024,2048]{1,0:T(8,128)(2,1)}, s32[64,128]{1,0:T(8,128)S(1)}, bf16[64,512]{1,0:T(8,128)(2,1)S(1)}, bf16[2048,16]{1,0:T(8,128)(2,1)S(1)}...) custom-call(bf16[128,2048]{1,0:T(8,128)(2,1)S(1)} %bitcast.238, ...), custom_call_target="tpu_custom_call" | custom-call | bytes 1530000 | tf_op jit(solution)/shard_map/gather_tokens/pallas_call | solution.py:813
  84.5 11.4 %attend.1.refs_0_ = bf16[1024,512]{1,0:T(8,128)(2,1)S(1)} custom-call(f32[1024,768]{1,0:T(8,128)S(1)} %fusion.7.q_ref.kv_ref, f32[1024,768]{1,0:T(8,128)S(1)} %fusion.7.q_ref.kv_ref, s32[1024,1]{1,0:T(8,128)S(1)} %iota_subtract_fusion.doc_ref, f32[1024,256]{1,0:T(8,128)S(1)} %pad_maximum_fusion.11.cos_ref.sin_ref, ...), custom_call_target="tpu_custom_call" | custom-call | flops 1048576 | bytes 524288 | tf_op jit(solution)/shard_map/attend/pallas_call | solution.py:183
  95.9 66.8 %scatter_attention.1 = (f32[128,2048]{1,0:T(8,128)S(1)}, bf16[1024,2048]{1,0:T(8,128)(2,1)}, bf16[2048,768]{1,0:T(8,128)(2,1)}) custom-call(bf16[1024,512]{1,0:T(8,128)(2,1)S(1)} %attend.1.refs_0_, bf16[2048,512]{1,0:T(8,128)(2,1)S(1)} %copy-done.19, bf16[128,2048]{1,0:T(8,128)(2,1)S(1)} %bitcast.239, bf16[16,512,768]{2,1,0:T(8,128)(2,1)} %refs_2_.1), custom_call_target="tpu_custom_call" | custom-call | bytes 1700000 | tf_op jit(solution)/shard_map/scatter_attention/pallas_call | solution.py:813
  164.8 46.7 %gather_mixture.1 = (bf16[1024,2048]{1,0:T(8,128)(2,1)}, f32[1024,128]{1,0:T(8,128)S(1)}, bf16[2048,768]{1,0:T(8,128)(2,1)S(1)}) custom-call(bf16[128,2048]{1,0:T(8,128)(2,1)S(1)} %multiply_convert_fusion.6.refs_0_, f32[128,128]{1,0:T(8,128)S(1)} %pad.28.refs_1_, bf16[16,512,768]{2,1,0:T(8,128)(2,1)} %refs_2_.1), custom_call_target="tpu_custom_call" | custom-call | bytes 1530000 | tf_op jit(solution)/shard_map/gather_mixture/pallas_call | solution.py:813
  213.2 7.3 fusion.88
  221.2 6.4 fusion.76
  239.8 5.7 fusion.15
  285.3 8.8 %fusion.90 = f32[1024,768]{0,1:T(8,128)} fusion(bf16[1024,2048]{1,0:T(8,128)(2,1)} %get-tuple-element.106, bf16[2048,768]{1,0:T(8,128)(2,1)S(1)} %slice.152), kind=kOutput, calls=%fused_computation.240 | convolution fusion | flops 3221225472 | bytes 10485760 | tf_op jit(solution)/shard_map/dot_general | solution.py:39
  294.2 8.1 fusion.6
  302.4 7.5 convolution_convert_fusion.3
  351.8 6.0 fusion.91
  357.9 5.7 fusion.92
  369.3 13.4 %add_convert_fusion.refs_0_ = bf16[1024,2048]{1,0:T(8,128)(2,1)S(1)} fusion(f32[1024,2048]{1,0:T(8,128)} %fusion.93, f32[1024,2048]{1,0:T(8,128)} %fusion.91, f32[1024,2048]{1,0:T(8,128)} %fusion.92, bf16[1024,768]{0,1:T(8,128)(2,1)} %copy-done.53, bf16[2048,768]{1,0:T(8,128)(2,1)} %copy-done.37), kind=kOutput, calls=%fused_computation.5 | convolution fusion | flops 3229614080 | bytes 34078720 | tf_op jit(solution)/shard_map/dot_general | solution.py:43
  382.7 16.0 %collective-permute-done.9 = bf16[2,512,1152]{2,1,0:T(8,128)(2,1)} collective-permute-done((bf16[2,512,1152]{2,1,0:T(8,128)(2,1)}, bf16[2,512,1152]{2,1,0:T(8,128)(2,1)}, u32[]{:S(2)}, u32[]{:S(2)}) %collective-permute-start.9) | collective-permute-done | bytes 2359328 | tf_op jit(solution)/shard_map/ppermute | solution.py:945
  404.3 83.6 %scatter_mixture.1 = (f32[128,2048]{1,0:T(8,128)S(1)}, f32[128,128]{1,0:T(8,128)S(1)}) custom-call(bf16[1024,2048]{1,0:T(8,128)(2,1)S(1)} %add_convert_fusion.refs_0_, bf16[1024,128]{1,0:T(8,128)(2,1)S(1)} %add_convert_fusion.6.refs_1_), custom_call_target="tpu_custom_call" | custom-call | bytes 2040000 | tf_op jit(solution)/shard_map/scatter_mixture/pallas_call | solution.py:813
  497.2 82.2 %gather_attention.1 = bf16[1024,2048]{1,0:T(8,128)(2,1)S(1)} custom-call(bf16[128,2048]{1,0:T(8,128)(2,1)S(1)} %get-tuple-element.144.refs_0_), custom_call_target="tpu_custom_call" | custom-call | bytes 1530000 | tf_op jit(solution)/shard_map/gather_attention/pallas_call | solution.py:813
  587.2 19.1 %attend_back.1 = (bf16[1024,512]{1,0:T(8,128)(2,1)S(1)}, f32[1024,256]{1,0:T(8,128)S(1)}, f32[1,128]{1,0:T(1,128)S(1)}, f32[1,128]{1,0:T(1,128)S(1)}) custom-call(f32[1024,768]{1,0:T(8,128)S(1)} %copy-done.1, f32[1024,768]{1,0:T(8,128)S(1)} %copy-done.1, s32[1024,1]{1,0:T(8,128)S(1)} %copy-done.9, f32[1024,256]{1,0:T(8,128)S(1)} %copy-done.3, ...), custom_call_target="tpu_custom_call" | custom-call | flops 1048576 | bytes 524288 | tf_op jit(solution)/shard_map/attend_back/pallas_call | solution.py:204
  607.0 7.6 add_convert_fusion.1.refs_0_
  620.0 8.6 %collective-permute-done.12 = bf16[2,512,256]{2,1,0:T(8,128)(2,1)} collective-permute-done((bf16[2,512,256]{2,1,0:T(8,128)(2,1)S(1)}, bf16[2,512,256]{2,1,0:T(8,128)(2,1)}, u32[]{:S(2)}, u32[]{:S(2)}) %collective-permute-start.12) | collective-permute-done | bytes 524320 | tf_op jit(solution)/shard_map/ppermute | solution.py:945
  637.8 60.7 %scatter_grads.1 = (f32[128,2048]{1,0:T(8,128)S(1)}, bf16[512,768]{1,0:T(8,128)(2,1)S(1)}) custom-call(bf16[1024,2048]{1,0:T(8,128)(2,1)} %add_convert_fusion.1.refs_0_, bf16[2048,768]{1,0:T(8,128)(2,1)S(1)} %add_convert_fusion.2.refs_1_), custom_call_target="tpu_custom_call" | custom-call | bytes 2040000 | tf_op jit(solution)/shard_map/scatter_grads/pallas_call | solution.py:813
  705.7 20.9 %widen.2 = (f32[8,2,512,768]{3,2,1,0:T(8,128)}, f32[8,2,512,768]{3,2,1,0:T(8,128)}, f32[8,2,512,768]{3,2,1,0:T(8,128)}) custom-call(bf16[8,1,512,768]{3,2,1,0:T(8,128)(2,1)} %bitcast.249, bf16[8,2,512,768]{3,2,1,0:T(8,128)(2,1)} %bitcast.247), custom_call_target="tpu_custom_call" | custom-call | bytes 589824 | tf_op jit(solution)/shard_map/widen/pallas_call | solution.py:987
  727.9 78.6 %scatter_normed.1 = f32[128,2048]{1,0:T(8,128)S(1)} custom-call(bf16[1024,640]{1,0:T(8,128)(2,1)S(1)} %copy-done.7, bf16[2048,640]{1,0:T(8,128)(2,1)S(1)} %pad_maximum_fusion.refs_1_), custom_call_target="tpu_custom_call" | custom-call | bytes 2040000 | tf_op jit(solution)/shard_map/scatter_normed/pallas_call | solution.py:813
  809.1 20.8 %widen.3 = (f32[8,2,512,768]{3,2,1,0:T(8,128)}, f32[8,2,512,768]{3,2,1,0:T(8,128)}, f32[8,2,512,768]{3,2,1,0:T(8,128)}) custom-call(bf16[8,3,512,768]{3,2,1,0:T(8,128)(2,1)} %bitcast.246, f32[8,2,512,768]{3,2,1,0:T(8,128)} %get-tuple-element.170.refs_1_, ...), custom_call_target="tpu_custom_call", output_to_operand_aliasing={{0}: (1, {}), {1}: (2, {}), {2}: (3, {})} | custom-call | bytes 589824 | tf_op jit(solution)/shard_map/widen/pallas_call | solution.py:987
  833.9 15.5 %finish_attention.1 = (f32[512,4096]{1,0:T(8,128)}, f32[512,512]{1,0:T(8,128)}, f32[512,512]{1,0:T(8,128)}, f32[512,4096]{1,0:T(8,128)}, f32[16,512]{1,0:T(8,128...) custom-call(bf16[8,512,1280]{2,1,0:T(8,128)(2,1)} %bitcast.248, ...), custom_call_target="tpu_custom_call" | custom-call | bytes 327680 | tf_op jit(solution)/shard_map/finish_attention/pallas_call | solution.py:1069
  (392 shorter events, 183.3 us)
Async XLA Ops:
  7.2 214.0 %all-gather.10.cloned.1.call-start = ((), (), s32[]{:S(2)}) async-start(), calls=%async_computation | async-start | bytes 7864320 | tf_op jit(solution)/shard_map/all_gather | solution.py:1134
  71.6 92.1 %copy-start.16 = (bf16[2048,16]{1,0:T(8,128)(2,1)}, bf16[2048,16]{1,0:T(8,128)(2,1)S(1)}, u32[]{:S(2)}) copy-start(bf16[2048,16]{1,0:T(8,128)(2,1)S(1)} %get-tuple-element.104) | copy-start | bytes 196612
  71.7 211.4 %all-gather.12.cloned.1.call-start = ((), (), s32[]{:S(2)}) async-start(), calls=%async_computation.1 | async-start | bytes 7864320 | tf_op jit(solution)/shard_map/all_gather | solution.py:1134
  72.4 424.8 %all-gather.14.cloned.1.call-start = ((), (), s32[]{:S(2)}) async-start(), calls=%async_computation.2 | async-start | bytes 7077888 | tf_op jit(solution)/shard_map/all_gather | solution.py:1339
  238.0 24.0 %collective-permute-start = (bf16[2,512,384]{1,2,0:T(8,128)(2,1)S(1)}, bf16[2,512,384]{1,2,0:T(8,128)(2,1)S(1)}, u32[]{:S(2)}, u32[]{:S(2)}) collective-permute-start(bf16[2,512,384]{1,2,0:T(8,128)(2,1)S(1)} %pad_maximum_fusion.12), channel_id=1, source_target_pairs={{0,8},{8,0},{16,24},{24,16},{1,9},{9,1},{17,25},{25,17},{2,10},{10... | collective-permute-start | bytes 2359304 | tf_op jit(solution)/shard_map/ppermute | solution.py:945
  238.7 23.2 %collective-permute-start.1 = (bf16[2,512,384]{1,2,0:T(8,128)(2,1)S(1)}, bf16[2,512,384]{1,2,0:T(8,128)(2,1)S(1)}, u32[]{:S(2)}, u32[]{:S(2)}) collective-permute-start(bf16[2,512,384]{1,2,0:T(8,128)(2,1)S(1)} %pad_maximum_fusion.13), channel_id=1, source_target_pairs={{0,16},{8,24},{16,0},{24,8},{1,17},{9,25},{17,1},{25,9},{2,18},{10... | collective-permute-start | bytes 2359304 | tf_op jit(solution)/shard_map/ppermute | solution.py:945
  262.9 9.8 %collective-permute-start.3 = (bf16[1,512,384]{1,2,0:T(8,128)(2,1)}, bf16[1,512,384]{1,2,0:T(8,128)(2,1)S(1)}, u32[]{:S(2)}, u32[]{:S(2)}) collective-permute-start(bf16[1,512,384]{1,2,0:T(8,128)(2,1)} %fusion.64), channel_id=1, source_target_pairs={{0,8},{8,0},{16,24},{24,16},{1,9},{9,1},{17,25},{25,17},{2,10},{10... | collective-permute-start | bytes 1179656 | tf_op jit(solution)/shard_map/ppermute | solution.py:945
  265.0 9.5 %collective-permute-start.2 = (bf16[1,512,384]{1,2,0:T(8,128)(2,1)}, bf16[1,512,384]{1,2,0:T(8,128)(2,1)}, u32[]{:S(2)}, u32[]{:S(2)}) collective-permute-start(bf16[1,512,384]{1,2,0:T(8,128)(2,1)} %fusion.63), channel_id=1, source_target_pairs={{0,16},{8,24},{16,0},{24,8},{1,17},{9,25},{17,1},{25,9},{2,18},{10... | collective-permute-start | bytes 1179656 | tf_op jit(solution)/shard_map/ppermute | solution.py:945
  278.2 359.6 %all-gather.16.cloned.1.call-start = ((), (), s32[]{:S(2)}) async-start(), calls=%async_computation.3 | async-start | bytes 14155776 | tf_op jit(solution)/shard_map/all_gather | solution.py:1339
  280.1 33.7 %collective-permute-start.5 = (bf16[2,512,768]{2,1,0:T(8,128)(2,1)S(1)}, bf16[2,512,768]{2,1,0:T(8,128)(2,1)}, u32[]{:S(2)}, u32[]{:S(2)}) collective-permute-start(bf16[2,512,768]{2,1,0:T(8,128)(2,1)S(1)} %pad_maximum_fusion.7), channel_id=1, source_target_pairs={{0,16},{8,24},{16,0},{24,8},{1,17},{9,25},{17,1},{25,9},{2,18},{10... | collective-permute-start | bytes 4718600 | tf_op jit(solution)/shard_map/ppermute | solution.py:945
  282.0 33.8 %collective-permute-start.4 = (bf16[2,512,768]{2,1,0:T(8,128)(2,1)}, bf16[2,512,768]{2,1,0:T(8,128)(2,1)}, u32[]{:S(2)}, u32[]{:S(2)}) collective-permute-start(bf16[2,512,768]{2,1,0:T(8,128)(2,1)} %pad_maximum_fusion.6), channel_id=1, source_target_pairs={{0,8},{8,0},{16,24},{24,16},{1,9},{9,1},{17,25},{25,17},{2,10},{10... | collective-permute-start | bytes 4718600 | tf_op jit(solution)/shard_map/ppermute | solution.py:945
  317.2 15.8 %collective-permute-start.7 = (bf16[1,512,768]{2,1,0:T(8,128)(2,1)S(1)}, bf16[1,512,768]{2,1,0:T(8,128)(2,1)S(1)}, u32[]{:S(2)}, u32[]{:S(2)}) collective-permute-start(bf16[1,512,768]{2,1,0:T(8,128)(2,1)S(1)} %fusion.44), channel_id=1, source_target_pairs={{0,8},{8,0},{16,24},{24,16},{1,9},{9,1},{17,25},{25,17},{2,10},{10... | collective-permute-start | bytes 2359304 | tf_op jit(solution)/shard_map/ppermute | solution.py:945
  319.5 15.4 %collective-permute-start.6 = (bf16[1,512,768]{2,1,0:T(8,128)(2,1)S(1)}, bf16[1,512,768]{2,1,0:T(8,128)(2,1)S(1)}, u32[]{:S(2)}, u32[]{:S(2)}) collective-permute-start(bf16[1,512,768]{2,1,0:T(8,128)(2,1)S(1)} %fusion.43), channel_id=1, source_target_pairs={{0,16},{8,24},{16,0},{24,8},{1,17},{9,25},{17,1},{25,9},{2,18},{10... | collective-permute-start | bytes 2359304 | tf_op jit(solution)/shard_map/ppermute | solution.py:945
  339.2 469.9 %all-gather.20.cloned.1.call-start = ((), (), s32[]{:S(2)}) async-start(), calls=%async_computation.5 | async-start | bytes 21233664 | tf_op jit(solution)/shard_map/all_gather | solution.py:1339
  345.7 53.0 %collective-permute-start.8 = (bf16[2,512,1152]{2,1,0:T(8,128)(2,1)}, bf16[2,512,1152]{2,1,0:T(8,128)(2,1)}, u32[]{:S(2)}, u32[]{:S(2)}) collective-permute-start(bf16[2,512,1152]{2,1,0:T(8,128)(2,1)} %pad_maximum_fusion.1), channel_id=1, source_target_pairs={{0,8},{8,0},{16,24},{24,16},{1,9},{9,1},{17,25},{25,17},{2,10},{10... | collective-permute-start | bytes 7077896 | tf_op jit(solution)/shard_map/ppermute | solution.py:945
  350.4 48.3 %collective-permute-start.9 = (bf16[2,512,1152]{2,1,0:T(8,128)(2,1)}, bf16[2,512,1152]{2,1,0:T(8,128)(2,1)}, u32[]{:S(2)}, u32[]{:S(2)}) collective-permute-start(bf16[2,512,1152]{2,1,0:T(8,128)(2,1)} %pad_maximum_fusion.2), channel_id=1, source_target_pairs={{0,16},{8,24},{16,0},{24,8},{1,17},{9,25},{17,1},{25,9},{2,18},{10... | collective-permute-start | bytes 7077896 | tf_op jit(solution)/shard_map/ppermute | solution.py:945
  400.3 87.6 %collective-permute-start.15 = (bf16[1,512,1152]{2,1,0:T(8,128)(2,1)S(1)}, bf16[1,512,1152]{2,1,0:T(8,128)(2,1)S(1)}, u32[]{:S(2)}, u32[]{:S(2)}) collective-permute-start(bf16[1,512,1152]{2,1,0:T(8,128)(2,1)S(1)} %add_convert_fusion.4), channel_id=1, source_target_pairs={{0,16},{8,24},{16,0},{24,8},{1,17},{9,25},{17,1},{25,9},{2,18},{10... | collective-permute-start | bytes 3538952 | tf_op jit(solution)/shard_map/ppermute | solution.py:945
  402.3 87.5 %collective-permute-start.16 = (bf16[1,512,1152]{2,1,0:T(8,128)(2,1)S(1)}, bf16[1,512,1152]{2,1,0:T(8,128)(2,1)S(1)}, u32[]{:S(2)}, u32[]{:S(2)}) collective-permute-start(bf16[1,512,1152]{2,1,0:T(8,128)(2,1)S(1)} %add_convert_fusion.3), channel_id=1, source_target_pairs={{0,8},{8,0},{16,24},{24,16},{1,9},{9,1},{17,25},{25,17},{2,10},{10... | collective-permute-start | bytes 3538952 | tf_op jit(solution)/shard_map/ppermute | solution.py:945
  493.5 340.4 %all-gather.18.cloned.1.call-start = ((), (), s32[]{:S(2)}) async-start(), calls=%async_computation.4 | async-start | bytes 11796480 | tf_op jit(solution)/shard_map/all_gather | solution.py:1411
  606.3 12.3 %collective-permute-start.10 = (f32[1024,256]{1,0:T(8,128)S(1)}, f32[1024,256]{1,0:T(8,128)}, u32[]{:S(2)}, u32[]{:S(2)}) collective-permute-start(f32[1024,256]{1,0:T(8,128)S(1)} %get-tuple-element.147), channel_id=1, source_target_pairs={{0,1},{1,0},{2,3},{3,2},{4,5},{5,4},{6,7},{7,6},{8,9},{9,8},{10,11... | collective-permute-start | bytes 3145736 | tf_op jit(solution)/shard_map/ppermute | solution.py:1371
  614.8 13.9 %collective-permute-start.11 = (bf16[2,512,256]{2,1,0:T(8,128)(2,1)}, bf16[2,512,256]{2,1,0:T(8,128)(2,1)}, u32[]{:S(2)}, u32[]{:S(2)}) collective-permute-start(bf16[2,512,256]{2,1,0:T(8,128)(2,1)} %pad_maximum_fusion.15), channel_id=1, source_target_pairs={{0,8},{8,0},{16,24},{24,16},{1,9},{9,1},{17,25},{25,17},{2,10},{10... | collective-permute-start | bytes 1572872 | tf_op jit(solution)/shard_map/ppermute | solution.py:945
  614.8 13.8 %collective-permute-start.12 = (bf16[2,512,256]{2,1,0:T(8,128)(2,1)S(1)}, bf16[2,512,256]{2,1,0:T(8,128)(2,1)}, u32[]{:S(2)}, u32[]{:S(2)}) collective-permute-start(bf16[2,512,256]{2,1,0:T(8,128)(2,1)S(1)} %pad_maximum_fusion.16), channel_id=1, source_target_pairs={{0,16},{8,24},{16,0},{24,8},{1,17},{9,25},{17,1},{25,9},{2,18},{10... | collective-permute-start | bytes 1572872 | tf_op jit(solution)/shard_map/ppermute | solution.py:945
  630.5 69.0 %collective-permute-start.14 = (bf16[1,512,256]{2,1,0:T(8,128)(2,1)}, bf16[1,512,256]{2,1,0:T(8,128)(2,1)S(1)}, u32[]{:S(2)}, u32[]{:S(2)}) collective-permute-start(bf16[1,512,256]{2,1,0:T(8,128)(2,1)} %fusion.66), channel_id=1, source_target_pairs={{0,8},{8,0},{16,24},{24,16},{1,9},{9,1},{17,25},{25,17},{2,10},{10... | collective-permute-start | bytes 786440 | tf_op jit(solution)/shard_map/ppermute | solution.py:945
  633.3 66.2 %collective-permute-start.13 = (bf16[1,512,256]{2,1,0:T(8,128)(2,1)}, bf16[1,512,256]{2,1,0:T(8,128)(2,1)}, u32[]{:S(2)}, u32[]{:S(2)}) collective-permute-start(bf16[1,512,256]{2,1,0:T(8,128)(2,1)} %fusion.65), channel_id=1, source_target_pairs={{0,16},{8,24},{16,0},{24,8},{1,17},{9,25},{17,1},{25,9},{2,18},{10... | collective-permute-start | bytes 786440 | tf_op jit(solution)/shard_map/ppermute | solution.py:945
  (97 other events, 1192.1 us)
Sparse Core Ops, SparseCore 0:
  71.8 86.1 all-gather.9
  159.8 90.2 all-gather.11
  278.3 65.5 all-gather.13
  345.5 150.5 all-gather.15
  497.6 192.2 all-gather.19
  703.2 130.6 all-gather.17

commit v4 on v3

--- a/solution.py
+++ b/solution.py
@@ -15,6 +15,7 @@
 TOPK = 8
 EXPERTS = 16
 PAD = 128
+SMALL = 32
 
 EPS = 1e-06
 ROPE_BASE = 1000000.0
@@ -1005,6 +1006,7 @@
 def finish_attention_kernel(
     sharers,
     packed_ref,
+    small_ref,
     query_ref,
     key_ref,
     value_ref,
@@ -1018,23 +1020,23 @@
     mixture_ref,
     qg_ref,
     kg_ref,
+    rows_ref,
     sums_ref,
 ):
-    width = o_ref.shape[1]
+    shard, width = o_ref.shape
     share = 2 * HD // sharers
     at = pl.program_id(0)
     o_ref[...] = packed_ref[0, :, :width].astype(F32)
     query = packed_ref[0, :, width : 2 * width].astype(F32)
     q_ref[...] = query
-    gain = jnp.sum(query * query_ref[...].astype(F32), axis=1, keepdims=True)
-    small = packed_ref[0, :, 2 * width + share :].astype(F32)
 
     @pl.when(at == 0)
     def _():
+        rows_ref[...] = jnp.zeros_like(rows_ref)
         sums_ref[...] = jnp.zeros_like(sums_ref)
 
-    lane = lax.broadcasted_iota(jnp.int32, small.shape, 1)
-    sums_ref[...] += small + jnp.where(lane == EXPERTS + 3, gain, 0.0)
+    rows_ref[...] += small_ref[0, :, :shard].astype(F32)
+    sums_ref[...] += jnp.sum(query * query_ref[...].astype(F32), axis=1, keepdims=True)
     for number in range(sharers):
 
         @pl.when(lax.rem(at, sharers) == number)
@@ -1047,22 +1049,20 @@
             else:
                 weight = value_ref[:, start - HD : start - HD + share]
                 v_ref[:, start - HD : start - HD + share] = piece
-            more = jnp.sum(piece * weight.astype(F32), axis=1, keepdims=True)
-            sums_ref[...] += jnp.where(lane == EXPERTS + 3, more, 0.0)
+            sums_ref[...] += jnp.sum(piece * weight.astype(F32), axis=1, keepdims=True)
 
     @pl.when(at == pl.num_programs(0) - 1)
     def _():
-        rows = jnp.transpose(sums_ref[...], (1, 0))
-        router_ref[...] = rows[:EXPERTS, :]
-        mixture_ref[...] = rows[EXPERTS : EXPERTS + 1, :]
-        qg_ref[...] = rows[EXPERTS + 1 : EXPERTS + 2, :]
-        kg_ref[...] = rows[EXPERTS + 2 : EXPERTS + 3, :]
-        attention_ref[...] = rows[EXPERTS + 3 : EXPERTS + 4, :] / gain_ref[...]
+        router_ref[...] = rows_ref[:EXPERTS, :]
+        mixture_ref[...] = rows_ref[EXPERTS : EXPERTS + 1, :]
+        qg_ref[...] = rows_ref[EXPERTS + 1 : EXPERTS + 2, :]
+        kg_ref[...] = rows_ref[EXPERTS + 2 : EXPERTS + 3, :]
+        attention_ref[...] = jnp.transpose(sums_ref[...], (1, 0))[:1, :] / gain_ref[...]
 
 
 def finish_attention(packed, weights, width, sharers):
-    parts, shard, total = packed.shape
-    spare = total - 2 * width - 2 * HD // sharers
+    parts, tall, total = packed.shape
+    shard = tall - SMALL
     head = pl.BlockSpec((shard, HD), lambda c: (0, c // sharers))
     own = pl.BlockSpec((shard, width), lambda c: (0, c))
     whole = lambda c: (0, 0)
@@ -1081,6 +1081,7 @@
             grid=(parts,),
             in_specs=[
                 pl.BlockSpec((1, shard, total), lambda c: (c, 0, 0)),
+                pl.BlockSpec((1, SMALL, total), lambda c: (c, shard // SMALL, 0)),
                 own,
                 head,
                 head,
@@ -1094,11 +1095,11 @@
                 pl.BlockSpec((EXPERTS, shard), whole),
             )
             + (pl.BlockSpec((1, shard), whole),) * 4,
-            scratch_shapes=[pltpu.VMEM((shard, spare), F32)],
+            scratch_shapes=[pltpu.VMEM((SMALL, shard), F32), pltpu.VMEM((shard, PAD), F32)],
         ),
         cost_estimate=pl.CostEstimate(flops=0, bytes_accessed=packed.size // 16, transcendentals=0),
         name="finish_attention",
-    )(packed, *weights)
+    )(packed, packed, *weights)
 
 
 def per_device(
@@ -1407,7 +1408,14 @@
     layer_out = (hidden + layer_sum).astype(BF16)[None]
     add_all(output_sums, qkv_piece)
     finish_all(output_sums)
-    attn_piece = jnp.concatenate([one.held[0] for one in output_sums] + [qkv_piece], axis=1)
+    wide = jnp.concatenate(
+        [one.held[0] for one in output_sums] + [qkv_piece[:, : width + share]], axis=1
+    )
+    low_rows = jnp.pad(
+        qkv_piece[:, width + share : width + share + EXPERTS + 3].T,
+        ((0, SMALL - EXPERTS - 3), (0, wide.shape[1] - shard)),
+    )
+    attn_piece = jnp.concatenate([wide, low_rows], axis=0)
     attn_grads = lax.all_gather(attn_piece, "ctx")
     (normed_grad,) = comm(
         plan_scatter,

time: 864 us -> 860 us (level)
    unnamed x203 -> x204, local copies, waits for them, and re-layouts: 17.5 us -> 17.6 us
where the time goes in v4:
time: 860 us; the launch traced here: 855 us
  Pallas kernels  556 us (65%)
  matrix products  133 us (15%)
  other arithmetic  55 us (6%)
  waiting for transfers between devices  46.6 us (5%)
  local copies, waits for them, and re-layouts  37 us (4%)
  between operations  15.9 us (2%)
  starting transfers between devices  11.8 us (1%)
    pallas_call x7, Pallas kernels, comm_call(): pl.pallas_call(functools.partial(comm_kernel, plan, chips, owners, counts...  469 us
    dot_general x9, matrix products, dot(): return jnp.dot(left, right, preferred_element_type=F32)  48.4 us
    dot_general x7, matrix products, dot_nt(): lax.dot_general(left, right, (((1,), (1,)), ((), ())), preferred_element_...  46 us
    ppermute x16, waiting for transfers between devices, send(): self.got = lax.ppermute(self.sent, 'group', pairs)  43.7 us
    pallas_call x2, Pallas kernels, widen(): pl.pallas_call(functools.partial(widen_kernel, counts), out_shape=(shape,...  41.4 us
    dot_general x9, matrix products, dot_tn(): lax.dot_general(left, right, (((0,), (0,)), ((), ())), preferred_element_...  38.1 us
    pallas_call x1, Pallas kernels, attend_back(): pl.pallas_call(functools.partial(attend_back_kernel, 256), out_shape=(jax...  19.1 us
    unnamed x204, local copies, waits for them, and re-layouts  17.6 us
  transfers between devices with their start and end apart: 23, of which 12 were waited for; matrix products, arithmetic and copies ran while one was open for 23% of the time, Pallas kernels for 57%

profile of v4, /device:TPU:17, one launch (start us, length us, event | category | flops | bytes accessed | tf_op | source)
XLA Modules:
  0.0 855.1 jit_solution(5122176181567985860)
XLA Ops:
  18.2 52.1 %gather_tokens.1 = (bf16[1024,2048]{1,0:T(8,128)(2,1)}, s32[64,128]{1,0:T(8,128)S(1)}, bf16[64,512]{1,0:T(8,128)(2,1)S(1)}, bf16[2048,16]{1,0:T(8,128)(2,1)S(1)}...) custom-call(bf16[128,2048]{1,0:T(8,128)(2,1)S(1)} %bitcast.240, ...), custom_call_target="tpu_custom_call" | custom-call | bytes 1530000 | tf_op jit(solution)/shard_map/gather_tokens/pallas_call | solution.py:814
  84.5 11.4 %attend.1.refs_0_ = bf16[1024,512]{1,0:T(8,128)(2,1)S(1)} custom-call(f32[1024,768]{1,0:T(8,128)S(1)} %fusion.7.q_ref.kv_ref, f32[1024,768]{1,0:T(8,128)S(1)} %fusion.7.q_ref.kv_ref, s32[1024,1]{1,0:T(8,128)S(1)} %iota_subtract_fusion.doc_ref, f32[1024,256]{1,0:T(8,128)S(1)} %pad_maximum_fusion.10.cos_ref.sin_ref, ...), custom_call_target="tpu_custom_call" | custom-call | flops 1048576 | bytes 524288 | tf_op jit(solution)/shard_map/attend/pallas_call | solution.py:184
  95.9 66.8 %scatter_attention.1 = (f32[128,2048]{1,0:T(8,128)S(1)}, bf16[1024,2048]{1,0:T(8,128)(2,1)}, bf16[2048,768]{1,0:T(8,128)(2,1)}) custom-call(bf16[1024,512]{1,0:T(8,128)(2,1)S(1)} %attend.1.refs_0_, bf16[2048,512]{1,0:T(8,128)(2,1)S(1)} %copy-done.19, bf16[128,2048]{1,0:T(8,128)(2,1)S(1)} %bitcast.241, bf16[16,512,768]{2,1,0:T(8,128)(2,1)} %refs_2_.1), custom_call_target="tpu_custom_call" | custom-call | bytes 1700000 | tf_op jit(solution)/shard_map/scatter_attention/pallas_call | solution.py:814
  164.8 46.7 %gather_mixture.1 = (bf16[1024,2048]{1,0:T(8,128)(2,1)}, f32[1024,128]{1,0:T(8,128)S(1)}, bf16[2048,768]{1,0:T(8,128)(2,1)S(1)}) custom-call(bf16[128,2048]{1,0:T(8,128)(2,1)S(1)} %multiply_convert_fusion.6.refs_0_, f32[128,128]{1,0:T(8,128)S(1)} %pad.32.refs_1_, bf16[16,512,768]{2,1,0:T(8,128)(2,1)} %refs_2_.1), custom_call_target="tpu_custom_call" | custom-call | bytes 1530000 | tf_op jit(solution)/shard_map/gather_mixture/pallas_call | solution.py:814
  213.2 7.3 fusion.90
  221.2 6.4 fusion.78
  239.8 5.7 fusion.15
  285.3 8.8 %fusion.92 = f32[1024,768]{0,1:T(8,128)} fusion(bf16[1024,2048]{1,0:T(8,128)(2,1)} %get-tuple-element.106, bf16[2048,768]{1,0:T(8,128)(2,1)S(1)} %slice.158), kind=kOutput, calls=%fused_computation.243 | convolution fusion | flops 3221225472 | bytes 10485760 | tf_op jit(solution)/shard_map/dot_general | solution.py:40
  294.2 8.1 fusion.6
  302.4 7.5 convolution_convert_fusion.3
  351.8 6.0 fusion.93
  357.9 5.7 fusion.94
  369.3 13.4 %add_convert_fusion.refs_0_ = bf16[1024,2048]{1,0:T(8,128)(2,1)S(1)} fusion(f32[1024,2048]{1,0:T(8,128)} %fusion.95, f32[1024,2048]{1,0:T(8,128)} %fusion.93, f32[1024,2048]{1,0:T(8,128)} %fusion.94, bf16[1024,768]{0,1:T(8,128)(2,1)} %copy-done.53, bf16[2048,768]{1,0:T(8,128)(2,1)} %copy-done.37), kind=kOutput, calls=%fused_computation.5 | convolution fusion | flops 3229614080 | bytes 34078720 | tf_op jit(solution)/shard_map/dot_general | solution.py:44
  382.7 16.0 %collective-permute-done.9 = bf16[2,512,1152]{2,1,0:T(8,128)(2,1)} collective-permute-done((bf16[2,512,1152]{2,1,0:T(8,128)(2,1)}, bf16[2,512,1152]{2,1,0:T(8,128)(2,1)}, u32[]{:S(2)}, u32[]{:S(2)}) %collective-permute-start.9) | collective-permute-done | bytes 2359328 | tf_op jit(solution)/shard_map/ppermute | solution.py:946
  404.3 83.6 %scatter_mixture.1 = (f32[128,2048]{1,0:T(8,128)S(1)}, f32[128,128]{1,0:T(8,128)S(1)}) custom-call(bf16[1024,2048]{1,0:T(8,128)(2,1)S(1)} %add_convert_fusion.refs_0_, bf16[1024,128]{1,0:T(8,128)(2,1)S(1)} %add_convert_fusion.6.refs_1_), custom_call_target="tpu_custom_call" | custom-call | bytes 2040000 | tf_op jit(solution)/shard_map/scatter_mixture/pallas_call | solution.py:814
  497.2 82.2 %gather_attention.1 = bf16[1024,2048]{1,0:T(8,128)(2,1)S(1)} custom-call(bf16[128,2048]{1,0:T(8,128)(2,1)S(1)} %get-tuple-element.144.refs_0_), custom_call_target="tpu_custom_call" | custom-call | bytes 1530000 | tf_op jit(solution)/shard_map/gather_attention/pallas_call | solution.py:814
  587.2 19.1 %attend_back.1 = (bf16[1024,512]{1,0:T(8,128)(2,1)S(1)}, f32[1024,256]{1,0:T(8,128)S(1)}, f32[1,128]{1,0:T(1,128)S(1)}, f32[1,128]{1,0:T(1,128)S(1)}) custom-call(f32[1024,768]{1,0:T(8,128)S(1)} %copy-done.1, f32[1024,768]{1,0:T(8,128)S(1)} %copy-done.1, s32[1024,1]{1,0:T(8,128)S(1)} %copy-done.9, f32[1024,256]{1,0:T(8,128)S(1)} %copy-done.3, ...), custom_call_target="tpu_custom_call" | custom-call | flops 1048576 | bytes 524288 | tf_op jit(solution)/shard_map/attend_back/pallas_call | solution.py:205
  607.0 7.6 add_convert_fusion.1.refs_0_
  620.0 8.6 %collective-permute-done.12 = bf16[2,512,256]{2,1,0:T(8,128)(2,1)} collective-permute-done((bf16[2,512,256]{2,1,0:T(8,128)(2,1)S(1)}, bf16[2,512,256]{2,1,0:T(8,128)(2,1)}, u32[]{:S(2)}, u32[]{:S(2)}) %collective-permute-start.12) | collective-permute-done | bytes 524320 | tf_op jit(solution)/shard_map/ppermute | solution.py:946
  637.8 60.6 %scatter_grads.1 = (f32[128,2048]{1,0:T(8,128)S(1)}, bf16[512,768]{1,0:T(8,128)(2,1)S(1)}) custom-call(bf16[1024,2048]{1,0:T(8,128)(2,1)} %add_convert_fusion.1.refs_0_, bf16[2048,768]{1,0:T(8,128)(2,1)S(1)} %add_convert_fusion.2.refs_1_), custom_call_target="tpu_custom_call" | custom-call | bytes 2040000 | tf_op jit(solution)/shard_map/scatter_grads/pallas_call | solution.py:814
  705.9 20.6 %widen.2 = (f32[8,2,512,768]{3,2,1,0:T(8,128)}, f32[8,2,512,768]{3,2,1,0:T(8,128)}, f32[8,2,512,768]{3,2,1,0:T(8,128)}) custom-call(bf16[8,1,512,768]{3,2,1,0:T(8,128)(2,1)} %bitcast.252, bf16[8,2,512,768]{3,2,1,0:T(8,128)(2,1)} %bitcast.251), custom_call_target="tpu_custom_call" | custom-call | bytes 589824 | tf_op jit(solution)/shard_map/widen/pallas_call | solution.py:988
  727.9 77.1 %scatter_normed.1 = f32[128,2048]{1,0:T(8,128)S(1)} custom-call(bf16[1024,640]{1,0:T(8,128)(2,1)S(1)} %copy-done.7, bf16[2048,640]{1,0:T(8,128)(2,1)S(1)} %pad_maximum_fusion.refs_1_), custom_call_target="tpu_custom_call" | custom-call | bytes 2040000 | tf_op jit(solution)/shard_map/scatter_normed/pallas_call | solution.py:814
  807.5 20.8 %widen.3 = (f32[8,2,512,768]{3,2,1,0:T(8,128)}, f32[8,2,512,768]{3,2,1,0:T(8,128)}, f32[8,2,512,768]{3,2,1,0:T(8,128)}) custom-call(bf16[8,3,512,768]{3,2,1,0:T(8,128)(2,1)} %bitcast.250, f32[8,2,512,768]{3,2,1,0:T(8,128)} %get-tuple-element.170.refs_1_, ...), custom_call_target="tpu_custom_call", output_to_operand_aliasing={{0}: (1, {}), {1}: (2, {}), {2}: (3, {})} | custom-call | bytes 589824 | tf_op jit(solution)/shard_map/widen/pallas_call | solution.py:988
  830.4 15.3 %finish_attention.1 = (f32[512,4096]{1,0:T(8,128)}, f32[512,512]{1,0:T(8,128)}, f32[512,512]{1,0:T(8,128)}, f32[512,4096]{1,0:T(8,128)}, f32[16,512]{1,0:T(8,128...) custom-call(bf16[8,544,1152]{2,1,0:T(8,128)(2,1)} %bitcast.245, ...), custom_call_target="tpu_custom_call" | custom-call | bytes 313344 | tf_op jit(solution)/shard_map/finish_attention/pallas_call | solution.py:1069
  (395 shorter events, 181.7 us)
Async XLA Ops:
  7.2 214.0 %all-gather.10.cloned.1.call-start = ((), (), s32[]{:S(2)}) async-start(), calls=%async_computation | async-start | bytes 7864320 | tf_op jit(solution)/shard_map/all_gather | solution.py:1135
  71.6 92.1 %copy-start.16 = (bf16[2048,16]{1,0:T(8,128)(2,1)}, bf16[2048,16]{1,0:T(8,128)(2,1)S(1)}, u32[]{:S(2)}) copy-start(bf16[2048,16]{1,0:T(8,128)(2,1)S(1)} %get-tuple-element.104) | copy-start | bytes 196612
  71.7 211.4 %all-gather.12.cloned.1.call-start = ((), (), s32[]{:S(2)}) async-start(), calls=%async_computation.1 | async-start | bytes 7864320 | tf_op jit(solution)/shard_map/all_gather | solution.py:1135
  72.4 424.8 %all-gather.14.cloned.1.call-start = ((), (), s32[]{:S(2)}) async-start(), calls=%async_computation.2 | async-start | bytes 7077888 | tf_op jit(solution)/shard_map/all_gather | solution.py:1340
  238.0 24.0 %collective-permute-start = (bf16[2,512,384]{1,2,0:T(8,128)(2,1)S(1)}, bf16[2,512,384]{1,2,0:T(8,128)(2,1)S(1)}, u32[]{:S(2)}, u32[]{:S(2)}) collective-permute-start(bf16[2,512,384]{1,2,0:T(8,128)(2,1)S(1)} %pad_maximum_fusion.11), channel_id=1, source_target_pairs={{0,8},{8,0},{16,24},{24,16},{1,9},{9,1},{17,25},{25,17},{2,10},{10... | collective-permute-start | bytes 2359304 | tf_op jit(solution)/shard_map/ppermute | solution.py:946
  238.7 23.2 %collective-permute-start.1 = (bf16[2,512,384]{1,2,0:T(8,128)(2,1)S(1)}, bf16[2,512,384]{1,2,0:T(8,128)(2,1)S(1)}, u32[]{:S(2)}, u32[]{:S(2)}) collective-permute-start(bf16[2,512,384]{1,2,0:T(8,128)(2,1)S(1)} %pad_maximum_fusion.12), channel_id=1, source_target_pairs={{0,16},{8,24},{16,0},{24,8},{1,17},{9,25},{17,1},{25,9},{2,18},{10... | collective-permute-start | bytes 2359304 | tf_op jit(solution)/shard_map/ppermute | solution.py:946
  262.9 9.8 %collective-permute-start.3 = (bf16[1,512,384]{1,2,0:T(8,128)(2,1)}, bf16[1,512,384]{1,2,0:T(8,128)(2,1)S(1)}, u32[]{:S(2)}, u32[]{:S(2)}) collective-permute-start(bf16[1,512,384]{1,2,0:T(8,128)(2,1)} %fusion.66), channel_id=1, source_target_pairs={{0,8},{8,0},{16,24},{24,16},{1,9},{9,1},{17,25},{25,17},{2,10},{10... | collective-permute-start | bytes 1179656 | tf_op jit(solution)/shard_map/ppermute | solution.py:946
  265.0 9.5 %collective-permute-start.2 = (bf16[1,512,384]{1,2,0:T(8,128)(2,1)}, bf16[1,512,384]{1,2,0:T(8,128)(2,1)}, u32[]{:S(2)}, u32[]{:S(2)}) collective-permute-start(bf16[1,512,384]{1,2,0:T(8,128)(2,1)} %fusion.65), channel_id=1, source_target_pairs={{0,16},{8,24},{16,0},{24,8},{1,17},{9,25},{17,1},{25,9},{2,18},{10... | collective-permute-start | bytes 1179656 | tf_op jit(solution)/shard_map/ppermute | solution.py:946
  278.2 359.6 %all-gather.16.cloned.1.call-start = ((), (), s32[]{:S(2)}) async-start(), calls=%async_computation.3 | async-start | bytes 14155776 | tf_op jit(solution)/shard_map/all_gather | solution.py:1340
  280.1 33.7 %collective-permute-start.5 = (bf16[2,512,768]{2,1,0:T(8,128)(2,1)S(1)}, bf16[2,512,768]{2,1,0:T(8,128)(2,1)}, u32[]{:S(2)}, u32[]{:S(2)}) collective-permute-start(bf16[2,512,768]{2,1,0:T(8,128)(2,1)S(1)} %pad_maximum_fusion.7), channel_id=1, source_target_pairs={{0,16},{8,24},{16,0},{24,8},{1,17},{9,25},{17,1},{25,9},{2,18},{10... | collective-permute-start | bytes 4718600 | tf_op jit(solution)/shard_map/ppermute | solution.py:946
  282.0 33.8 %collective-permute-start.4 = (bf16[2,512,768]{2,1,0:T(8,128)(2,1)}, bf16[2,512,768]{2,1,0:T(8,128)(2,1)}, u32[]{:S(2)}, u32[]{:S(2)}) collective-permute-start(bf16[2,512,768]{2,1,0:T(8,128)(2,1)} %pad_maximum_fusion.6), channel_id=1, source_target_pairs={{0,8},{8,0},{16,24},{24,16},{1,9},{9,1},{17,25},{25,17},{2,10},{10... | collective-permute-start | bytes 4718600 | tf_op jit(solution)/shard_map/ppermute | solution.py:946
  317.2 15.8 %collective-permute-start.7 = (bf16[1,512,768]{2,1,0:T(8,128)(2,1)S(1)}, bf16[1,512,768]{2,1,0:T(8,128)(2,1)S(1)}, u32[]{:S(2)}, u32[]{:S(2)}) collective-permute-start(bf16[1,512,768]{2,1,0:T(8,128)(2,1)S(1)} %fusion.46), channel_id=1, source_target_pairs={{0,8},{8,0},{16,24},{24,16},{1,9},{9,1},{17,25},{25,17},{2,10},{10... | collective-permute-start | bytes 2359304 | tf_op jit(solution)/shard_map/ppermute | solution.py:946
  319.5 15.4 %collective-permute-start.6 = (bf16[1,512,768]{2,1,0:T(8,128)(2,1)S(1)}, bf16[1,512,768]{2,1,0:T(8,128)(2,1)S(1)}, u32[]{:S(2)}, u32[]{:S(2)}) collective-permute-start(bf16[1,512,768]{2,1,0:T(8,128)(2,1)S(1)} %fusion.45), channel_id=1, source_target_pairs={{0,16},{8,24},{16,0},{24,8},{1,17},{9,25},{17,1},{25,9},{2,18},{10... | collective-permute-start | bytes 2359304 | tf_op jit(solution)/shard_map/ppermute | solution.py:946
  339.2 468.3 %all-gather.20.cloned.1.call-start = ((), (), s32[]{:S(2)}) async-start(), calls=%async_computation.5 | async-start | bytes 21233664 | tf_op jit(solution)/shard_map/all_gather | solution.py:1340
  345.7 53.0 %collective-permute-start.8 = (bf16[2,512,1152]{2,1,0:T(8,128)(2,1)}, bf16[2,512,1152]{2,1,0:T(8,128)(2,1)}, u32[]{:S(2)}, u32[]{:S(2)}) collective-permute-start(bf16[2,512,1152]{2,1,0:T(8,128)(2,1)} %pad_maximum_fusion.1), channel_id=1, source_target_pairs={{0,8},{8,0},{16,24},{24,16},{1,9},{9,1},{17,25},{25,17},{2,10},{10... | collective-permute-start | bytes 7077896 | tf_op jit(solution)/shard_map/ppermute | solution.py:946
  350.4 48.3 %collective-permute-start.9 = (bf16[2,512,1152]{2,1,0:T(8,128)(2,1)}, bf16[2,512,1152]{2,1,0:T(8,128)(2,1)}, u32[]{:S(2)}, u32[]{:S(2)}) collective-permute-start(bf16[2,512,1152]{2,1,0:T(8,128)(2,1)} %pad_maximum_fusion.2), channel_id=1, source_target_pairs={{0,16},{8,24},{16,0},{24,8},{1,17},{9,25},{17,1},{25,9},{2,18},{10... | collective-permute-start | bytes 7077896 | tf_op jit(solution)/shard_map/ppermute | solution.py:946
  400.3 87.6 %collective-permute-start.15 = (bf16[1,512,1152]{2,1,0:T(8,128)(2,1)S(1)}, bf16[1,512,1152]{2,1,0:T(8,128)(2,1)S(1)}, u32[]{:S(2)}, u32[]{:S(2)}) collective-permute-start(bf16[1,512,1152]{2,1,0:T(8,128)(2,1)S(1)} %add_convert_fusion.4), channel_id=1, source_target_pairs={{0,16},{8,24},{16,0},{24,8},{1,17},{9,25},{17,1},{25,9},{2,18},{10... | collective-permute-start | bytes 3538952 | tf_op jit(solution)/shard_map/ppermute | solution.py:946
  402.3 87.5 %collective-permute-start.16 = (bf16[1,512,1152]{2,1,0:T(8,128)(2,1)S(1)}, bf16[1,512,1152]{2,1,0:T(8,128)(2,1)S(1)}, u32[]{:S(2)}, u32[]{:S(2)}) collective-permute-start(bf16[1,512,1152]{2,1,0:T(8,128)(2,1)S(1)} %add_convert_fusion.3), channel_id=1, source_target_pairs={{0,8},{8,0},{16,24},{24,16},{1,9},{9,1},{17,25},{25,17},{2,10},{10... | collective-permute-start | bytes 3538952 | tf_op jit(solution)/shard_map/ppermute | solution.py:946
  493.5 336.9 %all-gather.18.cloned.1.call-start = ((), (), s32[]{:S(2)}) async-start(), calls=%async_computation.4 | async-start | bytes 11280384 | tf_op jit(solution)/shard_map/all_gather | solution.py:1419
  606.3 12.3 %collective-permute-start.10 = (f32[1024,256]{1,0:T(8,128)S(1)}, f32[1024,256]{1,0:T(8,128)}, u32[]{:S(2)}, u32[]{:S(2)}) collective-permute-start(f32[1024,256]{1,0:T(8,128)S(1)} %get-tuple-element.147), channel_id=1, source_target_pairs={{0,1},{1,0},{2,3},{3,2},{4,5},{5,4},{6,7},{7,6},{8,9},{9,8},{10,11... | collective-permute-start | bytes 3145736 | tf_op jit(solution)/shard_map/ppermute | solution.py:1372
  614.8 13.9 %collective-permute-start.11 = (bf16[2,512,256]{2,1,0:T(8,128)(2,1)}, bf16[2,512,256]{2,1,0:T(8,128)(2,1)}, u32[]{:S(2)}, u32[]{:S(2)}) collective-permute-start(bf16[2,512,256]{2,1,0:T(8,128)(2,1)} %pad_maximum_fusion.14), channel_id=1, source_target_pairs={{0,8},{8,0},{16,24},{24,16},{1,9},{9,1},{17,25},{25,17},{2,10},{10... | collective-permute-start | bytes 1572872 | tf_op jit(solution)/shard_map/ppermute | solution.py:946
  614.8 13.8 %collective-permute-start.12 = (bf16[2,512,256]{2,1,0:T(8,128)(2,1)S(1)}, bf16[2,512,256]{2,1,0:T(8,128)(2,1)}, u32[]{:S(2)}, u32[]{:S(2)}) collective-permute-start(bf16[2,512,256]{2,1,0:T(8,128)(2,1)S(1)} %pad_maximum_fusion.15), channel_id=1, source_target_pairs={{0,16},{8,24},{16,0},{24,8},{1,17},{9,25},{17,1},{25,9},{2,18},{10... | collective-permute-start | bytes 1572872 | tf_op jit(solution)/shard_map/ppermute | solution.py:946
  630.5 69.2 %collective-permute-start.14 = (bf16[1,512,256]{2,1,0:T(8,128)(2,1)}, bf16[1,512,256]{2,1,0:T(8,128)(2,1)S(1)}, u32[]{:S(2)}, u32[]{:S(2)}) collective-permute-start(bf16[1,512,256]{2,1,0:T(8,128)(2,1)} %fusion.68), channel_id=1, source_target_pairs={{0,8},{8,0},{16,24},{24,16},{1,9},{9,1},{17,25},{25,17},{2,10},{10... | collective-permute-start | bytes 786440 | tf_op jit(solution)/shard_map/ppermute | solution.py:946
  633.3 66.4 %collective-permute-start.13 = (bf16[1,512,256]{2,1,0:T(8,128)(2,1)}, bf16[1,512,256]{2,1,0:T(8,128)(2,1)}, u32[]{:S(2)}, u32[]{:S(2)}) collective-permute-start(bf16[1,512,256]{2,1,0:T(8,128)(2,1)} %fusion.67), channel_id=1, source_target_pairs={{0,16},{8,24},{16,0},{24,8},{1,17},{9,25},{17,1},{25,9},{2,18},{10... | collective-permute-start | bytes 786440 | tf_op jit(solution)/shard_map/ppermute | solution.py:946
  (97 other events, 1188.0 us)
Sparse Core Ops, SparseCore 0:
  71.8 86.1 all-gather.9
  159.8 90.2 all-gather.11
  278.3 65.5 all-gather.13
  345.5 150.5 all-gather.15
  497.6 192.2 all-gather.19
  703.4 126.8 all-gather.17

commit v5 on v4

--- a/solution.py
+++ b/solution.py
@@ -1417,12 +1417,15 @@
     )
     attn_piece = jnp.concatenate([wide, low_rows], axis=0)
     attn_grads = lax.all_gather(attn_piece, "ctx")
+    finished = ()
+    for number in range(experts):
+        finished = widen(expert_packs[number], number, experts, finished)
     (normed_grad,) = comm(
         plan_scatter,
         5,
         "scatter_normed",
         60,
-        scatter=((after(qkv_low, attn_piece), wqkv_share),),
+        scatter=((after(qkv_low, attn_piece, *finished), wqkv_share),),
     )
     input_part, unused = rms_back(inputs, attn_factor, attention_gains, normed_grad)
     tokens_grad = (hidden_grad + input_part).astype(BF16)[None]
@@ -1432,9 +1435,6 @@
         width,
         sharers,
     )
-    finished = ()
-    for number in range(experts):
-        finished = widen(expert_packs[number], number, experts, finished)
     whole = lambda v: v.reshape(EXPERTS, shard, F)
     return (
         layer_out,

time: 860 us -> 857 us (level)
    unnamed x204 -> x198, local copies, waits for them, and re-layouts: 17.6 us -> 15.4 us
  transfers between devices with their start and end apart: 23 -> 23, of which waited for: 12 -> 11; matrix products, arithmetic and copies ran while one was open for 23% -> 24% of each run, Pallas kernels for 57% -> 57%
where the time goes in v5:
time: 857 us; the launch traced here: 851 us
  Pallas kernels  552 us (64%)
  matrix products  134 us (16%)
  other arithmetic  56.3 us (7%)
  waiting for transfers between devices  45.1 us (5%)
  local copies, waits for them, and re-layouts  34.1 us (4%)
  between operations  15.9 us (2%)
  starting transfers between devices  14.7 us (2%)
    pallas_call x7, Pallas kernels, comm_call(): pl.pallas_call(functools.partial(comm_kernel, plan, chips, owners, counts...  464 us
    dot_general x9, matrix products, dot(): return jnp.dot(left, right, preferred_element_type=F32)  49.3 us
    dot_general x7, matrix products, dot_nt(): lax.dot_general(left, right, (((1,), (1,)), ((), ())), preferred_element_...  46.1 us
    ppermute x16, waiting for transfers between devices, send(): self.got = lax.ppermute(self.sent, 'group', pairs)  42.5 us
    pallas_call x2, Pallas kernels, widen(): pl.pallas_call(functools.partial(widen_kernel, counts), out_shape=(shape,...  41.6 us
    dot_general x9, matrix products, dot_tn(): lax.dot_general(left, right, (((0,), (0,)), ((), ())), preferred_element_...  38.3 us
    pallas_call x1, Pallas kernels, attend_back(): pl.pallas_call(functools.partial(attend_back_kernel, 256), out_shape=(jax...  19.1 us
  transfers between devices with their start and end apart: 23, of which 11 were waited for; matrix products, arithmetic and copies ran while one was open for 24% of the time, Pallas kernels for 57%

profile of v5, /device:TPU:17, one launch (start us, length us, event | category | flops | bytes accessed | tf_op | source)
XLA Modules:
  0.0 851.4 jit_solution(14694632368634474294)
XLA Ops:
  15.5 52.1 %gather_tokens.1 = (bf16[1024,2048]{1,0:T(8,128)(2,1)}, s32[64,128]{1,0:T(8,128)S(1)}, bf16[64,512]{1,0:T(8,128)(2,1)S(1)}, bf16[2048,16]{1,0:T(8,128)(2,1)S(1)}...) custom-call(bf16[128,2048]{1,0:T(8,128)(2,1)S(1)} %bitcast.240, ...), custom_call_target="tpu_custom_call" | custom-call | bytes 1530000 | tf_op jit(solution)/shard_map/gather_tokens/pallas_call | solution.py:814
  76.1 6.6 fusion.7.q_ref.kv_ref
  82.8 11.4 %attend.1.refs_0_ = bf16[1024,512]{1,0:T(8,128)(2,1)S(1)} custom-call(f32[1024,768]{1,0:T(8,128)S(1)} %fusion.7.q_ref.kv_ref, f32[1024,768]{1,0:T(8,128)S(1)} %fusion.7.q_ref.kv_ref, s32[1024,1]{1,0:T(8,128)S(1)} %iota_subtract_fusion.doc_ref, f32[1024,256]{1,0:T(8,128)S(1)} %pad_maximum_fusion.10.cos_ref.sin_ref, ...), custom_call_target="tpu_custom_call" | custom-call | flops 1048576 | bytes 524288 | tf_op jit(solution)/shard_map/attend/pallas_call | solution.py:184
  94.2 65.0 %scatter_attention.1 = (f32[128,2048]{1,0:T(8,128)S(1)}, bf16[1024,2048]{1,0:T(8,128)(2,1)}, bf16[2048,768]{1,0:T(8,128)(2,1)}) custom-call(bf16[1024,512]{1,0:T(8,128)(2,1)S(1)} %attend.1.refs_0_, bf16[2048,512]{1,0:T(8,128)(2,1)S(1)} %copy-done.18, bf16[128,2048]{1,0:T(8,128)(2,1)S(1)} %bitcast.241, bf16[16,512,768]{2,1,0:T(8,128)(2,1)} %refs_2_.1), custom_call_target="tpu_custom_call" | custom-call | bytes 1700000 | tf_op jit(solution)/shard_map/scatter_attention/pallas_call | solution.py:814
  161.2 46.7 %gather_mixture.1 = (bf16[1024,2048]{1,0:T(8,128)(2,1)}, f32[1024,128]{1,0:T(8,128)S(1)}, bf16[2048,768]{1,0:T(8,128)(2,1)S(1)}) custom-call(bf16[128,2048]{1,0:T(8,128)(2,1)S(1)} %multiply_convert_fusion.6.refs_0_, f32[128,128]{1,0:T(8,128)S(1)} %pad.32.refs_1_, bf16[16,512,768]{2,1,0:T(8,128)(2,1)} %refs_2_.1), custom_call_target="tpu_custom_call" | custom-call | bytes 1530000 | tf_op jit(solution)/shard_map/gather_mixture/pallas_call | solution.py:814
  209.6 7.3 fusion.90
  217.6 6.4 fusion.78
  236.2 5.7 fusion.15
  282.0 8.8 %fusion.92 = f32[1024,768]{0,1:T(8,128)} fusion(bf16[1024,2048]{1,0:T(8,128)(2,1)} %get-tuple-element.106, bf16[2048,768]{1,0:T(8,128)(2,1)S(1)} %slice.158), kind=kOutput, calls=%fused_computation.243 | convolution fusion | flops 3221225472 | bytes 10485760 | tf_op jit(solution)/shard_map/dot_general | solution.py:40
  290.9 8.1 fusion.6
  299.0 7.5 convolution_convert_fusion.3
  348.0 6.2 fusion.95
  365.6 13.4 %add_convert_fusion.refs_0_ = bf16[1024,2048]{1,0:T(8,128)(2,1)S(1)} fusion(f32[1024,2048]{1,0:T(8,128)} %fusion.95, f32[1024,2048]{1,0:T(8,128)} %fusion.93, f32[1024,2048]{1,0:T(8,128)} %fusion.94, bf16[1024,768]{0,1:T(8,128)(2,1)} %copy-done.49, bf16[2048,768]{1,0:T(8,128)(2,1)} %copy-done.34), kind=kOutput, calls=%fused_computation.5 | convolution fusion | flops 3229614080 | bytes 34078720 | tf_op jit(solution)/shard_map/dot_general | solution.py:44
  379.0 11.3 %collective-permute-done.8 = bf16[2,512,1152]{2,1,0:T(8,128)(2,1)} collective-permute-done((bf16[2,512,1152]{2,1,0:T(8,128)(2,1)}, bf16[2,512,1152]{2,1,0:T(8,128)(2,1)}, u32[]{:S(2)}, u32[]{:S(2)}) %collective-permute-start.8) | collective-permute-done | bytes 2359328 | tf_op jit(solution)/shard_map/ppermute | solution.py:946
  401.3 82.9 %scatter_mixture.1 = (f32[128,2048]{1,0:T(8,128)S(1)}, f32[128,128]{1,0:T(8,128)S(1)}) custom-call(bf16[1024,2048]{1,0:T(8,128)(2,1)S(1)} %add_convert_fusion.refs_0_, bf16[1024,128]{1,0:T(8,128)(2,1)S(1)} %add_convert_fusion.6.refs_1_), custom_call_target="tpu_custom_call" | custom-call | bytes 2040000 | tf_op jit(solution)/shard_map/scatter_mixture/pallas_call | solution.py:814
  493.5 80.8 %gather_attention.1 = bf16[1024,2048]{1,0:T(8,128)(2,1)S(1)} custom-call(bf16[128,2048]{1,0:T(8,128)(2,1)S(1)} %get-tuple-element.144.refs_0_), custom_call_target="tpu_custom_call" | custom-call | bytes 1530000 | tf_op jit(solution)/shard_map/gather_attention/pallas_call | solution.py:814
  582.2 19.1 %attend_back.1 = (bf16[1024,512]{1,0:T(8,128)(2,1)S(1)}, f32[1024,256]{1,0:T(8,128)S(1)}, f32[1,128]{1,0:T(1,128)S(1)}, f32[1,128]{1,0:T(1,128)S(1)}) custom-call(f32[1024,768]{1,0:T(8,128)S(1)} %copy-done.1, f32[1024,768]{1,0:T(8,128)S(1)} %copy-done.1, s32[1024,1]{1,0:T(8,128)S(1)} %iota_subtract_fusion.doc_ref, f32[1024,256]{1,0:T(8,128)S(1)} %copy-done.3, ...), custom_call_target="tpu_custom_call" | custom-call | flops 1048576 | bytes 524288 | tf_op jit(solution)/shard_map/attend_back/pallas_call | solution.py:205
  602.5 7.5 add_convert_fusion.1.refs_0_
  615.5 8.8 %collective-permute-done.11 = bf16[2,512,256]{2,1,0:T(8,128)(2,1)} collective-permute-done((bf16[2,512,256]{2,1,0:T(8,128)(2,1)}, bf16[2,512,256]{2,1,0:T(8,128)(2,1)}, u32[]{:S(2)}, u32[]{:S(2)}) %collective-permute-start.11) | collective-permute-done | bytes 524320 | tf_op jit(solution)/shard_map/ppermute | solution.py:946
  633.6 61.2 %scatter_grads.1 = (f32[128,2048]{1,0:T(8,128)S(1)}, bf16[512,768]{1,0:T(8,128)(2,1)S(1)}) custom-call(bf16[1024,2048]{1,0:T(8,128)(2,1)} %add_convert_fusion.1.refs_0_, bf16[2048,768]{1,0:T(8,128)(2,1)S(1)} %add_convert_fusion.2.refs_1_), custom_call_target="tpu_custom_call" | custom-call | bytes 2040000 | tf_op jit(solution)/shard_map/scatter_grads/pallas_call | solution.py:814
  702.3 20.7 %widen.2 = (f32[8,2,512,768]{3,2,1,0:T(8,128)}, f32[8,2,512,768]{3,2,1,0:T(8,128)}, f32[8,2,512,768]{3,2,1,0:T(8,128)}) custom-call(bf16[8,1,512,768]{3,2,1,0:T(8,128)(2,1)} %bitcast.252, bf16[8,2,512,768]{3,2,1,0:T(8,128)(2,1)} %bitcast.251), custom_call_target="tpu_custom_call" | custom-call | bytes 589824 | tf_op jit(solution)/shard_map/widen/pallas_call | solution.py:988
  725.4 20.9 %widen.3 = (f32[8,2,512,768]{3,2,1,0:T(8,128)}, f32[8,2,512,768]{3,2,1,0:T(8,128)}, f32[8,2,512,768]{3,2,1,0:T(8,128)}) custom-call(bf16[8,3,512,768]{3,2,1,0:T(8,128)(2,1)} %bitcast.250, f32[8,2,512,768]{3,2,1,0:T(8,128)} %get-tuple-element.160.refs_1_, ...), custom_call_target="tpu_custom_call", output_to_operand_aliasing={{0}: (1, {}), {1}: (2, {}), {2}: (3, {})} | custom-call | bytes 589824 | tf_op jit(solution)/shard_map/widen/pallas_call | solution.py:988
  747.7 75.6 %scatter_normed.1 = f32[128,2048]{1,0:T(8,128)S(1)} custom-call(bf16[1024,640]{1,0:T(8,128)(2,1)S(1)} %copy-done.7, bf16[2048,640]{1,0:T(8,128)(2,1)S(1)} %pad_maximum_fusion.refs_1_), custom_call_target="tpu_custom_call" | custom-call | bytes 2040000 | tf_op jit(solution)/shard_map/scatter_normed/pallas_call | solution.py:814
  826.7 15.3 %finish_attention.1 = (f32[512,4096]{1,0:T(8,128)}, f32[512,512]{1,0:T(8,128)}, f32[512,512]{1,0:T(8,128)}, f32[512,4096]{1,0:T(8,128)}, f32[16,512]{1,0:T(8,128...) custom-call(bf16[8,544,1152]{2,1,0:T(8,128)(2,1)} %bitcast.245, ...), custom_call_target="tpu_custom_call" | custom-call | bytes 313344 | tf_op jit(solution)/shard_map/finish_attention/pallas_call | solution.py:1069
  (389 shorter events, 186.3 us)
Async XLA Ops:
  7.2 210.4 %all-gather.10.cloned.1.call-start = ((), (), s32[]{:S(2)}) async-start(), calls=%async_computation | async-start | bytes 7864320 | tf_op jit(solution)/shard_map/all_gather | solution.py:1135
  69.0 91.2 %copy-start.14 = (bf16[2048,16]{1,0:T(8,128)(2,1)}, bf16[2048,16]{1,0:T(8,128)(2,1)S(1)}, u32[]{:S(2)}) copy-start(bf16[2048,16]{1,0:T(8,128)(2,1)S(1)} %get-tuple-element.104) | copy-start | bytes 196612
  69.0 210.7 %all-gather.12.cloned.1.call-start = ((), (), s32[]{:S(2)}) async-start(), calls=%async_computation.1 | async-start | bytes 7864320 | tf_op jit(solution)/shard_map/all_gather | solution.py:1135
  69.8 423.7 %all-gather.14.cloned.1.call-start = ((), (), s32[]{:S(2)}) async-start(), calls=%async_computation.2 | async-start | bytes 7077888 | tf_op jit(solution)/shard_map/all_gather | solution.py:1340
  234.4 24.0 %collective-permute-start = (bf16[2,512,384]{1,2,0:T(8,128)(2,1)S(1)}, bf16[2,512,384]{1,2,0:T(8,128)(2,1)S(1)}, u32[]{:S(2)}, u32[]{:S(2)}) collective-permute-start(bf16[2,512,384]{1,2,0:T(8,128)(2,1)S(1)} %pad_maximum_fusion.11), channel_id=1, source_target_pairs={{0,8},{8,0},{16,24},{24,16},{1,9},{9,1},{17,25},{25,17},{2,10},{10... | collective-permute-start | bytes 2359304 | tf_op jit(solution)/shard_map/ppermute | solution.py:946
  235.1 23.3 %collective-permute-start.1 = (bf16[2,512,384]{1,2,0:T(8,128)(2,1)S(1)}, bf16[2,512,384]{1,2,0:T(8,128)(2,1)S(1)}, u32[]{:S(2)}, u32[]{:S(2)}) collective-permute-start(bf16[2,512,384]{1,2,0:T(8,128)(2,1)S(1)} %pad_maximum_fusion.12), channel_id=1, source_target_pairs={{0,16},{8,24},{16,0},{24,8},{1,17},{9,25},{17,1},{25,9},{2,18},{10... | collective-permute-start | bytes 2359304 | tf_op jit(solution)/shard_map/ppermute | solution.py:946
  259.5 9.8 %collective-permute-start.3 = (bf16[1,512,384]{1,2,0:T(8,128)(2,1)}, bf16[1,512,384]{1,2,0:T(8,128)(2,1)}, u32[]{:S(2)}, u32[]{:S(2)}) collective-permute-start(bf16[1,512,384]{1,2,0:T(8,128)(2,1)} %fusion.66), channel_id=1, source_target_pairs={{0,8},{8,0},{16,24},{24,16},{1,9},{9,1},{17,25},{25,17},{2,10},{10... | collective-permute-start | bytes 1179656 | tf_op jit(solution)/shard_map/ppermute | solution.py:946
  261.4 9.5 %collective-permute-start.2 = (bf16[1,512,384]{1,2,0:T(8,128)(2,1)}, bf16[1,512,384]{1,2,0:T(8,128)(2,1)}, u32[]{:S(2)}, u32[]{:S(2)}) collective-permute-start(bf16[1,512,384]{1,2,0:T(8,128)(2,1)} %fusion.65), channel_id=1, source_target_pairs={{0,16},{8,24},{16,0},{24,8},{1,17},{9,25},{17,1},{25,9},{2,18},{10... | collective-permute-start | bytes 1179656 | tf_op jit(solution)/shard_map/ppermute | solution.py:946
  274.7 358.9 %all-gather.16.cloned.1.call-start = ((), (), s32[]{:S(2)}) async-start(), calls=%async_computation.3 | async-start | bytes 14155776 | tf_op jit(solution)/shard_map/all_gather | solution.py:1340
  276.6 33.7 %collective-permute-start.4 = (bf16[2,512,768]{2,1,0:T(8,128)(2,1)S(1)}, bf16[2,512,768]{2,1,0:T(8,128)(2,1)}, u32[]{:S(2)}, u32[]{:S(2)}) collective-permute-start(bf16[2,512,768]{2,1,0:T(8,128)(2,1)S(1)} %pad_maximum_fusion.6), channel_id=1, source_target_pairs={{0,8},{8,0},{16,24},{24,16},{1,9},{9,1},{17,25},{25,17},{2,10},{10... | collective-permute-start | bytes 4718600 | tf_op jit(solution)/shard_map/ppermute | solution.py:946
  278.5 33.6 %collective-permute-start.5 = (bf16[2,512,768]{2,1,0:T(8,128)(2,1)}, bf16[2,512,768]{2,1,0:T(8,128)(2,1)}, u32[]{:S(2)}, u32[]{:S(2)}) collective-permute-start(bf16[2,512,768]{2,1,0:T(8,128)(2,1)} %pad_maximum_fusion.7), channel_id=1, source_target_pairs={{0,16},{8,24},{16,0},{24,8},{1,17},{9,25},{17,1},{25,9},{2,18},{10... | collective-permute-start | bytes 4718600 | tf_op jit(solution)/shard_map/ppermute | solution.py:946
  313.5 15.7 %collective-permute-start.7 = (bf16[1,512,768]{2,1,0:T(8,128)(2,1)S(1)}, bf16[1,512,768]{2,1,0:T(8,128)(2,1)S(1)}, u32[]{:S(2)}, u32[]{:S(2)}) collective-permute-start(bf16[1,512,768]{2,1,0:T(8,128)(2,1)S(1)} %fusion.46), channel_id=1, source_target_pairs={{0,8},{8,0},{16,24},{24,16},{1,9},{9,1},{17,25},{25,17},{2,10},{10... | collective-permute-start | bytes 2359304 | tf_op jit(solution)/shard_map/ppermute | solution.py:946
  315.9 15.4 %collective-permute-start.6 = (bf16[1,512,768]{2,1,0:T(8,128)(2,1)S(1)}, bf16[1,512,768]{2,1,0:T(8,128)(2,1)S(1)}, u32[]{:S(2)}, u32[]{:S(2)}) collective-permute-start(bf16[1,512,768]{2,1,0:T(8,128)(2,1)S(1)} %fusion.45), channel_id=1, source_target_pairs={{0,16},{8,24},{16,0},{24,8},{1,17},{9,25},{17,1},{25,9},{2,18},{10... | collective-permute-start | bytes 2359304 | tf_op jit(solution)/shard_map/ppermute | solution.py:946
  335.5 390.0 %all-gather.18.cloned.1.call-start = ((), (), s32[]{:S(2)}) async-start(), calls=%async_computation.4 | async-start | bytes 21233664 | tf_op jit(solution)/shard_map/all_gather | solution.py:1340
  341.9 48.4 %collective-permute-start.8 = (bf16[2,512,1152]{2,1,0:T(8,128)(2,1)}, bf16[2,512,1152]{2,1,0:T(8,128)(2,1)}, u32[]{:S(2)}, u32[]{:S(2)}) collective-permute-start(bf16[2,512,1152]{2,1,0:T(8,128)(2,1)} %pad_maximum_fusion.1), channel_id=1, source_target_pairs={{0,8},{8,0},{16,24},{24,16},{1,9},{9,1},{17,25},{25,17},{2,10},{10... | collective-permute-start | bytes 7077896 | tf_op jit(solution)/shard_map/ppermute | solution.py:946
  346.6 48.1 %collective-permute-start.9 = (bf16[2,512,1152]{2,1,0:T(8,128)(2,1)}, bf16[2,512,1152]{2,1,0:T(8,128)(2,1)}, u32[]{:S(2)}, u32[]{:S(2)}) collective-permute-start(bf16[2,512,1152]{2,1,0:T(8,128)(2,1)} %pad_maximum_fusion.2), channel_id=1, source_target_pairs={{0,16},{8,24},{16,0},{24,8},{1,17},{9,25},{17,1},{25,9},{2,18},{10... | collective-permute-start | bytes 7077896 | tf_op jit(solution)/shard_map/ppermute | solution.py:946
  396.4 87.8 %collective-permute-start.16 = (bf16[1,512,1152]{2,1,0:T(8,128)(2,1)S(1)}, bf16[1,512,1152]{2,1,0:T(8,128)(2,1)S(1)}, u32[]{:S(2)}, u32[]{:S(2)}) collective-permute-start(bf16[1,512,1152]{2,1,0:T(8,128)(2,1)S(1)} %add_convert_fusion.3), channel_id=1, source_target_pairs={{0,8},{8,0},{16,24},{24,16},{1,9},{9,1},{17,25},{25,17},{2,10},{10... | collective-permute-start | bytes 3538952 | tf_op jit(solution)/shard_map/ppermute | solution.py:946
  398.9 85.3 %collective-permute-start.15 = (bf16[1,512,1152]{2,1,0:T(8,128)(2,1)S(1)}, bf16[1,512,1152]{2,1,0:T(8,128)(2,1)S(1)}, u32[]{:S(2)}, u32[]{:S(2)}) collective-permute-start(bf16[1,512,1152]{2,1,0:T(8,128)(2,1)S(1)} %add_convert_fusion.4), channel_id=1, source_target_pairs={{0,16},{8,24},{16,0},{24,8},{1,17},{9,25},{17,1},{25,9},{2,18},{10... | collective-permute-start | bytes 3538952 | tf_op jit(solution)/shard_map/ppermute | solution.py:946
  489.7 336.9 %all-gather.20.cloned.1.call-start = ((), (), s32[]{:S(2)}) async-start(), calls=%async_computation.5 | async-start | bytes 11280384 | tf_op jit(solution)/shard_map/all_gather | solution.py:1419
  601.2 12.8 %collective-permute-start.10 = (f32[1024,256]{1,0:T(8,128)S(1)}, f32[1024,256]{1,0:T(8,128)}, u32[]{:S(2)}, u32[]{:S(2)}) collective-permute-start(f32[1024,256]{1,0:T(8,128)S(1)} %get-tuple-element.147), channel_id=1, source_target_pairs={{0,1},{1,0},{2,3},{3,2},{4,5},{5,4},{6,7},{7,6},{8,9},{9,8},{10,11... | collective-permute-start | bytes 3145736 | tf_op jit(solution)/shard_map/ppermute | solution.py:1372
  610.3 14.0 %collective-permute-start.11 = (bf16[2,512,256]{2,1,0:T(8,128)(2,1)}, bf16[2,512,256]{2,1,0:T(8,128)(2,1)}, u32[]{:S(2)}, u32[]{:S(2)}) collective-permute-start(bf16[2,512,256]{2,1,0:T(8,128)(2,1)} %pad_maximum_fusion.14), channel_id=1, source_target_pairs={{0,8},{8,0},{16,24},{24,16},{1,9},{9,1},{17,25},{25,17},{2,10},{10... | collective-permute-start | bytes 1572872 | tf_op jit(solution)/shard_map/ppermute | solution.py:946
  610.6 13.6 %collective-permute-start.12 = (bf16[2,512,256]{2,1,0:T(8,128)(2,1)}, bf16[2,512,256]{2,1,0:T(8,128)(2,1)}, u32[]{:S(2)}, u32[]{:S(2)}) collective-permute-start(bf16[2,512,256]{2,1,0:T(8,128)(2,1)} %pad_maximum_fusion.15), channel_id=1, source_target_pairs={{0,16},{8,24},{16,0},{24,8},{1,17},{9,25},{17,1},{25,9},{2,18},{10... | collective-permute-start | bytes 1572872 | tf_op jit(solution)/shard_map/ppermute | solution.py:946
  626.0 70.0 %collective-permute-start.14 = (bf16[1,512,256]{2,1,0:T(8,128)(2,1)}, bf16[1,512,256]{2,1,0:T(8,128)(2,1)S(1)}, u32[]{:S(2)}, u32[]{:S(2)}) collective-permute-start(bf16[1,512,256]{2,1,0:T(8,128)(2,1)} %fusion.68), channel_id=1, source_target_pairs={{0,8},{8,0},{16,24},{24,16},{1,9},{9,1},{17,25},{25,17},{2,10},{10... | collective-permute-start | bytes 786440 | tf_op jit(solution)/shard_map/ppermute | solution.py:946
  629.0 67.1 %collective-permute-start.13 = (bf16[1,512,256]{2,1,0:T(8,128)(2,1)}, bf16[1,512,256]{2,1,0:T(8,128)(2,1)}, u32[]{:S(2)}, u32[]{:S(2)}) collective-permute-start(bf16[1,512,256]{2,1,0:T(8,128)(2,1)} %fusion.67), channel_id=1, source_target_pairs={{0,16},{8,24},{16,0},{24,8},{1,17},{9,25},{17,1},{25,9},{2,18},{10... | collective-permute-start | bytes 786440 | tf_op jit(solution)/shard_map/ppermute | solution.py:946
  (94 other events, 1170.0 us)
Sparse Core Ops, SparseCore 0:
  69.1 83.4 all-gather.9
  154.5 92.0 all-gather.11
  274.8 65.7 all-gather.13
  342.2 150.5 all-gather.15
  494.2 191.7 all-gather.17
  699.8 126.8 all-gather.19
